TPU v7x, 32 devices: a whole 2x2x4 slice. The times are simulated.
32 devices in a mesh: dp: 4 (over z), fsdp: 8 (over y, x, core).
Axes of the slice: x: 2, y: 2, z: 4, core: 2. Of those that a mesh axis runs over, the one named last changes fastest.
Arguments:
- tokens: bfloat16 [131072, 512], P(('dp', 'fsdp')), may hold values from -6 to 6
- cotangent: bfloat16 [131072, 512], P(('dp', 'fsdp')), may hold values from -6 to 6
- block_target: int32 [4096], P(('dp', 'fsdp')), may hold values from 0 to 1023, as said below
- sequence_lengths: int32 [32, 4], P(('dp', 'fsdp')), may hold values from 1 to 2048, 4096 in all within a row
- norm_gain: bfloat16 [512], P(('dp', 'fsdp')), may hold values from 0.5 to 1.5
- norm_shift: bfloat16 [512], P(('dp', 'fsdp')), may hold values from -3 to 3
- decay_real: bfloat16 [384], P(('dp', 'fsdp')), may hold values from -0.796875 to -0.19921875
- decay_rotation: bfloat16 [384], P(('dp', 'fsdp')), may hold values from -10 to 10
- log_timestep: bfloat16 [384], P(('dp', 'fsdp')), may hold values from -6.875 to -2.296875
- drive_matrix: bfloat16 [512, 768], P(('dp', 'fsdp')), may hold values from -1 to 1
- readout_matrix: bfloat16 [768, 512], P(('dp', 'fsdp')), may hold values from -0.3125 to 0.3125
- feedthrough: bfloat16 [512], P(('dp', 'fsdp')), may hold values from -3 to 3
- mixer_weight: bfloat16 [512, 1024], P(('dp', 'fsdp')), may hold values from -0.25 to 0.25
- mixer_bias: bfloat16 [1024], P(('dp', 'fsdp')), may hold values from -3 to 3
Outputs:
- layer_output: float32 [131072, 512], P(('dp', 'fsdp'))
- token_grad: float32 [131072, 512], P(('dp', 'fsdp'))
- gain_grad: float32 [512], P(('dp', 'fsdp'))
- shift_grad: float32 [512], P(('dp', 'fsdp'))
- real_grad: float32 [384], P(('dp', 'fsdp'))
- rotation_grad: float32 [384], P(('dp', 'fsdp'))
- timestep_grad: float32 [384], P(('dp', 'fsdp'))
- drive_grad: float32 [512, 768], P(('dp', 'fsdp'))
- readout_grad: float32 [768, 512], P(('dp', 'fsdp'))
- feedthrough_grad: float32 [512], P(('dp', 'fsdp'))
- weight_grad: float32 [512, 1024], P(('dp', 'fsdp'))
- bias_grad: float32 [1024], P(('dp', 'fsdp'))
Inputs may be any that keep to these rules, and one draw needn't show every extreme that they name: Within each run of 1024 blocks (one group) the entries are a permutation of 0 to 1023, so every dealt device receives exactly 128 blocks; block b goes to dealt device block_target[b] // 128 of its group; one device sends 0, 16 or 32 of its blocks to any one device, and 32 to some device. `sequence_lengths`: each row sums to 4096.
All inputs are finite; a program needn't handle non-finite values.
Results may differ from a plain program's by a relative error of at most 0.019.
Values may be sent and summed in bfloat16 or wider, within the bound.
A program may use at most 320 MiB of HBM per device.

v0:
```python
import jax
import jax.numpy as jnp
from jax import lax
from jax.sharding import PartitionSpec as P

EPSILON = 1e-05
INNER_ROWS = 16


def combine(earlier, later):
    return (
        later[0] * earlier[0] - later[1] * earlier[1],
        later[0] * earlier[1] + later[1] * earlier[0],
        later[0] * earlier[2] - later[1] * earlier[3] + later[2],
        later[0] * earlier[3] + later[1] * earlier[2] + later[3],
    )


def run_scan(keeping, factor_real, factor_quad, driven):
    states = factor_real.shape[0]
    row_total = driven.shape[0]
    outer = row_total // INNER_ROWS

    def fold(values):
        return values.reshape(outer, INNER_ROWS, states).transpose(1, 0, 2)

    def unfold(values):
        return values.transpose(1, 0, 2).reshape(row_total, states)

    rate_real = keeping[:, None] * factor_real[None, :]
    rate_quad = keeping[:, None] * factor_quad[None, :]
    inputs = (fold(rate_real), fold(rate_quad), fold(driven[:, :states]), fold(driven[:, states:]))
    zeros = jnp.zeros((outer, states), jnp.float32)
    start = (jnp.ones((outer, states), jnp.float32), zeros, zeros, zeros)

    def inner_step(carry, item):
        joined_now = combine(carry, item)
        return (joined_now, joined_now)

    unused, local = lax.scan(inner_step, start, inputs)
    totals = tuple((piece[-1] for piece in local))
    prefix = lax.associative_scan(combine, totals, axis=0)
    first_row = jnp.zeros((1, states), jnp.float32)
    carry_real = jnp.concatenate([first_row, prefix[2][:-1]], axis=0)
    carry_quad = jnp.concatenate([first_row, prefix[3][:-1]], axis=0)
    state_real = local[2] + local[0] * carry_real[None] - local[1] * carry_quad[None]
    state_quad = local[3] + local[0] * carry_quad[None] + local[1] * carry_real[None]
    return jnp.concatenate([unfold(state_real), -unfold(state_quad)], axis=-1)


def discretize(decay_real, decay_rotation, log_timestep, drive_matrix):
    states = decay_real.shape[0]
    timestep = jnp.exp(log_timestep)
    magnitude = jnp.exp(decay_real * timestep)
    turned = decay_rotation * timestep
    factor_real = magnitude * jnp.cos(turned)
    factor_quad = magnitude * jnp.sin(turned)
    modulus = decay_real * decay_real + decay_rotation * decay_rotation
    scale_real = ((factor_real - 1.0) * decay_real + factor_quad * decay_rotation) / modulus
    scale_quad = (factor_quad * decay_real - (factor_real - 1.0) * decay_rotation) / modulus
    drive_real = drive_matrix[:, :states]
    drive_quad = drive_matrix[:, states:]
    drive_bar = jnp.concatenate(
        [
            scale_real * drive_real - scale_quad * drive_quad,
            scale_real * drive_quad + scale_quad * drive_real,
        ],
        axis=-1,
    )
    return (factor_real, factor_quad, drive_bar)


def normalize(values, norm_gain, norm_shift):
    center = jnp.mean(values, axis=-1, keepdims=True)
    spread = jnp.mean((values - center) ** 2, axis=-1, keepdims=True)
    return (values - center) * lax.rsqrt(spread + EPSILON) * norm_gain + norm_shift


def mixer_out(hidden):
    halfway = hidden.shape[1] // 2
    return hidden[:, :halfway] * jax.nn.sigmoid(hidden[:, halfway:])


def activate(values):
    return jax.nn.gelu(values, approximate=False)


def contract_rows(left, right):
    return lax.dot_general(
        left, right, (((0,), (0,)), ((), ())), preferred_element_type=jnp.float32
    )


def contract_cols(left, right):
    return lax.dot_general(
        left, right, (((1,), (1,)), ((), ())), preferred_element_type=jnp.float32
    )


def prepare(gathered):
    gain = gathered[0].astype(jnp.float32)
    shift = gathered[1].astype(jnp.float32)
    converted, convert_back = jax.vjp(
        discretize,
        gathered[2].astype(jnp.float32),
        gathered[3].astype(jnp.float32),
        gathered[4].astype(jnp.float32),
        gathered[5].astype(jnp.float32),
    )
    return (
        gain,
        shift,
        converted[0],
        converted[1],
        converted[2].astype(jnp.bfloat16),
        convert_back,
        gathered[6],
        gathered[7].astype(jnp.float32),
        gathered[8],
        gathered[9].astype(jnp.float32),
    )


def body(
    tokens,
    cotangent,
    block_target,
    sequence_lengths,
    norm_gain,
    norm_shift,
    decay_real,
    decay_rotation,
    log_timestep,
    drive_matrix,
    readout_matrix,
    feedthrough,
    mixer_weight,
    mixer_bias,
):
    members = lax.axis_size("fsdp")
    device_blocks = block_target.shape[0]
    row_count = tokens.shape[0]
    block_rows = row_count // device_blocks
    capacity = 2 * device_blocks // members
    slot_count = members * capacity
    forward_set = prepare(
        (
            lax.all_gather(norm_gain, ("dp", "fsdp"), axis=0, tiled=True),
            lax.all_gather(norm_shift, ("dp", "fsdp"), axis=0, tiled=True),
            lax.all_gather(decay_real, ("dp", "fsdp"), axis=0, tiled=True),
            lax.all_gather(decay_rotation, ("dp", "fsdp"), axis=0, tiled=True),
            lax.all_gather(log_timestep, ("dp", "fsdp"), axis=0, tiled=True),
            lax.all_gather(drive_matrix, ("dp", "fsdp"), axis=0, tiled=True),
            lax.all_gather(readout_matrix, ("dp", "fsdp"), axis=0, tiled=True),
            lax.all_gather(feedthrough, ("dp", "fsdp"), axis=0, tiled=True),
            lax.all_gather(mixer_weight, ("dp", "fsdp"), axis=0, tiled=True),
            lax.all_gather(mixer_bias, ("dp", "fsdp"), axis=0, tiled=True),
        )
    )
    target_device = block_target // device_blocks
    target_row = block_target % device_blocks
    one_hot = (target_device[:, None] == jnp.arange(members, dtype=jnp.int32)[None, :]).astype(
        jnp.int32
    )
    earlier_count = jnp.cumsum(one_hot, axis=0) - one_hot
    send_slot = target_device * capacity + jnp.sum(one_hot * earlier_count, axis=1)
    filled = (
        jnp.zeros((slot_count,), jnp.int32)
        .at[send_slot]
        .set(jnp.arange(device_blocks, dtype=jnp.int32) + 1)
    )
    source_block = jnp.maximum(filled - 1, 0)
    occupied = filled > 0
    positions = jnp.where(occupied, target_row[source_block], -1)

    def pack_given(values):
        columns = values.shape[1]
        blocks = values.reshape(device_blocks, block_rows, columns)[source_block]
        blocks = jnp.where(occupied[:, None, None], blocks, jnp.zeros_like(blocks))
        return blocks.reshape(members, capacity * block_rows, columns)

    def unpack_given(received_rows):
        columns = received_rows.shape[2]
        return received_rows.reshape(slot_count, block_rows, columns)[send_slot].reshape(
            row_count, columns
        )

    rows_f32 = tokens.astype(jnp.float32)
    cotangent_f32 = cotangent.astype(jnp.float32)
    normed_low = normalize(rows_f32, forward_set[0], forward_set[1]).astype(jnp.bfloat16)
    received, arrived = (
        lax.all_to_all(pack_given(normed_low), "fsdp", split_axis=0, concat_axis=0, tiled=True),
        lax.all_to_all(
            positions.reshape(members, capacity), "fsdp", split_axis=0, concat_axis=0, tiled=True
        ),
    )
    arrived = arrived.reshape(slot_count)
    present = arrived >= 0
    inverse = (
        jnp.zeros((device_blocks,), jnp.int32)
        .at[jnp.where(present, arrived, device_blocks)]
        .set(jnp.arange(slot_count, dtype=jnp.int32), mode="drop")
    )
    from_slot = jnp.maximum(arrived, 0)

    def unpack_dealt(received_rows):
        columns = received_rows.shape[2]
        return received_rows.reshape(slot_count, block_rows, columns)[inverse].reshape(
            row_count, columns
        )

    def pack_dealt(values):
        columns = values.shape[1]
        blocks = values.reshape(device_blocks, block_rows, columns)[from_slot]
        blocks = jnp.where(present[:, None, None], blocks, jnp.zeros_like(blocks))
        return blocks.reshape(members, capacity * block_rows, columns)

    dealt = unpack_dealt(received)
    dealt_f32 = dealt.astype(jnp.float32)
    lengths = sequence_lengths[0]
    starts = jnp.cumsum(lengths) - lengths
    row_ids = jnp.arange(row_count, dtype=jnp.int32)
    keeping = 1.0 - jnp.any(row_ids[:, None] == starts[None, :], axis=1).astype(jnp.float32)

    def local_scan(factor_real, factor_quad, driven):
        return run_scan(keeping, factor_real, factor_quad, driven)

    driven = jnp.dot(dealt, forward_set[4], preferred_element_type=jnp.float32)
    joined, scan_back = jax.vjp(local_scan, forward_set[2], forward_set[3], driven)
    joined_low = joined.astype(jnp.bfloat16)
    mixed = (
        jnp.dot(joined_low, forward_set[6], preferred_element_type=jnp.float32)
        + forward_set[7] * dealt_f32
    )
    activated = activate(mixed).astype(jnp.bfloat16)
    features = unpack_given(
        lax.all_to_all(pack_dealt(activated), "fsdp", split_axis=0, concat_axis=0, tiled=True)
    )
    hidden = jnp.dot(features, forward_set[8], preferred_element_type=jnp.float32) + forward_set[9]
    gated, gate_back = jax.vjp(mixer_out, hidden)
    back_set = prepare(
        (
            lax.all_gather(norm_gain, ("dp", "fsdp"), axis=0, tiled=True),
            lax.all_gather(norm_shift, ("dp", "fsdp"), axis=0, tiled=True),
            lax.all_gather(decay_real, ("dp", "fsdp"), axis=0, tiled=True),
            lax.all_gather(decay_rotation, ("dp", "fsdp"), axis=0, tiled=True),
            lax.all_gather(log_timestep, ("dp", "fsdp"), axis=0, tiled=True),
            lax.all_gather(drive_matrix, ("dp", "fsdp"), axis=0, tiled=True),
            lax.all_gather(readout_matrix, ("dp", "fsdp"), axis=0, tiled=True),
            lax.all_gather(feedthrough, ("dp", "fsdp"), axis=0, tiled=True),
            lax.all_gather(mixer_weight, ("dp", "fsdp"), axis=0, tiled=True),
            lax.all_gather(mixer_bias, ("dp", "fsdp"), axis=0, tiled=True),
        )
    )
    hidden_grad = gate_back(cotangent_f32)[0]
    hidden_low = hidden_grad.astype(jnp.bfloat16)
    weight_grad = contract_rows(features, hidden_low)
    bias_grad = jnp.sum(hidden_low.astype(jnp.float32), axis=0)
    feature_grad = contract_cols(hidden_low, back_set[8]).astype(jnp.bfloat16)
    dealt_grad = unpack_dealt(
        lax.all_to_all(pack_given(feature_grad), "fsdp", split_axis=0, concat_axis=0, tiled=True)
    )
    mixed_grad = jax.vjp(activate, mixed)[1](dealt_grad.astype(jnp.float32))[0]
    mixed_low = mixed_grad.astype(jnp.bfloat16)
    mixed_f32 = mixed_low.astype(jnp.float32)
    feedthrough_grad = jnp.sum(mixed_f32 * dealt_f32, axis=0)
    readout_grad = contract_rows(joined_low, mixed_low)
    joined_grad = contract_cols(mixed_low, back_set[6])
    factor_real_grad, factor_quad_grad, driven_grad = scan_back(joined_grad)
    driven_low = driven_grad.astype(jnp.bfloat16)
    drive_part = contract_rows(dealt, driven_low)
    normed_grad = (back_set[7] * mixed_f32 + contract_cols(driven_low, back_set[4])).astype(
        jnp.bfloat16
    )
    layer_output = rows_f32 + gated
    given_grad = unpack_given(
        lax.all_to_all(pack_dealt(normed_grad), "fsdp", split_axis=0, concat_axis=0, tiled=True)
    )
    unused_norm, norm_back = jax.vjp(normalize, rows_f32, back_set[0], back_set[1])
    token_part, gain_grad, shift_grad = norm_back(given_grad.astype(jnp.float32))
    token_grad = cotangent_f32 + token_part
    real_grad, rotation_grad, timestep_grad, drive_grad = back_set[5](
        (factor_real_grad, factor_quad_grad, drive_part)
    )
    summed = (
        lax.psum_scatter(gain_grad, ("dp", "fsdp"), scatter_dimension=0, tiled=True),
        lax.psum_scatter(shift_grad, ("dp", "fsdp"), scatter_dimension=0, tiled=True),
        lax.psum_scatter(real_grad, ("dp", "fsdp"), scatter_dimension=0, tiled=True),
        lax.psum_scatter(rotation_grad, ("dp", "fsdp"), scatter_dimension=0, tiled=True),
        lax.psum_scatter(timestep_grad, ("dp", "fsdp"), scatter_dimension=0, tiled=True),
        lax.psum_scatter(drive_grad, ("dp", "fsdp"), scatter_dimension=0, tiled=True),
        lax.psum_scatter(readout_grad, ("dp", "fsdp"), scatter_dimension=0, tiled=True),
        lax.psum_scatter(feedthrough_grad, ("dp", "fsdp"), scatter_dimension=0, tiled=True),
        lax.psum_scatter(weight_grad, ("dp", "fsdp"), scatter_dimension=0, tiled=True),
        lax.psum_scatter(bias_grad, ("dp", "fsdp"), scatter_dimension=0, tiled=True),
    )
    return (layer_output, token_grad) + tuple(summed)


def solution(mesh):
    return jax.shard_map(
        body,
        mesh=mesh,
        in_specs=(
            P(("dp", "fsdp"), None),
            P(("dp", "fsdp"), None),
            P(("dp", "fsdp")),
            P(("dp", "fsdp"), None),
            P(("dp", "fsdp")),
            P(("dp", "fsdp")),
            P(("dp", "fsdp")),
            P(("dp", "fsdp")),
            P(("dp", "fsdp")),
            P(("dp", "fsdp"), None),
            P(("dp", "fsdp"), None),
            P(("dp", "fsdp")),
            P(("dp", "fsdp"), None),
            P(("dp", "fsdp")),
        ),
        out_specs=(
            P(("dp", "fsdp"), None),
            P(("dp", "fsdp"), None),
            P(("dp", "fsdp")),
            P(("dp", "fsdp")),
            P(("dp", "fsdp")),
            P(("dp", "fsdp")),
            P(("dp", "fsdp")),
            P(("dp", "fsdp"), None),
            P(("dp", "fsdp"), None),
            P(("dp", "fsdp")),
            P(("dp", "fsdp"), None),
            P(("dp", "fsdp")),
        ),
        check_vma=False,
    )
```

profile of v0, /device:TPU:0, one launch (start us, length us, event | category | flops | bytes accessed | tf_op | source)
XLA Modules:
  0.0 1841.7 jit_solution(2707017728986477611)
XLA Ops:
  23.0 41.0 %all-reduce.179 = (bf16[1024]{0:T(1024)(128)(2,1)}, bf16[512]{0:T(512)(128)(2,1)S(1)}, bf16[512]{0:T(512)(128)(2,1)S(1)}, bf16[512]{0:T(512)(128)(2,1)S(1)}, bf1...) all-reduce(bf16[1024]{0:T(1024)(128)(2,1)S(1)} %dynamic-update-slic, ...), channel_id=1, replica_groups=mesh['dp'=4,'fsdp'=8] {'dp','fsdp'}, use_global_device_ids=true, to_apply=%add.170 | all-reduce | flops 3712 | bytes 14848
  72.4 10.8 gather_fusion.1
  96.2 127.4 %all_gather.43 = bf16[512,768]{1,0:T(8,128)(2,1)S(1)} all-gather(bf16[16,768]{1,0:T(8,128)(2,1)S(1)} %copy-done.135), channel_id=1, replica_groups=mesh['dp'=4,'fsdp'=8] {'dp','fsdp'}, dimensions={0}, use_global_device_ids=true | all-gather | bytes 811008 | tf_op jit(solution)/shard_map/all_gather | solution.py:153
  225.2 41.4 %all_gather.44 = bf16[768,512]{1,0:T(8,128)(2,1)} all-gather(bf16[24,512]{1,0:T(8,128)(2,1)S(1)} %copy-done.136), channel_id=1, replica_groups=mesh['dp'=4,'fsdp'=8] {'dp','fsdp'}, dimensions={0}, use_global_device_ids=true | all-gather | bytes 811008 | tf_op jit(solution)/shard_map/all_gather | solution.py:154
  282.3 10.2 fusion.65
  339.7 51.0 %while.62 = (s32[]{:T(128)}, f32[256,384]{1,0:T(8,128)S(1)}, f32[256,384]{1,0:T(8,128)S(1)}, f32[256,384]{1,0:T(8,128)S(1)}, f32[256,384]{1,0:T(8,128)S(1)}, /*i...) while((s32[]{:T(128)}, f32[256,384]{1,0:T(8,128)S(1)}, ...), condition=%wide.region_9.10_spmd.clone, body=%wide.region_8.9_spmd.clone.sunk | while | flops 1769475 | bytes 7865015 | solution.py:40
  513.1 9.8 multiply_add_fusion
  523.3 10.6 fusion.61
  538.6 23.8 %multiply_convert_fusion = (bf16[4096,512]{1,0:T(8,128)(2,1)}, f32[4096,512]{1,0:T(8,128)}, f32[4096,512]{1,0:T(8,128)}) fusion(bf16[4096,512]{1,0:T(8,128)(2,1)S(1)} %bitcast.328, f32[512]{0:T(512)S(1)} %copy-done.165, bf16[768,512]{1,0:T(8,128)(2,1)S(1)} %copy-done.66, bf16[4096,384]{1,0:T(8,128)(2,1)S(1)} %bitcast.338, bf16[4096,384]{1,0:T(8,128)(2,1)S(1)} %bitcast.340), kind=kOutput, calls=%fused_computation.125 | convolution fusion | flops 3376414720 | bytes 32245760 | tf_op jit(solution)/shard_map/dot_general | solution.py:232
  562.4 11.2 gather_fusion.3
  587.0 96.3 %all-to-all-done.2 = bf16[8,1024,512]{2,1,0:T(8,128)(2,1)} async-done(((bf16[8,1024,512]{2,1,0:T(8,128)(2,1)}), bf16[8,1024,512]{2,1,0:T(8,128)(2,1)}, u32[]{:S(2)}, u32[]{:S(2)}) %all-to-all-start.2) | async-done | bytes 8388640 | tf_op jit(solution)/shard_map/all_to_all | solution.py:237
  689.5 13.0 broadcast_add_fusion
  702.5 14.7 fusion.41
  717.2 12.4 convolution_convert_fusion
  729.6 10.9 gather_fusion.5
  753.2 94.0 %all-to-all-done.3 = bf16[8,1024,512]{2,1,0:T(8,128)(2,1)} async-done(((bf16[8,1024,512]{2,1,0:T(8,128)(2,1)}), bf16[8,1024,512]{2,1,0:T(8,128)(2,1)}, u32[]{:S(2)}, u32[]{:S(2)}) %all-to-all-start.3) | async-done | bytes 8388640 | tf_op jit(solution)/shard_map/all_to_all | solution.py:261
  853.6 11.1 fusion.30
  873.1 10.3 fusion.125
  883.4 12.4 fusion.58
  963.1 16.1 bitcast_multiply_fusion.27
  979.2 10.0 fusion.60
  1001.9 444.8 %while.63 = (s32[]{:T(128)}, f32[256,384]{1,0:T(8,128)S(1)}, f32[256,384]{1,0:T(8,128)S(1)}, f32[256,384]{1,0:T(8,128)S(1)}, f32[256,384]{1,0:T(8,128)S(1)}, /*i...) while((s32[]{:T(128)}, f32[256,384]{1,0:T(8,128)S(1)}, ...), condition=%wide.region_15.16_spmd.clone, body=%wide.region_14.15_spmd.clone.sunk | while | flops 3735556 | bytes 18088180 | solution.py:40
  1020.5 9.3 dynamic_update_slice.92
  1048.4 9.3 dynamic_update_slice.92
  1076.2 9.3 dynamic_update_slice.92
  1446.8 11.4 fusion.29
  1458.2 11.1 gather_fusion.7
  1481.9 13.0 fusion.115
  1525.5 66.8 %all-to-all-done.4 = bf16[8,1024,512]{2,1,0:T(8,128)(2,1)} async-done(((bf16[8,1024,512]{2,1,0:T(8,128)(2,1)}), bf16[8,1024,512]{2,1,0:T(8,128)(2,1)}, u32[]{:S(2)}, u32[]{:S(2)}) %all-to-all-start.4) | async-done | bytes 8388640 | tf_op jit(solution)/shard_map/all_to_all | solution.py:277
  1609.0 37.2 %all-reduce.178 = (f32[512]{0:T(512)S(1)}, f32[512]{0:T(512)S(1)}, f32[384]{0:T(512)S(1)}, f32[384]{0:T(512)S(1)}, f32[384]{0:T(512)S(1)}, /*index=5*/f32[512]{0:T(512)S(1)}, f32[1024]{0:T(1024)S(1)}) all-reduce(f32[512]{0:T(512)S(1)} %get-tuple-element.680, ...), channel_id=2, replica_groups=mesh['dp'=4,'fsdp'=8] {'dp','fsdp'}, use_global_device_ids=true, to_apply=%region_20.21.clone | all-reduce | flops 3712 | bytes 29696
  1662.4 70.0 %reduce-scatter.6.cloned.1.call-done = f32[24,512]{1,0:T(8,128)} async-done(((f32[768,512]{1,0:T(8,128)}), f32[24,512]{1,0:T(8,128)}) %reduce-scatter.6.cloned.1.call-update) | async-done | bytes 49168 | tf_op jit(solution)/shard_map/reduce_scatter | solution.py:292
  1732.4 102.6 %reduce-scatter.4.cloned.1.call-done = f32[16,768]{1,0:T(8,128)} async-done(((f32[512,768]{1,0:T(8,128)}), f32[16,768]{1,0:T(8,128)}) %reduce-scatter.4.cloned.1.call-update) | async-done | bytes 49168 | tf_op jit(solution)/shard_map/reduce_scatter | solution.py:291
  (998 shorter events, 896.2 us)
Async XLA Ops:
  11.9 79.1 %all-to-all-start = ((s32[8,1,32]{2,1,0:T(1,128)}), s32[8,1,32]{2,1,0:T(1,128)S(1)}, u32[]{:S(2)}, u32[]{:S(2)}) async-start(s32[8,1,32]{2,1,0:T(1,128)} %all_to_all.18), calls=%async_computation | async-start | bytes 8192 | tf_op jit(solution)/shard_map/all_to_all | solution.py:193
  64.1 160.8 %copy-start.158 = (bf16[384]{0:T(512)(128)(2,1)}, bf16[384]{0:T(512)(128)(2,1)S(1)}, u32[]{:S(2)}) copy-start(bf16[384]{0:T(512)(128)(2,1)S(1)} %get-tuple-element.777) | copy-start | bytes 2308
  64.1 160.8 %copy-start.160 = (bf16[384]{0:T(512)(128)(2,1)}, bf16[384]{0:T(512)(128)(2,1)S(1)}, u32[]{:S(2)}) copy-start(bf16[384]{0:T(512)(128)(2,1)S(1)} %get-tuple-element.778) | copy-start | bytes 2308
  64.1 160.8 %copy-start.162 = (bf16[384]{0:T(512)(128)(2,1)}, bf16[384]{0:T(512)(128)(2,1)S(1)}, u32[]{:S(2)}) copy-start(bf16[384]{0:T(512)(128)(2,1)S(1)} %get-tuple-element.779) | copy-start | bytes 2308
  91.0 132.7 %copy-start.170 = (s32[1,4]{1,0:T(1,128)S(1)}, s32[1,4]{1,0:T(1,128)}, u32[]{:S(2)}) copy-start(s32[1,4]{1,0:T(1,128)} %param.21) | copy-start | bytes 52
  91.0 134.1 %copy-start.136 = (bf16[24,512]{1,0:T(8,128)(2,1)S(1)}, bf16[24,512]{1,0:T(8,128)(2,1)}, u32[]{:S(2)}) copy-start(bf16[24,512]{1,0:T(8,128)(2,1)} %param.28) | copy-start | bytes 73732
  91.0 185.1 %all-to-all-start.1 = ((bf16[8,1024,512]{2,1,0:T(8,128)(2,1)}), bf16[8,1024,512]{2,1,0:T(8,128)(2,1)}, u32[]{:S(2)}, u32[]{:S(2)}) async-start(bf16[8,1024,512]{2,1,0:T(8,128)(2,1)} %bitcast_select_fusion.3), calls=%async_computation.1 | async-start | bytes 16777216 | tf_op jit(solution)/shard_map/all_to_all | solution.py:192
  393.8 92.2 %copy-start.16 = (f32[128,384]{1,0:T(8,128)}, f32[128,384]{1,0:T(8,128)S(1)}, u32[]{:S(2)}) copy-start(f32[128,384]{1,0:T(8,128)S(1)} %slice.538) | copy-start | bytes 589828
  393.9 96.6 %copy-start.25 = (f32[128,384]{1,0:T(8,128)}, f32[128,384]{1,0:T(8,128)S(1)}, u32[]{:S(2)}) copy-start(f32[128,384]{1,0:T(8,128)S(1)} %slice.547) | copy-start | bytes 589828
  395.2 97.6 %copy-start.18 = (f32[128,384]{1,0:T(8,128)}, f32[128,384]{1,0:T(8,128)S(1)}, u32[]{:S(2)}) copy-start(f32[128,384]{1,0:T(8,128)S(1)} %slice.542) | copy-start | bytes 589828
  395.3 97.8 %copy-start.27 = (f32[128,384]{1,0:T(8,128)}, f32[128,384]{1,0:T(8,128)S(1)}, u32[]{:S(2)}) copy-start(f32[128,384]{1,0:T(8,128)S(1)} %slice.548) | copy-start | bytes 589828
  396.6 107.9 %copy-start.29 = (f32[128,384]{1,0:T(8,128)}, f32[128,384]{1,0:T(8,128)S(1)}, u32[]{:S(2)}) copy-start(f32[128,384]{1,0:T(8,128)S(1)} %slice.544) | copy-start | bytes 589828
  399.2 83.6 %copy-start.56 = (f32[128,384]{1,0:T(8,128)}, f32[128,384]{1,0:T(8,128)S(1)}, u32[]{:S(2)}) copy-start(f32[128,384]{1,0:T(8,128)S(1)} %get-tuple-element.922) | copy-start | bytes 589828
  399.2 110.9 %copy-start.38 = (f32[64,384]{1,0:T(8,128)}, f32[64,384]{1,0:T(8,128)S(1)}, u32[]{:S(2)}) copy-start(f32[64,384]{1,0:T(8,128)S(1)} %slice.551) | copy-start | bytes 294916
  400.9 110.1 %copy-start.40 = (f32[64,384]{1,0:T(8,128)}, f32[64,384]{1,0:T(8,128)S(1)}, u32[]{:S(2)}) copy-start(f32[64,384]{1,0:T(8,128)S(1)} %slice.550) | copy-start | bytes 294916
  401.9 109.1 %copy-start.42 = (f32[64,384]{1,0:T(8,128)}, f32[64,384]{1,0:T(8,128)S(1)}, u32[]{:S(2)}) copy-start(f32[64,384]{1,0:T(8,128)S(1)} %slice.557) | copy-start | bytes 294916
  402.0 109.1 %copy-start.44 = (f32[64,384]{1,0:T(8,128)}, f32[64,384]{1,0:T(8,128)S(1)}, u32[]{:S(2)}) copy-start(f32[64,384]{1,0:T(8,128)S(1)} %slice.552) | copy-start | bytes 294916
  403.0 108.1 %copy-start.46 = (f32[64,384]{1,0:T(8,128)}, f32[64,384]{1,0:T(8,128)S(1)}, u32[]{:S(2)}) copy-start(f32[64,384]{1,0:T(8,128)S(1)} %slice.558) | copy-start | bytes 294916
  403.0 108.1 %copy-start.48 = (f32[64,384]{1,0:T(8,128)}, f32[64,384]{1,0:T(8,128)S(1)}, u32[]{:S(2)}) copy-start(f32[64,384]{1,0:T(8,128)S(1)} %slice.554) | copy-start | bytes 294916
  432.7 79.1 %copy-start.104 = (f32[8,384]{1,0:T(8,128)}, f32[8,384]{1,0:T(8,128)S(1)}, u32[]{:S(2)}) copy-start(f32[8,384]{1,0:T(8,128)S(1)} %slice.581) | copy-start | bytes 36868
  581.1 102.2 %all-to-all-start.2 = ((bf16[8,1024,512]{2,1,0:T(8,128)(2,1)}), bf16[8,1024,512]{2,1,0:T(8,128)(2,1)}, u32[]{:S(2)}, u32[]{:S(2)}) async-start(bf16[8,1024,512]{2,1,0:T(8,128)(2,1)} %bitcast_select_fusion.2), calls=%async_computation.2 | async-start | bytes 16777216 | tf_op jit(solution)/shard_map/all_to_all | solution.py:237
  586.2 103.3 %all-gather.2.cloned.1.call-start = ((), (), s32[]{:S(2)}) async-start(), calls=%async_computation.8 | async-start | bytes 1081344 | tf_op jit(solution)/shard_map/all_gather | solution.py:156
  587.0 102.5 %copy-start.151 = (s32[1024]{0:T(1024)}, s32[1024]{0:T(1024)S(1)}, u32[]{:S(2)}) copy-start(s32[1024]{0:T(1024)S(1)} %pad_clamp_fusion) | copy-start | bytes 12292
  748.1 99.2 %all-to-all-start.3 = ((bf16[8,1024,512]{2,1,0:T(8,128)(2,1)}), bf16[8,1024,512]{2,1,0:T(8,128)(2,1)}, u32[]{:S(2)}, u32[]{:S(2)}) async-start(bf16[8,1024,512]{2,1,0:T(8,128)(2,1)} %bitcast_select_fusion.1), calls=%async_computation.3 | async-start | bytes 16777216 | tf_op jit(solution)/shard_map/all_to_all | solution.py:261
  1001.9 444.9 %copy-start.87 = (bf16[512,384]{1,0:T(8,128)(2,1)S(1)}, bf16[512,384]{1,0:T(8,128)(2,1)}, u32[]{:S(2)}) copy-start(bf16[512,384]{1,0:T(8,128)(2,1)} %copy-done.86) | copy-start | bytes 1179652
  1001.9 444.9 %copy-start.89 = (bf16[512,384]{1,0:T(8,128)(2,1)S(1)}, bf16[512,384]{1,0:T(8,128)(2,1)}, u32[]{:S(2)}) copy-start(bf16[512,384]{1,0:T(8,128)(2,1)} %copy-done.88) | copy-start | bytes 1179652
  1001.9 444.9 %copy-start.166 = (f32[512]{0:T(512)S(1)}, f32[512]{0:T(512)}, u32[]{:S(2)}) copy-start(f32[512]{0:T(512)} %convert_element_type.106) | copy-start | bytes 6148
  1476.8 115.5 %all-to-all-start.4 = ((bf16[8,1024,512]{2,1,0:T(8,128)(2,1)}), bf16[8,1024,512]{2,1,0:T(8,128)(2,1)}, u32[]{:S(2)}, u32[]{:S(2)}) async-start(bf16[8,1024,512]{2,1,0:T(8,128)(2,1)} %bitcast_select_fusion), calls=%async_computation.4 | async-start | bytes 16777216 | tf_op jit(solution)/shard_map/all_to_all | solution.py:277
  1481.8 180.6 %reduce-scatter.8.cloned.1.call-start = ((), (), s32[]{:S(2)}) async-start(), calls=%async_computation.11 | async-start | bytes 2162688 | tf_op jit(solution)/shard_map/reduce_scatter | solution.py:294
  1494.9 237.5 %reduce-scatter.6.cloned.1.call-start = ((), (), s32[]{:S(2)}) async-start(), calls=%async_computation.10 | async-start | bytes 1622016 | tf_op jit(solution)/shard_map/reduce_scatter | solution.py:292
  1502.7 332.2 %reduce-scatter.4.cloned.1.call-start = ((), (), s32[]{:S(2)}) async-start(), calls=%async_computation.9 | async-start | bytes 1622016 | tf_op jit(solution)/shard_map/reduce_scatter | solution.py:291
  1525.4 73.3 %copy-start.77 = (f32[4096]{0:T(1024)S(1)}, f32[4096]{0:T(1024)}, u32[]{:S(2)}) copy-start(f32[4096]{0:T(1024)} %copy-done.76) | copy-start | bytes 49156
  (158 other events, 2759.8 us)
Sparse Core Ops, SparseCore 0:
  589.9 71.0 all-gather.1
  1495.0 137.4 reduce-scatter.7
  1639.2 93.1 reduce-scatter.5
  1738.9 96.0 reduce-scatter.3
where the time goes:
time: 1870 us; the launch traced here: 1840 us
  local copies, waits for them, and re-layouts  635 us (34%)
  waiting for transfers between devices  430 us (23%)
  other arithmetic  379 us (20%)
  blocking collectives  247 us (13%)
  matrix products  106 us (6%)
  starting transfers between devices  25.6 us (1%)
    dynamic_update_slice x64, local copies, waits for them, and re-layouts, run_scan(): unused, local = lax.scan(inner_step, start, inputs)  309 us
    dynamic_update_slice x48, other arithmetic, run_scan(): unused, local = lax.scan(inner_step, start, inputs)  131 us
    all_gather x1, blocking collectives, body(): lax.all_gather(drive_matrix, ('dp', 'fsdp'), axis=0, tiled=True)  127 us
    reduce_scatter x1, waiting for transfers between devices, body(): lax.psum_scatter(drive_grad, ('dp', 'fsdp'), scatter_dimension=0, tiled=T...  103 us
    all_to_all x1, waiting for transfers between devices, body(): lax.all_to_all(pack_dealt(activated), 'fsdp', split_axis=0, concat_axis=0...  96.3 us
    all_to_all x1, waiting for transfers between devices, body(): lax.all_to_all(pack_given(feature_grad), 'fsdp', split_axis=0, concat_axi...  94 us
    slice x120, local copies, waits for them, and re-layouts, run_scan(): prefix = lax.associative_scan(combine, totals, axis=0)  91.3 us
    unnamed x2, blocking collectives  78.2 us
  transfers between devices with their start and end apart: 9, of which 5 were waited for; matrix products, arithmetic and copies ran while one was open for 7% of the time, Pallas kernels for 0%

commit v1 on v0

v1 whole, which is shorter than its diff:
```python
import functools
import itertools

import jax
import jax.numpy as jnp
from jax import lax
from jax.experimental import pallas as pl
from jax.experimental.pallas import tpu as pltpu
from jax.sharding import PartitionSpec as P

EPSILON = 1e-05
AXES = ("dp", "fsdp")
F32 = jnp.float32
BF16 = jnp.bfloat16
LANES = 128
SUB = 8
VMEM_LIMIT = 60 * 1024 * 1024


def dot(left, right):
    return jnp.dot(left, right, preferred_element_type=F32)


def contract_rows(left, right):
    return lax.dot_general(left, right, (((0,), (0,)), ((), ())), preferred_element_type=F32)


def contract_cols(left, right):
    return lax.dot_general(left, right, (((1,), (1,)), ((), ())), preferred_element_type=F32)


def lanes_to(mask, width):
    return jnp.concatenate([mask] * (width // LANES), axis=1)


def spread(vector, rows):
    return jnp.broadcast_to(vector, (rows, vector.shape[1]))


def erfc_abs(magnitude):
    t = 1.0 / (1.0 + 0.5 * magnitude)
    series = t * 0.17087277 - 0.82215223
    for term in (1.48851587, -1.13520398, 0.27886807, -0.18628806, 0.09678418, 0.37409196, 1.00002368):
        series = series * t + term
    return t * jnp.exp(series * t - 1.26551223 - magnitude * magnitude)


def gelu_parts(v):
    complement = 0.5 * erfc_abs(jnp.abs(v) * 0.7071067811865476)
    cdf = jnp.where(v < 0.0, complement, 1.0 - complement)
    density = 0.3989422804014327 * jnp.exp(-0.5 * v * v)
    return v * cdf, cdf + v * density


def permute_tile(perm, tile, span):
    return jnp.concatenate(
        [dot(perm, tile[i * span : (i + 1) * span]) for i in range(tile.shape[0] // span)], axis=0
    )


def norm_stats(rows):
    center = jnp.mean(rows, axis=-1, keepdims=True)
    moved = rows - center
    spread_of = jnp.mean(moved * moved, axis=-1, keepdims=True)
    return moved, lax.rsqrt(spread_of + EPSILON)


MESH = pl.DeviceIdType.MESH


class Grid:
    def __init__(self, sizes):
        self.dp, members = sizes
        self.bits = members.bit_length() - 1
        self.shape = (self.dp,) + (2,) * self.bits

    def here(self):
        row, column = lax.axis_index("dp"), lax.axis_index("fsdp")
        mine = [row] + [lax.rem(lax.div(column, 2**bit), 2) for bit in reversed(range(self.bits))]
        return row, column, mine

    def peers(self, dim):
        row, column, mine = self.here()
        if dim == 0:
            return [
                (away - 1, {"dp": lax.rem(row + away, self.dp)}, lax.rem(row + away, self.dp))
                for away in range(1, self.dp)
            ]
        step = 2 ** (self.bits - dim)
        return [(0, {"fsdp": column + step * (1 - 2 * mine[dim])}, 1 - mine[dim])]

    def orders(self, dims, last):
        return [tuple(dims[i:] + dims[:i]) + last for i in range(len(dims))]


def greet(grid):
    barrier = pltpu.get_barrier_semaphore()
    row, column, _ = grid.here()
    members = 2**grid.bits
    for away in range(1, grid.dp):
        pl.semaphore_signal(
            barrier, inc=1, device_id={"dp": lax.rem(row + away, grid.dp)}, device_id_type=MESH
        )
    for away in range(1, members):
        pl.semaphore_signal(
            barrier, inc=1, device_id={"fsdp": lax.rem(column + away, members)}, device_id_type=MESH
        )
    pl.semaphore_wait(barrier, grid.dp + members - 2)


def remote(source, target, send, recv, device):
    return pltpu.make_async_remote_copy(
        src_ref=source, dst_ref=target, send_sem=send, recv_sem=recv, device_id=device, device_id_type=MESH
    )


def gather_phase(grid, ref, axes, dim, done, send, recv, base):
    _, _, mine = grid.here()
    at = tuple(slice(None) if d in done else mine[d] for d in axes)
    return [
        pltpu.make_async_remote_copy(
            src_ref=ref.at[at], dst_ref=ref.at[at], send_sem=send.at[base + slot], recv_sem=recv.at[base + slot],
            device_id=device, device_id_type=MESH,
        )
        for slot, device, _ in grid.peers(dim)
    ]


def reduce_plan(grid, order):
    plan = []
    for phase, dim in enumerate(order):
        done = order[:phase]
        left = tuple(d for d in range(grid.bits + 1) if d not in done and d != dim)
        plan.append((dim, done, left))
    return plan


def lane_index(width):
    return lax.broadcasted_iota(jnp.int32, (1, width), 1).astype(F32)


def unpack(rows, row, count, width):
    lanes = lane_index(width)
    owner = jnp.floor((lanes + 0.5) * (1.0 / count))
    inner = lanes - count * owner
    taken = lax.broadcasted_iota(jnp.int32, (LANES, width), 0).astype(F32) == inner
    spread_out = dot(rows.astype(BF16), jnp.where(taken, 1.0, 0.0).astype(BF16))
    index = lax.broadcasted_iota(jnp.int32, (rows.shape[0], width), 0).astype(F32)
    return jnp.sum(jnp.where(index == owner * SUB + row, spread_out, 0.0), axis=0, keepdims=True)


def rates_of(real, rotation, step_log):
    timestep = jnp.exp(step_log)
    magnitude = jnp.exp(real * timestep)
    turned = rotation * timestep
    factor_re = magnitude * jnp.cos(turned)
    factor_im = magnitude * jnp.sin(turned)
    modulus = real * real + rotation * rotation
    scale_re = ((factor_re - 1.0) * real + factor_im * rotation) / modulus
    scale_im = (factor_im * real - (factor_re - 1.0) * rotation) / modulus
    return timestep, factor_re, factor_im, modulus, scale_re, scale_im


def cross_blocks(members, reverse, pieces, place, own_place, broken, flow_re, flow_im, dealt, carries):
    states = flow_re.shape[1]
    total = place.shape[1]
    steps = total // members
    rows = lax.broadcasted_iota(jnp.int32, (total, total), 0).astype(F32)
    chosen = jnp.where(rows == place[...], 1.0, 0.0).astype(BF16)
    dealt[...] = dot(chosen, pieces[...].reshape(total, 2 * states))
    rate_re = spread(flow_re, members)
    rate_im = spread(-flow_im if reverse else flow_im, members)
    marks = [broken[s] for s in range(broken.shape[0])]

    def step(i, state):
        re, im = state
        p = steps - 1 - i if reverse else i
        at = pl.multiple_of(p * members, members)
        here = dealt[pl.ds(at, members), :]
        met = marks[0] == p
        for mark in marks[1:]:
            met = met | (mark == p)
        mask = lanes_to(jnp.where(met, 0.0, 1.0), states)
        dealt[pl.ds(at, members), :] = jnp.concatenate([re, im], axis=1)
        return (
            mask * (rate_re * re - rate_im * im) + here[:, :states],
            mask * (rate_re * im + rate_im * re) + here[:, states:],
        )

    zero = jnp.zeros((members, states), F32)
    lax.fori_loop(0, steps, step, (zero, zero), unroll=4)
    own = own_place.shape[0]
    columns = lax.broadcasted_iota(jnp.int32, (own, total), 1).astype(F32)
    taken = jnp.where(columns == lanes_to(own_place[...], total), 1.0, 0.0).astype(BF16)
    high = dealt[...].astype(BF16)
    low = (dealt[...] - high.astype(F32)).astype(BF16)
    carries[...] = dot(taken, high) + dot(taken, low)


def front_kernel(
    grid, block_rows, counts, tokens, gain_s, shift_s, through_s, bias_s, real_s, rotation_s, step_s, target_s,
    lengths_s, drive_s, readout_s, mixer_s, perm,
    dealt, driven, keep, carries, drive, drive_raw, readout_w, mixer_w, vectors, rates, place, own_place, broken,
    xhat, table, drive_w, bits, pieces, dealt_ends, send, recv, local, push_send, push_recv,
):
    i = pl.program_id(0)
    tiles = (pl.num_programs(0) - 1) // 2
    row, column, mine = grid.here()
    members = 2**grid.bits
    blocks = target_s.shape[0]
    tile = tokens.shape[0]
    width = tokens.shape[1]
    both = drive.shape[1]
    states = both // 2
    span = SUB * block_rows
    chains = tile // span
    tile_blocks = tile // block_rows
    axes = tuple(range(grid.bits + 1))
    wholes = (table, drive_w, readout_w, mixer_w)
    dims = list(range(grid.bits))
    orders = grid.orders(dims, (grid.bits,))
    orders = [orders[0], orders[0], orders[1 % len(orders)], orders[2 % len(orders)]]
    slots = grid.dp - 1 + grid.bits
    phases = grid.bits + 1

    def phase_copies(k, phase):
        order = orders[k]
        base = k * slots + sum(len(grid.peers(d)) for d in order[:phase])
        return gather_phase(grid, wholes[k], axes, order[phase], order[:phase], send, recv, base)

    def advance(ks, phase):
        for k in ks:
            if phase:
                for copy in phase_copies(k, phase - 1):
                    copy.wait()
            if phase < phases:
                for copy in phase_copies(k, phase):
                    copy.start()

    @pl.when(i == 0)
    def _():
        copies = [
            pltpu.make_async_copy(shard, ref.at[tuple(mine)], local.at[k])
            for k, (shard, ref) in enumerate(zip((drive_s, readout_s, mixer_s), wholes[1:]))
        ]
        for copy in copies:
            copy.start()
        held = [gain_s, shift_s, through_s, bias_s, real_s, rotation_s, step_s, target_s]
        own = table.at[tuple(mine)]
        own[...] = jnp.zeros_like(own)
        for k, ref in enumerate(held):
            own[k : k + 1, : ref.shape[0]] = ref[...].astype(F32).reshape(1, ref.shape[0])
        sequences = lengths_s.shape[1]
        own[4:5, LANES // 2 : LANES // 2 + sequences] = lengths_s[...].astype(F32)
        greet(grid)
        for copy in copies:
            copy.wait()
        advance((0, 1, 2, 3), 0)

    for phase in range(1, phases):
        @pl.when(i == min(2 * phase, tiles))
        def _():
            advance((0, 1), phase)

        @pl.when(i == min(4 * phase - 1, 2 * tiles - 2))
        def _():
            advance((2, 3), phase)

    @pl.when(i < tiles)
    def _():
        moved, rstd = norm_stats(tokens[...].astype(F32))
        xhat[pl.ds(pl.multiple_of(i * tile, tile), tile), :] = moved * rstd

    @pl.when(i == tiles)
    def _():
        advance((0, 1), phases)
        rows = table[...].reshape(-1, LANES)
        vectors[...] = jnp.zeros_like(vectors)
        for k, size in enumerate((width, width, width, 2 * width)):
            vectors[k : k + 1, :size] = unpack(rows, k, counts[k], size)
        real, rotation, step_log = [unpack(rows, k, counts[k], states) for k in (4, 5, 6)]
        _, factor_re, factor_im, _, scale_re, scale_im = rates_of(real, rotation, step_log)
        flow_re, flow_im = factor_re, factor_im
        power = 1
        while power < block_rows:
            flow_re, flow_im = flow_re * flow_re - flow_im * flow_im, 2.0 * flow_re * flow_im
            power *= 2
        for k, value in enumerate((factor_re, factor_im, flow_re, flow_im, real, rotation, step_log)):
            rates[k : k + 1, :] = value
        drive_raw[...] = drive_w[...].reshape(width, both)
        raw = drive_raw[...].astype(F32)
        drive[:, :states] = (scale_re * raw[:, :states] - scale_im * raw[:, states:]).astype(BF16)
        drive[:, states:] = (scale_re * raw[:, states:] + scale_im * raw[:, :states]).astype(BF16)
        group = table[row].reshape(members * SUB, LANES)
        for m in range(members):
            q = group[m * SUB + 7 : m * SUB + 8, :blocks]
            d = jnp.floor(q * (1.0 / blocks))
            place[:, m * blocks : (m + 1) * blocks] = (q - d * blocks) * members + d
        lengths = jnp.concatenate([group[m * SUB + 4 : m * SUB + 5, :] for m in range(members)], axis=0)
        sequences = lengths_s.shape[1]
        q = table[tuple(mine) + (slice(7, 8), slice(None))]
        diagonal = lax.broadcasted_iota(jnp.int32, (blocks, LANES), 0) == lax.broadcasted_iota(
            jnp.int32, (blocks, LANES), 1
        )
        q = jnp.sum(jnp.where(diagonal, jnp.broadcast_to(q, (blocks, LANES)), 0.0), axis=1, keepdims=True)
        q = jnp.broadcast_to(q, (blocks, LANES))
        d = jnp.floor(q * (1.0 / blocks))
        p = q - d * blocks
        own_place[...] = p * members + d
        start = jnp.zeros((members, LANES), F32)
        marks = jnp.zeros((blocks, LANES), jnp.int32)
        for s in range(sequences):
            broken[s] = jnp.floor(start * (1.0 / block_rows)).astype(jnp.int32)
            mark = jnp.zeros((blocks, LANES), F32)
            for m in range(members):
                mark = jnp.where(d == float(m), jnp.broadcast_to(start[m : m + 1, :], (blocks, LANES)), mark)
            mark = mark - p * block_rows
            inside = (mark >= 0.0) & (mark < block_rows)
            shift = jnp.where(inside, mark, 0.0).astype(jnp.int32)
            marks = marks | jnp.where(inside, lax.shift_left(jnp.ones_like(shift), shift), 0)
            column_of = lengths[:, LANES // 2 + s : LANES // 2 + s + 1]
            start = start + jnp.broadcast_to(column_of, (members, LANES))
        bits[...] = marks

    def pushes(j):
        at = (column, pl.ds(pl.multiple_of(j * tile_blocks, tile_blocks), tile_blocks))
        return push_to(at)

    def push_to(at):
        far = [
            remote(
                pieces.at[at], pieces.at[at], push_send.at[away // 2], push_recv.at[away // 2],
                {"fsdp": lax.rem(column + away, members)},
            )
            for away in range(2, members, 2)
        ]
        near = remote(pieces.at[at], pieces.at[at], push_send.at[0], push_recv.at[0], {"fsdp": sibling})
        return far + [near]

    sibling = column + 1 - 2 * mine[-1]

    @pl.when((i >= tiles) & (i < 2 * tiles))
    def _():
        j = i - tiles
        gain = vectors[0:1, :width]
        shift = vectors[1:2, :width]
        normed = xhat[pl.ds(pl.multiple_of(j * tile, tile), tile), :] * gain + shift
        dealt[...] = permute_tile(perm[...], normed.astype(BF16), span).astype(BF16)
        driven[...] = dot(dealt[...], drive[...])
        rate_re = spread(rates[0:1, :], SUB)
        rate_im = spread(rates[1:2, :], SUB)
        first = pl.multiple_of(j * tile_blocks, tile_blocks)
        mark = bits[pl.ds(first, tile_blocks), :]
        state = [(jnp.zeros((SUB, states), F32), jnp.zeros((SUB, states), F32)) for _ in range(chains)]
        for t in range(block_rows):
            single = 1 << t if t < 31 else -(1 << 31)
            for c in range(chains):
                at = c * span + t * SUB
                narrow = jnp.where((mark[c * SUB : (c + 1) * SUB] & single) == 0, 1.0, 0.0)
                keep[at : at + SUB, :] = narrow
                mask = lanes_to(narrow, states)
                re, im = state[c]
                now_re = mask * (rate_re * re - rate_im * im) + driven[at : at + SUB, :states]
                now_im = mask * (rate_re * im + rate_im * re) + driven[at : at + SUB, states:]
                state[c] = (now_re, now_im)
        ends = jnp.concatenate([jnp.concatenate(state[c], axis=1) for c in range(chains)], axis=0)
        pieces[column, pl.ds(first, tile_blocks), :] = ends.astype(BF16)
        for copy in pushes(j):
            copy.start()

    @pl.when(i == 2 * tiles)
    def _():
        onward = []
        for k, copy in enumerate(push_to((column,))[:-1]):
            copy.wait()
            from_there = lax.rem(column + members - 2 * (k + 1), members)
            slot = members // 2 + k
            onward.append(
                remote(
                    pieces.at[from_there], pieces.at[from_there], push_send.at[slot], push_recv.at[slot],
                    {"fsdp": sibling},
                )
            )
            onward[-1].start()
        push_to((column,))[-1].wait()
        for copy in onward:
            copy.wait()
        cross_blocks(
            members, False, pieces, place, own_place, broken, rates[2:3, :], rates[3:4, :], dealt_ends, carries
        )
        advance((2, 3), phases)


def main_kernel(
    grid, block_rows, cotangent, dealt, driven, carry, keep, rates, readout, vectors, mixer, perm, back, place,
    own_place, broken,
    gated_low, mixed_low, joined, joined_grad, weight_grad, bias_grad, through_grad, readout_grad, coming,
    pieces, dealt_heads, push_send, push_recv,
):
    i = pl.program_id(0)
    tiles = pl.num_programs(0) - 1
    _, column, _ = grid.here()
    members = 2**grid.bits
    span = SUB * block_rows
    tile, width = cotangent.shape
    states = rates.shape[1]
    chains = tile // span
    tile_blocks = tile // block_rows

    def push_to(at):
        return [
            remote(
                pieces.at[at], pieces.at[at], push_send.at[away - 1], push_recv.at[away - 1],
                {"fsdp": lax.rem(column + away, members)},
            )
            for away in range(1, members)
        ]

    @pl.when(i == 0)
    def _():
        weight_grad[...] = jnp.zeros_like(weight_grad)
        bias_grad[...] = jnp.zeros_like(bias_grad)
        through_grad[...] = jnp.zeros_like(through_grad)
        readout_grad[...] = jnp.zeros_like(readout_grad)
        greet(grid)

    @pl.when(i < tiles)
    def _():
        through = vectors[2:3, :width]
        bias = vectors[3:4, : 2 * width]
        rate_re = spread(rates[0:1, :], SUB)
        rate_im = spread(rates[1:2, :], SUB)
        state = [
            (carry[c * SUB : (c + 1) * SUB, :states], carry[c * SUB : (c + 1) * SUB, states:])
            for c in range(chains)
        ]
        for t in range(0, block_rows, 2):
            for c in range(chains):
                held = []
                for step in (t, t + 1):
                    at = c * span + step * SUB
                    mask = lanes_to(keep[at : at + SUB, :], states)
                    re, im = state[c]
                    now_re = mask * (rate_re * re - rate_im * im) + driven[at : at + SUB, :states]
                    now_im = mask * (rate_re * im + rate_im * re) + driven[at : at + SUB, states:]
                    state[c] = (now_re, now_im)
                    held.append(state[c])
                at = c * span + t * SUB
                joined[at : at + 2 * SUB, :states] = jnp.concatenate([held[0][0], held[1][0]], axis=0).astype(BF16)
                joined[at : at + 2 * SUB, states:] = (-jnp.concatenate([held[0][1], held[1][1]], axis=0)).astype(BF16)

        dealt_f32 = dealt[...].astype(F32)
        mixed = dot(joined[...], readout[...]) + through * dealt_f32
        activated, slope = gelu_parts(mixed)
        features = permute_tile(back[...], activated.astype(BF16), span).astype(BF16)
        hidden = dot(features, mixer[...]) + bias
        value = hidden[:, :width]
        sig = 1.0 / (1.0 + jnp.exp(-hidden[:, width:]))
        gated_low[...] = (value * sig).astype(BF16)
        cot_sig = cotangent[...].astype(F32) * sig
        hidden_low = jnp.concatenate(
            [cot_sig.astype(BF16), (cot_sig * value * (1.0 - sig)).astype(BF16)], axis=1
        )
        weight_grad[...] += contract_rows(features, hidden_low)
        bias_grad[...] += jnp.sum(hidden_low.astype(F32), axis=0, keepdims=True)
        feature_grad = contract_cols(hidden_low, mixer[...]).astype(BF16)
        mixed_grad = (permute_tile(perm[...], feature_grad, span) * slope).astype(BF16)
        mixed_low[...] = mixed_grad
        through_grad[...] += jnp.sum(mixed_grad.astype(F32) * dealt_f32, axis=0, keepdims=True)
        readout_grad[...] += contract_rows(joined[...], mixed_grad)
        joined_grad[...] = contract_cols(mixed_grad, readout[...])

        going = [(jnp.zeros((SUB, states), F32), jnp.zeros((SUB, states), F32)) for _ in range(chains)]
        for t in reversed(range(block_rows)):
            for c in range(chains):
                at = c * span + t * SUB
                mask = lanes_to(keep[at : at + SUB, :], states)
                re = joined_grad[at : at + SUB, :states] + going[c][0]
                im = going[c][1] - joined_grad[at : at + SUB, states:]
                going[c] = (mask * (rate_re * re + rate_im * im), mask * (rate_re * im - rate_im * re))
        heads = jnp.concatenate([jnp.concatenate(going[c], axis=1) for c in range(chains)], axis=0)
        at = (column, pl.ds(pl.multiple_of(i * tile_blocks, tile_blocks), tile_blocks))
        pieces[at + (slice(None),)] = heads.astype(BF16)
        for copy in push_to(at):
            copy.start()

    @pl.when(i == tiles)
    def _():
        for copy in push_to((column,)):
            copy.wait()
        cross_blocks(
            members, True, pieces, place, own_place, broken, rates[2:3, :], rates[3:4, :], dealt_heads, coming
        )


def last_kernel(
    grid, block_rows, orders, dealt, joined, joined_grad, carry, coming, keep, mixed_low, tokens, rates, vectors, drive,
    drive_raw, back, readout_grad, weight_grad, bias_grad, through_grad,
    given_low, drive_sum, readout_sum, weight_sum, vector_sum,
    driven_all, drive_grad, drive_parts, decay_cot, gain_grad, shift_grad, *rest,
):
    i = pl.program_id(0)
    tiles = (pl.num_programs(0) - 1) // 2
    row, column, mine = grid.here()
    members = 2**grid.bits
    core = grid.bits
    phases = grid.bits + 1
    span = SUB * block_rows
    tile, width = tokens.shape
    both = joined.shape[1]
    states = both // 2
    chains = tile // span
    rest = list(rest)
    parts = (readout_grad, weight_grad, drive_parts)
    outs = (readout_sum, weight_sum, drive_sum)
    count = len(parts)
    accs = [rest.pop(0) for _ in range(count)]
    stages = [[rest.pop(0) for _ in range(phases)] for _ in range(count)]
    landed = [[rest.pop(0) for _ in range(phases)] for _ in range(count)]
    vector_stage, across, along, send, recv, vector_send, vector_recv = rest
    plans = [reduce_plan(grid, order) for order in orders]
    slots = grid.dp - 1 + grid.bits
    every = tuple(range(grid.bits + 1))
    kept = every[:-1]

    def combos(left):
        return list(itertools.product(*[range(grid.shape[d]) for d in left]))

    def at(dim, index, left, combo, dims):
        chosen = dict(zip(left, combo))
        chosen[dim] = index
        return tuple(chosen[d] if d in chosen else mine[d] for d in dims)

    def hops(k, phase):
        dim = plans[k][phase][0]
        base = k * slots + sum(len(grid.peers(d)) for d in orders[k][:phase])
        return [
            (
                remote(
                    stages[k][phase].at[slot], landed[k][phase].at[slot], send.at[base + slot], recv.at[base + slot],
                    device,
                ),
                slot,
                index,
            )
            for slot, device, index in grid.peers(dim)
        ]

    def begin(k, phase):
        dim, _, left = plans[k][phase]
        for copy, slot, index in hops(k, phase):
            for combo in combos(left):
                if dim == core:
                    piece = parts[k][at(dim, index, left, combo, every)]
                else:
                    piece = accs[k][at(dim, index, left, combo, kept)]
                stages[k][phase][(slot,) + combo] = piece.astype(BF16)
            copy.start()

    def finish(k, phase):
        dim, _, left = plans[k][phase]
        copies = hops(k, phase)
        for copy, _, _ in copies:
            copy.wait()
        for combo in combos(left):
            if dim == core:
                piece = parts[k][at(dim, mine[dim], left, combo, every)]
            else:
                piece = accs[k][at(dim, mine[dim], left, combo, kept)]
            for _, slot, _ in copies:
                piece = piece + landed[k][phase][(slot,) + combo].astype(F32)
            accs[k][at(dim, mine[dim], left, combo, kept)] = piece

    def advance(ks, phase):
        for k in ks:
            if phase:
                finish(k, phase - 1)
            if phase < phases:
                begin(k, phase)
            else:
                outs[k][...] = accs[k][tuple(mine[:-1])]

    rate_re = spread(rates[0:1, :], SUB)
    rate_im = spread(rates[1:2, :], SUB)

    @pl.when(i == 0)
    def _():
        drive_grad[...] = jnp.zeros_like(drive_grad)
        decay_cot[...] = jnp.zeros_like(decay_cot)
        gain_grad[...] = jnp.zeros_like(gain_grad)
        shift_grad[...] = jnp.zeros_like(shift_grad)
        greet(grid)
        advance((0, 1), 0)

    for phase in range(1, phases + 1):
        @pl.when(i == min(2 * phase, 2 * tiles - 1))
        def _():
            advance((0, 1), phase)

    @pl.when(i < tiles)
    def _():
        driven_low = driven_all.at[pl.ds(pl.multiple_of(i * tile, tile), tile)]
        going = [
            (coming[c * SUB : (c + 1) * SUB, :states], coming[c * SUB : (c + 1) * SUB, states:])
            for c in range(chains)
        ]
        total = [(jnp.zeros((SUB, states), F32), jnp.zeros((SUB, states), F32)) for _ in range(chains)]
        for t in reversed(range(0, block_rows, 2)):
            for c in range(chains):
                pair = c * span + t * SUB
                here_re = joined[pair : pair + SUB, :states].astype(F32)
                here_im = -joined[pair : pair + SUB, states:].astype(F32)
                if t == 0:
                    past_re = carry[c * SUB : (c + 1) * SUB, :states]
                    past_im = carry[c * SUB : (c + 1) * SUB, states:]
                else:
                    past_re = joined[pair - SUB : pair, :states].astype(F32)
                    past_im = -joined[pair - SUB : pair, states:].astype(F32)
                held = {}
                for step, (prev_re, prev_im) in ((t + 1, (here_re, here_im)), (t, (past_re, past_im))):
                    where = c * span + step * SUB
                    mask = lanes_to(keep[where : where + SUB, :], states)
                    re = joined_grad[where : where + SUB, :states] + going[c][0]
                    im = going[c][1] - joined_grad[where : where + SUB, states:]
                    held[step] = (re, im)
                    on_re = mask * (rate_re * re + rate_im * im)
                    on_im = mask * (rate_re * im - rate_im * re)
                    going[c] = (on_re, on_im)
                    total[c] = (
                        total[c][0] + (on_re * prev_re + on_im * prev_im),
                        total[c][1] + (on_im * prev_re - on_re * prev_im),
                    )
                driven_low[pair : pair + 2 * SUB, :states] = jnp.concatenate(
                    [held[t][0], held[t + 1][0]], axis=0
                ).astype(BF16)
                driven_low[pair : pair + 2 * SUB, states:] = jnp.concatenate(
                    [held[t][1], held[t + 1][1]], axis=0
                ).astype(BF16)
        for c in range(chains):
            decay_cot[...] += jnp.concatenate(total[c], axis=1)
        drive_grad[...] += contract_rows(dealt[...], driven_low[...])

    @pl.when(i == tiles)
    def _():
        shard = drive_parts.shape[-2]
        for s, place in enumerate(itertools.product(*[range(size) for size in grid.shape])):
            drive_parts[place] = drive_grad[s * shard : (s + 1) * shard, :]
        advance((2,), 0)

    for phase in range(1, phases):
        @pl.when(i == min(tiles + 2 * phase, 2 * tiles))
        def _():
            advance((2,), phase)

    @pl.when((i >= tiles) & (i < 2 * tiles))
    def _():
        j = i - tiles
        driven_low = driven_all[pl.ds(pl.multiple_of(j * tile, tile), tile), :]
        normed_grad = vectors[2:3, :width] * mixed_low[...].astype(F32) + contract_cols(driven_low, drive[...])
        given = permute_tile(back[...], normed_grad.astype(BF16), span)
        given_low[...] = given.astype(BF16)
        moved, rstd = norm_stats(tokens[...].astype(F32))
        gain_grad[...] += jnp.sum(given * (moved * rstd), axis=0, keepdims=True)
        shift_grad[...] += jnp.sum(given, axis=0, keepdims=True)

    @pl.when(i == 2 * tiles)
    def _():
        cot = jnp.sum(decay_cot[...], axis=0, keepdims=True)
        factor_re, factor_im = rates[0:1, :], rates[1:2, :]
        size = factor_re * factor_re + factor_im * factor_im
        vector_stage[...] = jnp.zeros_like(vector_stage)
        vector_stage[0:1, :width] = gain_grad[...]
        vector_stage[1:2, :width] = shift_grad[...]
        vector_stage[2:3, :width] = through_grad[...]
        vector_stage[3:4, :] = bias_grad[:, :both]
        vector_stage[4:5, : 2 * width - both] = bias_grad[:, both:]
        vector_stage[5:6, :states] = (cot[:, :states] * factor_re - cot[:, states:] * factor_im) / size
        vector_stage[5:6, states:] = (cot[:, :states] * factor_im + cot[:, states:] * factor_re) / size
        d_re, d_im = drive_grad[:, :states], drive_grad[:, states:]
        b_re, b_im = drive_raw[:, :states].astype(F32), drive_raw[:, states:].astype(F32)
        vector_stage[6:7, :states] = jnp.sum(d_re * b_re + d_im * b_im, axis=0, keepdims=True)
        vector_stage[6:7, states:] = jnp.sum(d_im * b_re - d_re * b_im, axis=0, keepdims=True)

        copies = [
            remote(
                vector_stage, across.at[away - 1], vector_send.at[away - 1], vector_recv.at[away - 1],
                {"fsdp": lax.rem(column + away, members)},
            )
            for away in range(1, members)
        ]
        for copy in copies:
            copy.start()
        for copy in copies:
            copy.wait()
        total = vector_stage[...]
        for k in range(members - 1):
            total = total + across[k]
        vector_sum[...] = total
        copies = [
            remote(
                vector_sum, along.at[away - 1], vector_send.at[members - 2 + away], vector_recv.at[members - 2 + away],
                {"dp": lax.rem(row + away, grid.dp)},
            )
            for away in range(1, grid.dp)
        ]
        for copy in copies:
            copy.start()
        advance((2,), phases)
        for copy in copies:
            copy.wait()
        total = vector_sum[...]
        for k in range(grid.dp - 1):
            total = total + along[k]
        vector_sum[...] = total


def tail_kernel(
    grid, tokens, cotangent, given_low, gated_low, vectors, rates, drive_sum, readout_sum, weight_sum, vector_sum,
    out, token_grad, gain_grad, shift_grad, real_grad, rotation_grad, timestep_grad, drive_grad, readout_grad,
    through_grad, weight_grad, bias_grad,
):
    width = tokens.shape[1]
    both = vector_sum.shape[1]
    states = both // 2
    rows = tokens[...].astype(F32)
    out[...] = rows + gated_low[...].astype(F32)
    moved, rstd = norm_stats(rows)
    xhat = moved * rstd
    scaled = given_low[...].astype(F32) * vectors[0:1, :width]
    inner = jnp.mean(scaled * xhat, axis=-1, keepdims=True)
    token_grad[...] = cotangent[...].astype(F32) + rstd * (
        scaled - jnp.mean(scaled, axis=-1, keepdims=True) - xhat * inner
    )

    @pl.when(pl.program_id(0) == 0)
    def _():
        row, column, _ = grid.here()
        me = row * 2**grid.bits + column
        real, rotation, step_log = [rates[k : k + 1, :] for k in (4, 5, 6)]
        timestep, factor_re, factor_im, modulus, scale_re, scale_im = rates_of(real, rotation, step_log)
        d_re, d_im = drive_sum[:, :states], drive_sum[:, states:]
        drive_grad[:, :states] = scale_re * d_re + scale_im * d_im
        drive_grad[:, states:] = scale_re * d_im - scale_im * d_re
        readout_grad[...] = readout_sum[...]
        weight_grad[...] = weight_sum[...]
        s_re, s_im = vector_sum[6:7, :states], vector_sum[6:7, states:]
        total_re = vector_sum[5:6, :states] + (s_re * real - s_im * rotation) / modulus
        total_im = vector_sum[5:6, states:] + (s_re * rotation + s_im * real) / modulus
        ratio_re = (scale_re * real + scale_im * rotation) / modulus
        ratio_im = (scale_im * real - scale_re * rotation) / modulus
        lambda_re = timestep * (total_re * factor_re + total_im * factor_im) - (s_re * ratio_re + s_im * ratio_im)
        lambda_im = timestep * (total_im * factor_re - total_re * factor_im) - (s_im * ratio_re - s_re * ratio_im)
        turn_re = real * factor_re - rotation * factor_im
        turn_im = real * factor_im + rotation * factor_re
        step_grad = timestep * (total_re * turn_re + total_im * turn_im)

        def own(vector, target):
            length, size = vector.shape[1], target.shape[0]
            wide = jnp.broadcast_to(vector, (SUB, length))
            rolled = pltpu.roll(wide, lax.rem(length - me * size, length), 1)
            target[...] = rolled[0:1, :size].reshape(size)

        own(vector_sum[0:1, :width], gain_grad)
        own(vector_sum[1:2, :width], shift_grad)
        own(vector_sum[2:3, :width], through_grad)
        own(jnp.concatenate([vector_sum[3:4, :], vector_sum[4:5, : 2 * width - both]], axis=1), bias_grad)
        own(lambda_re, real_grad)
        own(lambda_im, rotation_grad)
        own(step_grad, timestep_grad)


def whole(shape):
    return pl.BlockSpec(shape, lambda i: (0,) * len(shape), pipeline_mode=pl.Buffered(1))


def total_of(shape):
    return pl.BlockSpec(shape, lambda i: (0,) * len(shape))


def tiled(rows, columns):
    return pl.BlockSpec((rows, columns), lambda i: (i, 0))


def params(cid=None):
    if cid is None:
        return pltpu.CompilerParams(dimension_semantics=("arbitrary",), vmem_limit_bytes=VMEM_LIMIT)
    return pltpu.CompilerParams(
        dimension_semantics=("arbitrary",), vmem_limit_bytes=VMEM_LIMIT, collective_id=cid, has_side_effects=True
    )


def body(
    tokens, cotangent, block_target, sequence_lengths, norm_gain, norm_shift, decay_real, decay_rotation,
    log_timestep, drive_matrix, readout_matrix, feedthrough, mixer_weight, mixer_bias,
):
    members = lax.axis_size("fsdp")
    grid = Grid((lax.axis_size("dp"), members))
    blocks = block_target.shape[0]
    rows, width = tokens.shape
    both = drive_matrix.shape[1]
    states = both // 2
    block_rows = rows // blocks
    span = SUB * block_rows
    tile = 2 * span
    tiles = rows // tile
    tile_blocks = tile // block_rows
    total = blocks * members
    sequences = sequence_lengths.shape[1]
    shape = jax.ShapeDtypeStruct
    anywhere = pl.BlockSpec(memory_space=pl.ANY)
    regular = pltpu.SemaphoreType.DMA

    order = jnp.arange(span, dtype=jnp.int32)
    source = (order % SUB) * block_rows + order // SUB
    perm = (source[:, None] == order[None]).astype(BF16)
    back = (order[:, None] == source[None]).astype(BF16)

    def early(rows_of, columns):
        return pl.BlockSpec((rows_of, columns), lambda i: (jnp.minimum(i, tiles - 1), 0))

    def late(rows_of, columns):
        return pl.BlockSpec((rows_of, columns), lambda i: (jnp.clip(i - tiles, 0, tiles - 1), 0))

    def flat(size):
        return pl.BlockSpec((size,), lambda i: (0,))

    small = (norm_gain, norm_shift, feedthrough, mixer_bias, decay_real, decay_rotation, log_timestep, block_target)
    counts = tuple(v.shape[0] for v in small)
    shards = (drive_matrix, readout_matrix, mixer_weight)
    slots = grid.dp - 1 + grid.bits
    dealt, driven, keep, carry, drive, drive_raw, readout, mixer, vectors, rates, place, own_place, broken = pl.pallas_call(
        functools.partial(front_kernel, grid, block_rows, counts),
        grid=(2 * tiles + 1,),
        in_specs=[early(tile, width)]
        + [flat(size) for size in counts]
        + [whole((1, sequences)), anywhere, anywhere, anywhere, whole((span, span))],
        out_specs=[
            late(tile, width), late(tile, both), late(tile, LANES), total_of((blocks, both)), total_of((width, both)),
            total_of((width, both)), anywhere, anywhere, total_of((SUB, 2 * width)), total_of((SUB, states)),
            total_of((1, total)), total_of((blocks, LANES)), total_of((sequences, members, LANES)),
        ],
        out_shape=[
            shape((rows, width), BF16), shape((rows, both), F32), shape((rows, LANES), F32), shape((blocks, both), F32),
            shape((width, both), BF16), shape((width, both), BF16),
            shape(grid.shape + readout_matrix.shape, BF16), shape(grid.shape + mixer_weight.shape, BF16),
            shape((SUB, 2 * width), F32), shape((SUB, states), F32), shape((1, total), F32),
            shape((blocks, LANES), F32), shape((sequences, members, LANES), jnp.int32),
        ],
        scratch_shapes=[
            pltpu.VMEM((rows, width), F32),
            pltpu.VMEM(grid.shape + (SUB, LANES), F32),
            pltpu.VMEM(grid.shape + drive_matrix.shape, BF16),
            pltpu.VMEM((blocks, LANES), jnp.int32),
            pltpu.VMEM((members, blocks, both), BF16),
            pltpu.VMEM((total, both), F32),
            regular((4 * slots,)), regular((4 * slots,)), regular((len(shards),)), regular((members,)), regular((members,)),
        ],
        compiler_params=params(0),
        name="front",
    )(tokens, *small, sequence_lengths, *shards, perm)
    readout = readout.reshape(both, width)
    mixer = mixer.reshape(width, 2 * width)

    gated_low, mixed_low, joined, joined_grad, weight_grad, bias_grad, through_grad, readout_grad, coming = pl.pallas_call(
        functools.partial(main_kernel, grid, block_rows),
        grid=(tiles + 1,),
        in_specs=[
            early(tile, width), early(tile, width), early(tile, both), early(tile_blocks, both),
            early(tile, LANES), whole((SUB, states)), whole((both, width)), whole((SUB, 2 * width)),
            whole((width, 2 * width)), whole((span, span)), whole((span, span)), whole((1, total)),
            whole((blocks, LANES)), whole((sequences, members, LANES)),
        ],
        out_specs=[
            early(tile, width), early(tile, width), early(tile, both), early(tile, both),
            total_of((width, 2 * width)), total_of((1, 2 * width)), total_of((1, width)), total_of((both, width)),
            total_of((blocks, both)),
        ],
        out_shape=[
            shape((rows, width), BF16), shape((rows, width), BF16), shape((rows, both), BF16),
            shape((rows, both), F32), shape((width, 2 * width), F32), shape((1, 2 * width), F32),
            shape((1, width), F32), shape((both, width), F32), shape((blocks, both), F32),
        ],
        scratch_shapes=[
            pltpu.VMEM((members, blocks, both), BF16), pltpu.VMEM((total, both), F32), regular((members - 1,)),
            regular((members - 1,)),
        ],
        compiler_params=params(1),
        name="main",
    )(cotangent, dealt, driven, carry, keep, rates, readout, vectors, mixer, perm, back, place, own_place, broken)

    dims = list(range(grid.bits))
    turns = grid.orders(dims, ())
    orders = [(grid.bits,) + turns[k % len(turns)] for k in range(3)]
    weights = (readout_matrix, mixer_weight, drive_matrix)
    buffers = []
    for turn, weight in zip(orders, weights):
        for dim, _, left in reduce_plan(grid, turn):
            fan = grid.dp - 1 if dim == 0 else 1
            buffers.append(pltpu.VMEM((fan,) + tuple(grid.shape[d] for d in left) + weight.shape, BF16))
    given_low, drive_sum, readout_sum, weight_sum, vector_sum = pl.pallas_call(
        functools.partial(last_kernel, grid, block_rows, orders),
        grid=(2 * tiles + 1,),
        in_specs=[
            early(tile, width), early(tile, both), early(tile, both), early(tile_blocks, both), early(tile_blocks, both),
            early(tile, LANES), late(tile, width), late(tile, width), whole((SUB, states)), whole((SUB, 2 * width)),
            whole((width, both)), whole((width, both)), whole((span, span)), whole(grid.shape + readout_matrix.shape),
            whole(grid.shape + mixer_weight.shape), whole((1, 2 * width)), whole((1, width)),
        ],
        out_specs=[
            late(tile, width), total_of(drive_matrix.shape), total_of(readout_matrix.shape),
            total_of(mixer_weight.shape), total_of((SUB, both)),
        ],
        out_shape=[
            shape((rows, width), BF16), shape(drive_matrix.shape, F32), shape(readout_matrix.shape, F32),
            shape(mixer_weight.shape, F32), shape((SUB, both), F32),
        ],
        scratch_shapes=[
            pltpu.VMEM((rows, both), BF16), pltpu.VMEM((width, both), F32),
            pltpu.VMEM(grid.shape + drive_matrix.shape, F32), pltpu.VMEM((SUB, both), F32),
            pltpu.VMEM((1, width), F32), pltpu.VMEM((1, width), F32),
        ]
        + [pltpu.VMEM(grid.shape[:-1] + weight.shape, F32) for weight in weights]
        + buffers
        + buffers
        + [
            pltpu.VMEM((SUB, both), F32), pltpu.VMEM((members - 1, SUB, both), F32),
            pltpu.VMEM((grid.dp - 1, SUB, both), F32), regular((3 * slots,)), regular((3 * slots,)),
            regular((members + grid.dp - 2,)), regular((members + grid.dp - 2,)),
        ],
        compiler_params=params(2),
        name="last",
    )(
        dealt, joined, joined_grad, carry, coming, keep, mixed_low, tokens, rates, vectors, drive, drive_raw, back,
        readout_grad.reshape(grid.shape + readout_matrix.shape), weight_grad.reshape(grid.shape + mixer_weight.shape),
        bias_grad, through_grad,
    )

    vector_sizes = [v.shape[0] for v in (norm_gain, norm_shift, decay_real, decay_rotation, log_timestep)]
    outs = pl.pallas_call(
        functools.partial(tail_kernel, grid),
        grid=(tiles,),
        in_specs=[tiled(tile, width)] * 4
        + [
            whole((SUB, 2 * width)), whole((SUB, states)), whole(drive_matrix.shape), whole(readout_matrix.shape),
            whole(mixer_weight.shape), whole((SUB, both)),
        ],
        out_specs=[tiled(tile, width)] * 2
        + [flat(size) for size in vector_sizes]
        + [
            total_of(drive_matrix.shape), total_of(readout_matrix.shape), flat(feedthrough.shape[0]),
            total_of(mixer_weight.shape), flat(mixer_bias.shape[0]),
        ],
        out_shape=[shape((rows, width), F32)] * 2
        + [shape((size,), F32) for size in vector_sizes]
        + [
            shape(drive_matrix.shape, F32), shape(readout_matrix.shape, F32), shape(feedthrough.shape, F32),
            shape(mixer_weight.shape, F32), shape(mixer_bias.shape, F32),
        ],
        compiler_params=params(),
        name="tail",
    )(tokens, cotangent, given_low, gated_low, vectors, rates, drive_sum, readout_sum, weight_sum, vector_sum)
    return tuple(outs)


def solution(mesh):
    rows = P(AXES, None)
    flat = P(AXES)
    return jax.shard_map(
        body,
        mesh=mesh,
        in_specs=(rows, rows, flat, rows, flat, flat, flat, flat, flat, rows, rows, flat, rows, flat),
        out_specs=(rows, rows, flat, flat, flat, flat, flat, rows, rows, flat, rows, flat),
        check_vma=False,
    )
```

time: 1870 us -> 177 us (0.09); the launches traced: 1840 us -> 177 us
  local copies, waits for them, and re-layouts: 635 us -> 0 us
  waiting for transfers between devices: 430 us -> 0 us
  other arithmetic: 379 us -> 0.77 us
  blocking collectives: 247 us -> 0 us
  Pallas kernels: 0 us -> 175 us
  matrix products: 106 us -> 0 us
  starting transfers between devices: 25.6 us -> 0 us
    dynamic_update_slice x64 -> x0, local copies, waits for them, and re-layouts: 309 us -> none  [run_scan(): unused, local = lax.scan(inner_step, start, inputs)]
    all_to_all x5 -> x0, waiting for transfers between devices: 257 us -> none  [the longest x1 96.3 us: body(): lax.all_to_all(pack_dealt(activated), 'fsdp', split_axis=0, concat_axis=0...]
    pallas_call x0 -> x4, Pallas kernels: none -> 175 us  [the longest x1 61.4 us: body(): pl.pallas_call(functools.partial(main_kernel, grid, block_rows), grid=(ti...]
    reduce_scatter x3 -> x0, waiting for transfers between devices: 173 us -> none  [the longest x1 103 us: body(): lax.psum_scatter(drive_grad, ('dp', 'fsdp'), scatter_dimension=0, tiled=T...]
    all_gather x2 -> x0, blocking collectives: 169 us -> none  [the longest x1 127 us: body(): lax.all_gather(drive_matrix, ('dp', 'fsdp'), axis=0, tiled=True)]
    dynamic_update_slice x48 -> x0, other arithmetic: 131 us -> none  [run_scan(): unused, local = lax.scan(inner_step, start, inputs)]
    dot_general x9 -> x0, matrix products: 106 us -> none  [the longest x3 30.3 us: contract_cols(): lax.dot_general(left, right, (((1,), (1,)), ((), ())), preferred_element_...]
    slice x123 -> x0, local copies, waits for them, and re-layouts: 99.6 us -> none  [the longest x120 91.3 us: run_scan(): prefix = lax.associative_scan(combine, totals, axis=0)]
  transfers between devices with their start and end apart: 9 -> 0, of which waited for: 5 -> 0; matrix products, arithmetic and copies ran while one was open for 7% -> 0% of each run, Pallas kernels for 0% -> 0%
where the time goes in v1:
time: 177 us
  Pallas kernels  175 us (99%)
    pallas_call x1, Pallas kernels, body(): pl.pallas_call(functools.partial(main_kernel, grid, block_rows), grid=(ti...  61.4 us
    pallas_call x1, Pallas kernels, body(): pl.pallas_call(functools.partial(last_kernel, grid, block_rows, orders),...  52.7 us
    pallas_call x1, Pallas kernels, body(): pl.pallas_call(functools.partial(front_kernel, grid, block_rows, counts),...  44.7 us
    pallas_call x1, Pallas kernels, body(): pl.pallas_call(functools.partial(tail_kernel, grid), grid=(tiles,), in_sp...  16.2 us

profile of v1, /device:TPU:0, one launch (start us, length us, event | category | flops | bytes accessed | tf_op | source)
XLA Modules:
  0.0 176.6 jit_solution(941475760159397964)
XLA Ops:
  0.7 0.8 fusion.1
  1.4 44.7 %front.1 = (bf16[4096,512]{1,0:T(8,128)(2,1)}, f32[4096,768]{1,0:T(8,128)}, f32[4096,128]{1,0:T(8,128)}, f32[128,768]{1,0:T(8,128)}, bf16[512,768]{1,0:T(8,128)(...) custom-call(bf16[4096,512]{1,0:T(8,128)(2,1)} %tokens.5, ...), custom_call_target="tpu_custom_call" | custom-call | tf_op jit(solution)/shard_map/front/pallas_call | solution.py:831
  46.1 61.4 %main.1 = (bf16[4096,512]{1,0:T(8,128)(2,1)}, bf16[4096,512]{1,0:T(8,128)(2,1)}, bf16[4096,768]{1,0:T(8,128)(2,1)}, f32[4096,768]{1,0:T(8,128)}, f32[512,1024]{1...) custom-call(bf16[4096,512]{1,0:T(8,128)(2,1)} %cotangent.3, ...), custom_call_target="tpu_custom_call" | custom-call | tf_op jit(solution)/shard_map/main/pallas_call | solution.py:864
  107.6 52.7 %last.1 = (bf16[4096,512]{1,0:T(8,128)(2,1)}, f32[16,768]{1,0:T(8,128)}, f32[24,512]{1,0:T(8,128)}, f32[16,1024]{1,0:T(8,128)}, f32[8,768]{1,0:T(8,128)}) custom-call(bf16[4096,512]{1,0:T(8,128)(2,1)} %get-tuple-element.39.dealt, bf16[4096,768]{1,0:T(8,128)(2,1)} %get-tuple-element.50.joined, f32[4096,768]{1,0:T(8,128)} %get-tuple-element.51.joined_grad, ...), custom_call_target="tpu_custom_call" | custom-call | tf_op jit(solution)/shard_map/last/pallas_call | solution.py:900
  160.2 16.2 %tail.1 = (f32[4096,512]{1,0:T(8,128)}, f32[4096,512]{1,0:T(8,128)}, f32[16]{0:T(128)}, f32[16]{0:T(128)}, f32[12]{0:T(128)}, /*index=5*/f32[12]{0:T(128)}, f32[...) custom-call(bf16[4096,512]{1,0:T(8,128)(2,1)} %tokens.5, ...), custom_call_target="tpu_custom_call" | custom-call | tf_op jit(solution)/shard_map/tail/pallas_call | solution.py:939
  (1 shorter events, 0.0 us)

commit v2 on v1

--- a/solution.py
+++ b/solution.py
@@ -3,6 +3,7 @@
 
 import jax
 import jax.numpy as jnp
+import numpy as np
 from jax import lax
 from jax.experimental import pallas as pl
 from jax.experimental.pallas import tpu as pltpu
@@ -37,17 +38,8 @@
     return jnp.broadcast_to(vector, (rows, vector.shape[1]))
 
 
-def erfc_abs(magnitude):
-    t = 1.0 / (1.0 + 0.5 * magnitude)
-    series = t * 0.17087277 - 0.82215223
-    for term in (1.48851587, -1.13520398, 0.27886807, -0.18628806, 0.09678418, 0.37409196, 1.00002368):
-        series = series * t + term
-    return t * jnp.exp(series * t - 1.26551223 - magnitude * magnitude)
-
-
 def gelu_parts(v):
-    complement = 0.5 * erfc_abs(jnp.abs(v) * 0.7071067811865476)
-    cdf = jnp.where(v < 0.0, complement, 1.0 - complement)
+    cdf = 0.5 + 0.5 * lax.erf(v * 0.7071067811865476)
     density = 0.3989422804014327 * jnp.exp(-0.5 * v * v)
     return v * cdf, cdf + v * density
 
@@ -69,43 +61,48 @@
 
 
 class Grid:
-    def __init__(self, sizes):
-        self.dp, members = sizes
-        self.bits = members.bit_length() - 1
-        self.shape = (self.dp,) + (2,) * self.bits
+    def __init__(self, dp, members):
+        self.dp, self.members = dp, members
+        self.shape = (dp, members // 2, 2)
+        self.slots = dp - 1 + members // 2 - 1 + 1
 
     def here(self):
         row, column = lax.axis_index("dp"), lax.axis_index("fsdp")
-        mine = [row] + [lax.rem(lax.div(column, 2**bit), 2) for bit in reversed(range(self.bits))]
-        return row, column, mine
+        return row, column, (row, lax.div(column, 2), lax.rem(column, 2))
+
+    def fan(self, dim):
+        return self.shape[dim] - 1
 
     def peers(self, dim):
         row, column, mine = self.here()
-        if dim == 0:
-            return [
-                (away - 1, {"dp": lax.rem(row + away, self.dp)}, lax.rem(row + away, self.dp))
-                for away in range(1, self.dp)
-            ]
-        step = 2 ** (self.bits - dim)
-        return [(0, {"fsdp": column + step * (1 - 2 * mine[dim])}, 1 - mine[dim])]
-
-    def orders(self, dims, last):
-        return [tuple(dims[i:] + dims[:i]) + last for i in range(len(dims))]
-
-
-def greet(grid):
+        found = []
+        for away in range(1, self.shape[dim]):
+            index = lax.rem(mine[dim] + away, self.shape[dim])
+            if dim == 0:
+                device = {"dp": index}
+            elif dim == 1:
+                device = {"fsdp": 2 * index + mine[2]}
+            else:
+                device = {"fsdp": 2 * mine[1] + index}
+            found.append((away - 1, device, index))
+        return found
+
+
+def announce(grid):
     barrier = pltpu.get_barrier_semaphore()
     row, column, _ = grid.here()
-    members = 2**grid.bits
     for away in range(1, grid.dp):
         pl.semaphore_signal(
             barrier, inc=1, device_id={"dp": lax.rem(row + away, grid.dp)}, device_id_type=MESH
         )
-    for away in range(1, members):
+    for away in range(1, grid.members):
         pl.semaphore_signal(
-            barrier, inc=1, device_id={"fsdp": lax.rem(column + away, members)}, device_id_type=MESH
+            barrier, inc=1, device_id={"fsdp": lax.rem(column + away, grid.members)}, device_id_type=MESH
         )
-    pl.semaphore_wait(barrier, grid.dp + members - 2)
+
+
+def meet(grid):
+    pl.semaphore_wait(pltpu.get_barrier_semaphore(), grid.dp + grid.members - 2)
 
 
 def remote(source, target, send, recv, device):
@@ -130,7 +127,7 @@
     plan = []
     for phase, dim in enumerate(order):
         done = order[:phase]
-        left = tuple(d for d in range(grid.bits + 1) if d not in done and d != dim)
+        left = tuple(d for d in range(len(grid.shape)) if d not in done and d != dim)
         plan.append((dim, done, left))
     return plan
 
@@ -198,34 +195,30 @@
 
 
 def front_kernel(
-    grid, block_rows, counts, tokens, gain_s, shift_s, through_s, bias_s, real_s, rotation_s, step_s, target_s,
+    grid, block_rows, counts, tile, tokens, gain_s, shift_s, through_s, bias_s, real_s, rotation_s, step_s, target_s,
     lengths_s, drive_s, readout_s, mixer_s, perm,
     dealt, driven, keep, carries, drive, drive_raw, readout_w, mixer_w, vectors, rates, place, own_place, broken,
-    xhat, table, drive_w, bits, pieces, dealt_ends, send, recv, local, push_send, push_recv,
+    rows_in, normed, xhat, table, drive_w, bits, pieces, dealt_ends, send, recv, local, push_send, push_recv,
 ):
     i = pl.program_id(0)
-    tiles = (pl.num_programs(0) - 1) // 2
+    tiles = pl.num_programs(0) - 2
     row, column, mine = grid.here()
-    members = 2**grid.bits
+    members = grid.members
     blocks = target_s.shape[0]
-    tile = tokens.shape[0]
     width = tokens.shape[1]
     both = drive.shape[1]
     states = both // 2
     span = SUB * block_rows
     chains = tile // span
     tile_blocks = tile // block_rows
-    axes = tuple(range(grid.bits + 1))
+    axes = tuple(range(len(grid.shape)))
     wholes = (table, drive_w, readout_w, mixer_w)
-    dims = list(range(grid.bits))
-    orders = grid.orders(dims, (grid.bits,))
-    orders = [orders[0], orders[0], orders[1 % len(orders)], orders[2 % len(orders)]]
-    slots = grid.dp - 1 + grid.bits
-    phases = grid.bits + 1
+    orders = ((0, 1, 2), (0, 1, 2), (1, 0, 2), (0, 1, 2))
+    phases = 3
 
     def phase_copies(k, phase):
         order = orders[k]
-        base = k * slots + sum(len(grid.peers(d)) for d in order[:phase])
+        base = k * grid.slots + sum(grid.fan(d) for d in order[:phase])
         return gather_phase(grid, wholes[k], axes, order[phase], order[:phase], send, recv, base)
 
     def advance(ks, phase):
@@ -252,28 +245,36 @@
             own[k : k + 1, : ref.shape[0]] = ref[...].astype(F32).reshape(1, ref.shape[0])
         sequences = lengths_s.shape[1]
         own[4:5, LANES // 2 : LANES // 2 + sequences] = lengths_s[...].astype(F32)
-        greet(grid)
+        announce(grid)
+        chunks = [
+            pltpu.make_async_copy(
+                tokens.at[pl.ds(j * tile, tile)], rows_in.at[pl.ds(j * tile, tile)], local.at[len(copies) + j]
+            )
+            for j in range(tiles)
+        ]
+        for copy in chunks:
+            copy.start()
         for copy in copies:
             copy.wait()
-        advance((0, 1, 2, 3), 0)
-
-    for phase in range(1, phases):
-        @pl.when(i == min(2 * phase, tiles))
-        def _():
-            advance((0, 1), phase)
-
-        @pl.when(i == min(4 * phase - 1, 2 * tiles - 2))
-        def _():
-            advance((2, 3), phase)
-
-    @pl.when(i < tiles)
-    def _():
-        moved, rstd = norm_stats(tokens[...].astype(F32))
-        xhat[pl.ds(pl.multiple_of(i * tile, tile), tile), :] = moved * rstd
-
-    @pl.when(i == tiles)
-    def _():
-        advance((0, 1), phases)
+        meet(grid)
+        advance((0, 1), 0)
+
+        def stats(j, _):
+            at = pl.ds(pl.multiple_of(j * tile, tile), tile)
+            moved, rstd = norm_stats(rows_in[at, :].astype(F32))
+            xhat[at, :] = moved * rstd
+            return 0
+
+        for copy in chunks[: tiles // 2]:
+            copy.wait()
+        lax.fori_loop(0, tiles // 2, stats, 0)
+        advance((0, 1), 1)
+        advance((2, 3), 0)
+        for copy in chunks[tiles // 2 :]:
+            copy.wait()
+        lax.fori_loop(tiles // 2, tiles, stats, 0)
+        advance((0,), 2)
+        advance((0,), 3)
         rows = table[...].reshape(-1, LANES)
         vectors[...] = jnp.zeros_like(vectors)
         for k, size in enumerate((width, width, width, 2 * width)):
@@ -287,10 +288,6 @@
             power *= 2
         for k, value in enumerate((factor_re, factor_im, flow_re, flow_im, real, rotation, step_log)):
             rates[k : k + 1, :] = value
-        drive_raw[...] = drive_w[...].reshape(width, both)
-        raw = drive_raw[...].astype(F32)
-        drive[:, :states] = (scale_re * raw[:, :states] - scale_im * raw[:, states:]).astype(BF16)
-        drive[:, states:] = (scale_re * raw[:, states:] + scale_im * raw[:, :states]).astype(BF16)
         group = table[row].reshape(members * SUB, LANES)
         for m in range(members):
             q = group[m * SUB + 7 : m * SUB + 8, :blocks]
@@ -321,31 +318,48 @@
             column_of = lengths[:, LANES // 2 + s : LANES // 2 + s + 1]
             start = start + jnp.broadcast_to(column_of, (members, LANES))
         bits[...] = marks
-
-    def pushes(j):
-        at = (column, pl.ds(pl.multiple_of(j * tile_blocks, tile_blocks), tile_blocks))
-        return push_to(at)
-
-    def push_to(at):
-        far = [
-            remote(
-                pieces.at[at], pieces.at[at], push_send.at[away // 2], push_recv.at[away // 2],
-                {"fsdp": lax.rem(column + away, members)},
-            )
-            for away in range(2, members, 2)
+        gain = vectors[0:1, :width]
+        shift_by = vectors[1:2, :width]
+
+        def settle(j, _):
+            at = pl.ds(pl.multiple_of(j * tile, tile), tile)
+            rounded = (xhat[at, :] * gain + shift_by).astype(BF16)
+            normed[at, :] = permute_tile(perm[...], rounded, span).astype(BF16)
+            return 0
+
+        lax.fori_loop(0, tiles // 2, settle, 0)
+        advance((1,), 2)
+        lax.fori_loop(tiles // 2, tiles, settle, 0)
+        advance((1,), 3)
+        drive_raw[...] = drive_w[...].reshape(width, both)
+        raw = drive_raw[...].astype(F32)
+        drive[:, :states] = (scale_re * raw[:, :states] - scale_im * raw[:, states:]).astype(BF16)
+        drive[:, states:] = (scale_re * raw[:, states:] + scale_im * raw[:, :states]).astype(BF16)
+
+    @pl.when(i == 1)
+    def _():
+        advance((2, 3), 1)
+
+    @pl.when(i == tiles // 2 + 1)
+    def _():
+        advance((2, 3), 2)
+
+    def push_far(at):
+        return [
+            remote(pieces.at[at], pieces.at[at], push_send.at[slot], push_recv.at[slot], device)
+            for slot, device, _ in grid.peers(1)
         ]
-        near = remote(pieces.at[at], pieces.at[at], push_send.at[0], push_recv.at[0], {"fsdp": sibling})
-        return far + [near]
-
-    sibling = column + 1 - 2 * mine[-1]
-
-    @pl.when((i >= tiles) & (i < 2 * tiles))
-    def _():
-        j = i - tiles
-        gain = vectors[0:1, :width]
-        shift = vectors[1:2, :width]
-        normed = xhat[pl.ds(pl.multiple_of(j * tile, tile), tile), :] * gain + shift
-        dealt[...] = permute_tile(perm[...], normed.astype(BF16), span).astype(BF16)
+
+    def push_near(at, slot):
+        device = grid.peers(2)[0][1]
+        return remote(pieces.at[at], pieces.at[at], push_send.at[slot], push_recv.at[slot], device)
+
+    far = grid.fan(1)
+
+    @pl.when((i >= 1) & (i <= tiles))
+    def _():
+        j = i - 1
+        dealt[...] = normed[pl.ds(pl.multiple_of(j * tile, tile), tile), :]
         driven[...] = dot(dealt[...], drive[...])
         rate_re = spread(rates[0:1, :], SUB)
         rate_im = spread(rates[1:2, :], SUB)
@@ -365,24 +379,19 @@
                 state[c] = (now_re, now_im)
         ends = jnp.concatenate([jnp.concatenate(state[c], axis=1) for c in range(chains)], axis=0)
         pieces[column, pl.ds(first, tile_blocks), :] = ends.astype(BF16)
-        for copy in pushes(j):
+        at = (column, pl.ds(first, tile_blocks))
+        for copy in push_far(at) + [push_near(at, far)]:
             copy.start()
 
-    @pl.when(i == 2 * tiles)
+    @pl.when(i == tiles + 1)
     def _():
         onward = []
-        for k, copy in enumerate(push_to((column,))[:-1]):
+        for k, copy in enumerate(push_far((column,))):
             copy.wait()
-            from_there = lax.rem(column + members - 2 * (k + 1), members)
-            slot = members // 2 + k
-            onward.append(
-                remote(
-                    pieces.at[from_there], pieces.at[from_there], push_send.at[slot], push_recv.at[slot],
-                    {"fsdp": sibling},
-                )
-            )
+            there = 2 * lax.rem(mine[1] + grid.shape[1] - 1 - k, grid.shape[1]) + mine[2]
+            onward.append(push_near((there,), far + 1 + k))
             onward[-1].start()
-        push_to((column,))[-1].wait()
+        push_near((column,), far).wait()
         for copy in onward:
             copy.wait()
         cross_blocks(
@@ -394,13 +403,13 @@
 def main_kernel(
     grid, block_rows, cotangent, dealt, driven, carry, keep, rates, readout, vectors, mixer, perm, back, place,
     own_place, broken,
-    gated_low, mixed_low, joined, joined_grad, weight_grad, bias_grad, through_grad, readout_grad, coming,
+    gated_low, mixed_low, joined, joined_grad, weight_grad, bias_grad, through_grad, readout_grad, mixed_sum, coming,
     pieces, dealt_heads, push_send, push_recv,
 ):
     i = pl.program_id(0)
     tiles = pl.num_programs(0) - 1
     _, column, _ = grid.here()
-    members = 2**grid.bits
+    members = grid.members
     span = SUB * block_rows
     tile, width = cotangent.shape
     states = rates.shape[1]
@@ -422,7 +431,8 @@
         bias_grad[...] = jnp.zeros_like(bias_grad)
         through_grad[...] = jnp.zeros_like(through_grad)
         readout_grad[...] = jnp.zeros_like(readout_grad)
-        greet(grid)
+        mixed_sum[...] = jnp.zeros_like(mixed_sum)
+        announce(grid)
 
     @pl.when(i < tiles)
     def _():
@@ -466,7 +476,9 @@
         feature_grad = contract_cols(hidden_low, mixer[...]).astype(BF16)
         mixed_grad = (permute_tile(perm[...], feature_grad, span) * slope).astype(BF16)
         mixed_low[...] = mixed_grad
-        through_grad[...] += jnp.sum(mixed_grad.astype(F32) * dealt_f32, axis=0, keepdims=True)
+        mixed_f32 = mixed_grad.astype(F32)
+        through_grad[...] += jnp.sum(mixed_f32 * dealt_f32, axis=0, keepdims=True)
+        mixed_sum[...] += jnp.sum(mixed_f32, axis=0, keepdims=True)
         readout_grad[...] += contract_rows(joined[...], mixed_grad)
         joined_grad[...] = contract_cols(mixed_grad, readout[...])
 
@@ -481,6 +493,11 @@
         heads = jnp.concatenate([jnp.concatenate(going[c], axis=1) for c in range(chains)], axis=0)
         at = (column, pl.ds(pl.multiple_of(i * tile_blocks, tile_blocks), tile_blocks))
         pieces[at + (slice(None),)] = heads.astype(BF16)
+
+        @pl.when(i == 0)
+        def _():
+            meet(grid)
+
         for copy in push_to(at):
             copy.start()
 
@@ -493,18 +510,35 @@
         )
 
 
+def split(values):
+    high = values.astype(BF16)
+    rest = values - high.astype(F32)
+    middle = rest.astype(BF16)
+    return high, middle, (rest - middle.astype(F32)).astype(BF16)
+
+
+def row_times(row, matrix):
+    wide = [jnp.broadcast_to(piece.astype(F32), (SUB, row.shape[1])).astype(BF16) for piece in split(row)]
+    return sum(contract_cols(piece, matrix) for piece in wide)[0:1]
+
+
+def row_sums(matrix):
+    ones = jnp.ones((SUB, matrix.shape[1]), BF16)
+    return sum(contract_cols(ones, piece) for piece in split(matrix))[0:1]
+
+
 def last_kernel(
     grid, block_rows, orders, dealt, joined, joined_grad, carry, coming, keep, mixed_low, tokens, rates, vectors, drive,
-    drive_raw, back, readout_grad, weight_grad, bias_grad, through_grad,
-    given_low, drive_sum, readout_sum, weight_sum, vector_sum,
-    driven_all, drive_grad, drive_parts, decay_cot, gain_grad, shift_grad, *rest,
+    drive_raw, back, readout_grad, weight_grad, bias_grad, through_grad, mixed_sum,
+    token_part, drive_sum, readout_sum, weight_sum, vector_sum,
+    driven_all, drive_grad, drive_parts, decay_cot, driven_sum, *rest,
 ):
     i = pl.program_id(0)
     tiles = (pl.num_programs(0) - 1) // 2
     row, column, mine = grid.here()
-    members = 2**grid.bits
-    core = grid.bits
-    phases = grid.bits + 1
+    members = grid.members
+    core = 2
+    phases = 3
     span = SUB * block_rows
     tile, width = tokens.shape
     both = joined.shape[1]
@@ -519,8 +553,7 @@
     landed = [[rest.pop(0) for _ in range(phases)] for _ in range(count)]
     vector_stage, across, along, send, recv, vector_send, vector_recv = rest
     plans = [reduce_plan(grid, order) for order in orders]
-    slots = grid.dp - 1 + grid.bits
-    every = tuple(range(grid.bits + 1))
+    every = (0, 1, 2)
     kept = every[:-1]
 
     def combos(left):
@@ -533,7 +566,7 @@
 
     def hops(k, phase):
         dim = plans[k][phase][0]
-        base = k * slots + sum(len(grid.peers(d)) for d in orders[k][:phase])
+        base = k * grid.slots + sum(grid.fan(d) for d in orders[k][:phase])
         return [
             (
                 remote(
@@ -578,24 +611,55 @@
             if phase < phases:
                 begin(k, phase)
             else:
-                outs[k][...] = accs[k][tuple(mine[:-1])]
+                outs[k][...] = accs[k][mine[:-1]]
 
     rate_re = spread(rates[0:1, :], SUB)
     rate_im = spread(rates[1:2, :], SUB)
 
+    def vector_across():
+        return [
+            remote(
+                vector_stage, across.at[away - 1], vector_send.at[away - 1], vector_recv.at[away - 1],
+                {"fsdp": lax.rem(column + away, members)},
+            )
+            for away in range(1, members)
+        ]
+
+    def vector_along():
+        return [
+            remote(
+                vector_sum, along.at[slot], vector_send.at[members - 1 + slot], vector_recv.at[members - 1 + slot], device
+            )
+            for slot, device, _ in grid.peers(0)
+        ]
+
     @pl.when(i == 0)
     def _():
         drive_grad[...] = jnp.zeros_like(drive_grad)
         decay_cot[...] = jnp.zeros_like(decay_cot)
-        gain_grad[...] = jnp.zeros_like(gain_grad)
-        shift_grad[...] = jnp.zeros_like(shift_grad)
-        greet(grid)
+        driven_sum[...] = jnp.zeros_like(driven_sum)
+        announce(grid)
+
+    @pl.when(i == 1)
+    def _():
+        meet(grid)
         advance((0, 1), 0)
 
-    for phase in range(1, phases + 1):
-        @pl.when(i == min(2 * phase, 2 * tiles - 1))
-        def _():
-            advance((0, 1), phase)
+    @pl.when(i == 3)
+    def _():
+        advance((0, 1), 1)
+
+    @pl.when(i == tiles - 1)
+    def _():
+        advance((0,), 2)
+
+    @pl.when(i == tiles + 2)
+    def _():
+        advance((1,), 2)
+
+    @pl.when(i == 2 * tiles - 1)
+    def _():
+        advance((0, 1), 3)
 
     @pl.when(i < tiles)
     def _():
@@ -605,6 +669,7 @@
             for c in range(chains)
         ]
         total = [(jnp.zeros((SUB, states), F32), jnp.zeros((SUB, states), F32)) for _ in range(chains)]
+        sums = list(total)
         for t in reversed(range(0, block_rows, 2)):
             for c in range(chains):
                 pair = c * span + t * SUB
@@ -623,6 +688,7 @@
                     re = joined_grad[where : where + SUB, :states] + going[c][0]
                     im = going[c][1] - joined_grad[where : where + SUB, states:]
                     held[step] = (re, im)
+                    sums[c] = (sums[c][0] + re, sums[c][1] + im)
                     on_re = mask * (rate_re * re + rate_im * im)
                     on_im = mask * (rate_re * im - rate_im * re)
                     going[c] = (on_re, on_im)
@@ -638,6 +704,7 @@
                 ).astype(BF16)
         for c in range(chains):
             decay_cot[...] += jnp.concatenate(total[c], axis=1)
+            driven_sum[...] += jnp.concatenate(sums[c], axis=1)
         drive_grad[...] += contract_rows(dealt[...], driven_low[...])
 
     @pl.when(i == tiles)
@@ -646,31 +713,16 @@
         for s, place in enumerate(itertools.product(*[range(size) for size in grid.shape])):
             drive_parts[place] = drive_grad[s * shard : (s + 1) * shard, :]
         advance((2,), 0)
-
-    for phase in range(1, phases):
-        @pl.when(i == min(tiles + 2 * phase, 2 * tiles))
-        def _():
-            advance((2,), phase)
-
-    @pl.when((i >= tiles) & (i < 2 * tiles))
-    def _():
-        j = i - tiles
-        driven_low = driven_all[pl.ds(pl.multiple_of(j * tile, tile), tile), :]
-        normed_grad = vectors[2:3, :width] * mixed_low[...].astype(F32) + contract_cols(driven_low, drive[...])
-        given = permute_tile(back[...], normed_grad.astype(BF16), span)
-        given_low[...] = given.astype(BF16)
-        moved, rstd = norm_stats(tokens[...].astype(F32))
-        gain_grad[...] += jnp.sum(given * (moved * rstd), axis=0, keepdims=True)
-        shift_grad[...] += jnp.sum(given, axis=0, keepdims=True)
-
-    @pl.when(i == 2 * tiles)
-    def _():
         cot = jnp.sum(decay_cot[...], axis=0, keepdims=True)
         factor_re, factor_im = rates[0:1, :], rates[1:2, :]
         size = factor_re * factor_re + factor_im * factor_im
         vector_stage[...] = jnp.zeros_like(vector_stage)
-        vector_stage[0:1, :width] = gain_grad[...]
-        vector_stage[1:2, :width] = shift_grad[...]
+        through = vectors[2:3, :width]
+        summed = jnp.sum(driven_sum[...], axis=0, keepdims=True)
+        shift_sum = through * mixed_sum[...] + row_times(summed, drive[...])
+        crossed = row_sums(drive[...].astype(F32) * drive_grad[...]) + through * through_grad[...]
+        vector_stage[0:1, :width] = (crossed - vectors[1:2, :width] * shift_sum) / vectors[0:1, :width]
+        vector_stage[1:2, :width] = shift_sum
         vector_stage[2:3, :width] = through_grad[...]
         vector_stage[3:4, :] = bias_grad[:, :both]
         vector_stage[4:5, : 2 * width - both] = bias_grad[:, both:]
@@ -681,61 +733,68 @@
         vector_stage[6:7, :states] = jnp.sum(d_re * b_re + d_im * b_im, axis=0, keepdims=True)
         vector_stage[6:7, states:] = jnp.sum(d_im * b_re - d_re * b_im, axis=0, keepdims=True)
 
-        copies = [
-            remote(
-                vector_stage, across.at[away - 1], vector_send.at[away - 1], vector_recv.at[away - 1],
-                {"fsdp": lax.rem(column + away, members)},
-            )
-            for away in range(1, members)
-        ]
-        for copy in copies:
+        for copy in vector_across():
             copy.start()
-        for copy in copies:
+
+    @pl.when(i == tiles + 1)
+    def _():
+        advance((2,), 1)
+
+    @pl.when(i == tiles + 3)
+    def _():
+        for copy in vector_across():
             copy.wait()
         total = vector_stage[...]
         for k in range(members - 1):
             total = total + across[k]
         vector_sum[...] = total
-        copies = [
-            remote(
-                vector_sum, along.at[away - 1], vector_send.at[members - 2 + away], vector_recv.at[members - 2 + away],
-                {"dp": lax.rem(row + away, grid.dp)},
-            )
-            for away in range(1, grid.dp)
-        ]
-        for copy in copies:
+        for copy in vector_along():
             copy.start()
-        advance((2,), phases)
-        for copy in copies:
+
+    @pl.when(i == tiles + 5)
+    def _():
+        advance((2,), 2)
+
+    @pl.when(i == 2 * tiles)
+    def _():
+        for copy in vector_along():
             copy.wait()
         total = vector_sum[...]
         for k in range(grid.dp - 1):
             total = total + along[k]
         vector_sum[...] = total
+        advance((2,), 3)
+
+    @pl.when((i >= tiles) & (i < 2 * tiles))
+    def _():
+        j = i - tiles
+        driven_low = driven_all[pl.ds(pl.multiple_of(j * tile, tile), tile), :]
+        normed_grad = vectors[2:3, :width] * mixed_low[...].astype(F32) + contract_cols(driven_low, drive[...])
+        given = permute_tile(back[...], normed_grad.astype(BF16), span)
+        moved, rstd = norm_stats(tokens[...].astype(F32))
+        xhat = moved * rstd
+        scaled = given * vectors[0:1, :width]
+        inner = jnp.mean(scaled * xhat, axis=-1, keepdims=True)
+        token_part[...] = (
+            rstd * (scaled - jnp.mean(scaled, axis=-1, keepdims=True) - xhat * inner)
+        ).astype(BF16)
 
 
 def tail_kernel(
-    grid, tokens, cotangent, given_low, gated_low, vectors, rates, drive_sum, readout_sum, weight_sum, vector_sum,
+    grid, tokens, cotangent, token_part, gated_low, rates, drive_sum, readout_sum, weight_sum, vector_sum,
     out, token_grad, gain_grad, shift_grad, real_grad, rotation_grad, timestep_grad, drive_grad, readout_grad,
     through_grad, weight_grad, bias_grad,
 ):
     width = tokens.shape[1]
     both = vector_sum.shape[1]
     states = both // 2
-    rows = tokens[...].astype(F32)
-    out[...] = rows + gated_low[...].astype(F32)
-    moved, rstd = norm_stats(rows)
-    xhat = moved * rstd
-    scaled = given_low[...].astype(F32) * vectors[0:1, :width]
-    inner = jnp.mean(scaled * xhat, axis=-1, keepdims=True)
-    token_grad[...] = cotangent[...].astype(F32) + rstd * (
-        scaled - jnp.mean(scaled, axis=-1, keepdims=True) - xhat * inner
-    )
+    out[...] = tokens[...].astype(F32) + gated_low[...].astype(F32)
+    token_grad[...] = cotangent[...].astype(F32) + token_part[...].astype(F32)
 
     @pl.when(pl.program_id(0) == 0)
     def _():
         row, column, _ = grid.here()
-        me = row * 2**grid.bits + column
+        me = row * grid.members + column
         real, rotation, step_log = [rates[k : k + 1, :] for k in (4, 5, 6)]
         timestep, factor_re, factor_im, modulus, scale_re, scale_im = rates_of(real, rotation, step_log)
         d_re, d_im = drive_sum[:, :states], drive_sum[:, states:]
@@ -794,7 +853,7 @@
     log_timestep, drive_matrix, readout_matrix, feedthrough, mixer_weight, mixer_bias,
 ):
     members = lax.axis_size("fsdp")
-    grid = Grid((lax.axis_size("dp"), members))
+    grid = Grid(lax.axis_size("dp"), members)
     blocks = block_target.shape[0]
     rows, width = tokens.shape
     both = drive_matrix.shape[1]
@@ -810,10 +869,10 @@
     anywhere = pl.BlockSpec(memory_space=pl.ANY)
     regular = pltpu.SemaphoreType.DMA
 
-    order = jnp.arange(span, dtype=jnp.int32)
+    order = np.arange(span)
     source = (order % SUB) * block_rows + order // SUB
-    perm = (source[:, None] == order[None]).astype(BF16)
-    back = (order[:, None] == source[None]).astype(BF16)
+    perm = jnp.asarray(source[:, None] == order[None], BF16)
+    back = jnp.asarray(order[:, None] == source[None], BF16)
 
     def early(rows_of, columns):
         return pl.BlockSpec((rows_of, columns), lambda i: (jnp.minimum(i, tiles - 1), 0))
@@ -827,15 +886,20 @@
     small = (norm_gain, norm_shift, feedthrough, mixer_bias, decay_real, decay_rotation, log_timestep, block_target)
     counts = tuple(v.shape[0] for v in small)
     shards = (drive_matrix, readout_matrix, mixer_weight)
-    slots = grid.dp - 1 + grid.bits
+    slots = grid.slots
+
+    def shifted(rows_of, columns):
+        return pl.BlockSpec((rows_of, columns), lambda i: (jnp.clip(i - 1, 0, tiles - 1), 0))
+
     dealt, driven, keep, carry, drive, drive_raw, readout, mixer, vectors, rates, place, own_place, broken = pl.pallas_call(
-        functools.partial(front_kernel, grid, block_rows, counts),
-        grid=(2 * tiles + 1,),
-        in_specs=[early(tile, width)]
+        functools.partial(front_kernel, grid, block_rows, counts, tile),
+        grid=(tiles + 2,),
+        in_specs=[anywhere]
         + [flat(size) for size in counts]
         + [whole((1, sequences)), anywhere, anywhere, anywhere, whole((span, span))],
         out_specs=[
-            late(tile, width), late(tile, both), late(tile, LANES), total_of((blocks, both)), total_of((width, both)),
+            shifted(tile, width), shifted(tile, both), shifted(tile, LANES), total_of((blocks, both)),
+            total_of((width, both)),
             total_of((width, both)), anywhere, anywhere, total_of((SUB, 2 * width)), total_of((SUB, states)),
             total_of((1, total)), total_of((blocks, LANES)), total_of((sequences, members, LANES)),
         ],
@@ -847,13 +911,16 @@
             shape((blocks, LANES), F32), shape((sequences, members, LANES), jnp.int32),
         ],
         scratch_shapes=[
+            pltpu.VMEM((rows, width), BF16),
+            pltpu.VMEM((rows, width), BF16),
             pltpu.VMEM((rows, width), F32),
             pltpu.VMEM(grid.shape + (SUB, LANES), F32),
             pltpu.VMEM(grid.shape + drive_matrix.shape, BF16),
             pltpu.VMEM((blocks, LANES), jnp.int32),
             pltpu.VMEM((members, blocks, both), BF16),
             pltpu.VMEM((total, both), F32),
-            regular((4 * slots,)), regular((4 * slots,)), regular((len(shards),)), regular((members,)), regular((members,)),
+            regular((4 * slots,)), regular((4 * slots,)), regular((len(shards) + tiles,)), regular((members,)),
+            regular((members,)),
         ],
         compiler_params=params(0),
         name="front",
@@ -861,7 +928,7 @@
     readout = readout.reshape(both, width)
     mixer = mixer.reshape(width, 2 * width)
 
-    gated_low, mixed_low, joined, joined_grad, weight_grad, bias_grad, through_grad, readout_grad, coming = pl.pallas_call(
+    gated_low, mixed_low, joined, joined_grad, weight_grad, bias_grad, through_grad, readout_grad, mixed_sum, coming = pl.pallas_call(
         functools.partial(main_kernel, grid, block_rows),
         grid=(tiles + 1,),
         in_specs=[
@@ -873,12 +940,12 @@
         out_specs=[
             early(tile, width), early(tile, width), early(tile, both), early(tile, both),
             total_of((width, 2 * width)), total_of((1, 2 * width)), total_of((1, width)), total_of((both, width)),
-            total_of((blocks, both)),
+            total_of((1, width)), total_of((blocks, both)),
         ],
         out_shape=[
             shape((rows, width), BF16), shape((rows, width), BF16), shape((rows, both), BF16),
             shape((rows, both), F32), shape((width, 2 * width), F32), shape((1, 2 * width), F32),
-            shape((1, width), F32), shape((both, width), F32), shape((blocks, both), F32),
+            shape((1, width), F32), shape((both, width), F32), shape((1, width), F32), shape((blocks, both), F32),
         ],
         scratch_shapes=[
             pltpu.VMEM((members, blocks, both), BF16), pltpu.VMEM((total, both), F32), regular((members - 1,)),
@@ -888,23 +955,20 @@
         name="main",
     )(cotangent, dealt, driven, carry, keep, rates, readout, vectors, mixer, perm, back, place, own_place, broken)
 
-    dims = list(range(grid.bits))
-    turns = grid.orders(dims, ())
-    orders = [(grid.bits,) + turns[k % len(turns)] for k in range(3)]
+    orders = ((2, 0, 1), (2, 1, 0), (2, 1, 0))
     weights = (readout_matrix, mixer_weight, drive_matrix)
     buffers = []
     for turn, weight in zip(orders, weights):
         for dim, _, left in reduce_plan(grid, turn):
-            fan = grid.dp - 1 if dim == 0 else 1
-            buffers.append(pltpu.VMEM((fan,) + tuple(grid.shape[d] for d in left) + weight.shape, BF16))
-    given_low, drive_sum, readout_sum, weight_sum, vector_sum = pl.pallas_call(
+            buffers.append(pltpu.VMEM((grid.fan(dim),) + tuple(grid.shape[d] for d in left) + weight.shape, BF16))
+    token_part, drive_sum, readout_sum, weight_sum, vector_sum = pl.pallas_call(
         functools.partial(last_kernel, grid, block_rows, orders),
         grid=(2 * tiles + 1,),
         in_specs=[
             early(tile, width), early(tile, both), early(tile, both), early(tile_blocks, both), early(tile_blocks, both),
             early(tile, LANES), late(tile, width), late(tile, width), whole((SUB, states)), whole((SUB, 2 * width)),
             whole((width, both)), whole((width, both)), whole((span, span)), whole(grid.shape + readout_matrix.shape),
-            whole(grid.shape + mixer_weight.shape), whole((1, 2 * width)), whole((1, width)),
+            whole(grid.shape + mixer_weight.shape), whole((1, 2 * width)), whole((1, width)), whole((1, width)),
         ],
         out_specs=[
             late(tile, width), total_of(drive_matrix.shape), total_of(readout_matrix.shape),
@@ -917,7 +981,7 @@
         scratch_shapes=[
             pltpu.VMEM((rows, both), BF16), pltpu.VMEM((width, both), F32),
             pltpu.VMEM(grid.shape + drive_matrix.shape, F32), pltpu.VMEM((SUB, both), F32),
-            pltpu.VMEM((1, width), F32), pltpu.VMEM((1, width), F32),
+            pltpu.VMEM((SUB, both), F32),
         ]
         + [pltpu.VMEM(grid.shape[:-1] + weight.shape, F32) for weight in weights]
         + buffers
@@ -932,19 +996,20 @@
     )(
         dealt, joined, joined_grad, carry, coming, keep, mixed_low, tokens, rates, vectors, drive, drive_raw, back,
         readout_grad.reshape(grid.shape + readout_matrix.shape), weight_grad.reshape(grid.shape + mixer_weight.shape),
-        bias_grad, through_grad,
+        bias_grad, through_grad, mixed_sum,
     )
 
     vector_sizes = [v.shape[0] for v in (norm_gain, norm_shift, decay_real, decay_rotation, log_timestep)]
+    slab = 2 * tile
     outs = pl.pallas_call(
         functools.partial(tail_kernel, grid),
-        grid=(tiles,),
-        in_specs=[tiled(tile, width)] * 4
+        grid=(rows // slab,),
+        in_specs=[tiled(slab, width)] * 4
         + [
-            whole((SUB, 2 * width)), whole((SUB, states)), whole(drive_matrix.shape), whole(readout_matrix.shape),
+            whole((SUB, states)), whole(drive_matrix.shape), whole(readout_matrix.shape),
             whole(mixer_weight.shape), whole((SUB, both)),
         ],
-        out_specs=[tiled(tile, width)] * 2
+        out_specs=[tiled(slab, width)] * 2
         + [flat(size) for size in vector_sizes]
         + [
             total_of(drive_matrix.shape), total_of(readout_matrix.shape), flat(feedthrough.shape[0]),
@@ -958,7 +1023,7 @@
         ],
         compiler_params=params(),
         name="tail",
-    )(tokens, cotangent, given_low, gated_low, vectors, rates, drive_sum, readout_sum, weight_sum, vector_sum)
+    )(tokens, cotangent, token_part, gated_low, rates, drive_sum, readout_sum, weight_sum, vector_sum)
     return tuple(outs)
 
 

time: 177 us -> 148 us (0.84)
  Pallas kernels: 175 us -> 147 us
    pallas_call x1, Pallas kernels: 52.7 us -> 38.6 us  [body(): pl.pallas_call(functools.partial(last_kernel, grid, block_rows, orders),...]
    pallas_call x1, Pallas kernels: 61.4 us -> 51 us  [body(): pl.pallas_call(functools.partial(main_kernel, grid, block_rows), grid=(ti...]
    pallas_call x2, Pallas kernels: 60.9 us -> 57.4 us  [the longest x1 45.4 us: body(): pl.pallas_call(functools.partial(front_kernel, grid, block_rows, counts,...]
where the time goes in v2:
time: 148 us
  Pallas kernels  147 us (99%)
    pallas_call x1, Pallas kernels, body(): pl.pallas_call(functools.partial(main_kernel, grid, block_rows), grid=(ti...  51 us
    pallas_call x1, Pallas kernels, body(): pl.pallas_call(functools.partial(front_kernel, grid, block_rows, counts,...  45.4 us
    pallas_call x1, Pallas kernels, body(): pl.pallas_call(functools.partial(last_kernel, grid, block_rows, orders),...  38.6 us
    pallas_call x1, Pallas kernels, body(): pl.pallas_call(functools.partial(tail_kernel, grid), grid=(rows // slab,)...  12 us

profile of v2, /device:TPU:0, one launch (start us, length us, event | category | flops | bytes accessed | tf_op | source)
XLA Modules:
  0.0 147.8 jit_solution(15509725020209189409)
XLA Ops:
  0.6 45.4 %front.1 = (bf16[4096,512]{1,0:T(8,128)(2,1)}, f32[4096,768]{1,0:T(8,128)}, f32[4096,128]{1,0:T(8,128)}, f32[128,768]{1,0:T(8,128)}, bf16[512,768]{1,0:T(8,128)(...) custom-call(bf16[4096,512]{1,0:T(8,128)(2,1)} %tokens.5, ...), custom_call_target="tpu_custom_call" | custom-call | tf_op jit(solution)/shard_map/front/pallas_call | solution.py:894
  46.0 51.0 %main.1 = (bf16[4096,512]{1,0:T(8,128)(2,1)}, bf16[4096,512]{1,0:T(8,128)(2,1)}, bf16[4096,768]{1,0:T(8,128)(2,1)}, f32[4096,768]{1,0:T(8,128)}, f32[512,1024]{1...) custom-call(bf16[4096,512]{1,0:T(8,128)(2,1)} %cotangent.3, ...), custom_call_target="tpu_custom_call" | custom-call | tf_op jit(solution)/shard_map/main/pallas_call | solution.py:931
  97.1 38.6 %last.1 = (bf16[4096,512]{1,0:T(8,128)(2,1)}, f32[16,768]{1,0:T(8,128)}, f32[24,512]{1,0:T(8,128)}, f32[16,1024]{1,0:T(8,128)}, f32[8,768]{1,0:T(8,128)}) custom-call(bf16[4096,512]{1,0:T(8,128)(2,1)} %get-tuple-element.40.dealt, bf16[4096,768]{1,0:T(8,128)(2,1)} %get-tuple-element.51.joined, f32[4096,768]{1,0:T(8,128)} %get-tuple-element.52.joined_grad, ...), custom_call_target="tpu_custom_call" | custom-call | tf_op jit(solution)/shard_map/last/pallas_call | solution.py:964
  135.6 12.0 %tail.1 = (f32[4096,512]{1,0:T(8,128)}, f32[4096,512]{1,0:T(8,128)}, f32[16]{0:T(128)}, f32[16]{0:T(128)}, f32[12]{0:T(128)}, /*index=5*/f32[12]{0:T(128)}, f32[...) custom-call(bf16[4096,512]{1,0:T(8,128)(2,1)} %tokens.5, ...), custom_call_target="tpu_custom_call" | custom-call | tf_op jit(solution)/shard_map/tail/pallas_call | solution.py:1004

commit v3 on v2

--- a/solution.py
+++ b/solution.py
@@ -15,7 +15,7 @@
 BF16 = jnp.bfloat16
 LANES = 128
 SUB = 8
-VMEM_LIMIT = 60 * 1024 * 1024
+VMEM_LIMIT = 63 * 1024 * 1024
 
 
 def dot(left, right):
@@ -88,21 +88,25 @@
         return found
 
 
-def announce(grid):
+def others(grid, everyone):
+    row, column, _ = grid.here()
+    found = []
+    for down in range(grid.dp):
+        for away in range(grid.members):
+            if (down or away) and (everyone or not (down and away)):
+                found.append({"dp": lax.rem(row + down, grid.dp), "fsdp": lax.rem(column + away, grid.members)})
+    return found
+
+
+def announce(grid, everyone=False):
     barrier = pltpu.get_barrier_semaphore()
-    row, column, _ = grid.here()
-    for away in range(1, grid.dp):
-        pl.semaphore_signal(
-            barrier, inc=1, device_id={"dp": lax.rem(row + away, grid.dp)}, device_id_type=MESH
-        )
-    for away in range(1, grid.members):
-        pl.semaphore_signal(
-            barrier, inc=1, device_id={"fsdp": lax.rem(column + away, grid.members)}, device_id_type=MESH
-        )
-
-
-def meet(grid):
-    pl.semaphore_wait(pltpu.get_barrier_semaphore(), grid.dp + grid.members - 2)
+    for device in others(grid, everyone):
+        pl.semaphore_signal(barrier, inc=1, device_id=device, device_id_type=MESH)
+
+
+def meet(grid, everyone=False):
+    count = grid.dp * grid.members - 1 if everyone else grid.dp + grid.members - 2
+    pl.semaphore_wait(pltpu.get_barrier_semaphore(), count)
 
 
 def remote(source, target, send, recv, device):
@@ -111,9 +115,11 @@
     )
 
 
-def gather_phase(grid, ref, axes, dim, done, send, recv, base):
+def gather_phase(grid, ref, cut, axes, dim, done, send, recv, base):
     _, _, mine = grid.here()
     at = tuple(slice(None) if d in done else mine[d] for d in axes)
+    if cut is not None:
+        at = at + (slice(None), cut)
     return [
         pltpu.make_async_remote_copy(
             src_ref=ref.at[at], dst_ref=ref.at[at], send_sem=send.at[base + slot], recv_sem=recv.at[base + slot],
@@ -158,13 +164,22 @@
     return timestep, factor_re, factor_im, modulus, scale_re, scale_im
 
 
-def cross_blocks(members, reverse, pieces, place, own_place, broken, flow_re, flow_im, dealt, carries):
+def cross_blocks(members, reverse, arrive, pieces, place, own_place, broken, flow_re, flow_im, chosen, dealt, carries):
     states = flow_re.shape[1]
     total = place.shape[1]
     steps = total // members
-    rows = lax.broadcasted_iota(jnp.int32, (total, total), 0).astype(F32)
-    chosen = jnp.where(rows == place[...], 1.0, 0.0).astype(BF16)
-    dealt[...] = dot(chosen, pieces[...].reshape(total, 2 * states))
+    chunk = chosen.shape[0]
+
+    def choose(at):
+        rows = lax.broadcasted_iota(jnp.int32, (chunk, total), 0).astype(F32) + float(at)
+        return jnp.where(rows == place[...], 1.0, 0.0).astype(BF16)
+
+    chosen[...] = choose(0)
+    arrive()
+    for at in range(0, total, chunk):
+        if at:
+            chosen[...] = choose(at)
+        dealt[at : at + chunk, :] = dot(chosen[...], pieces[...].reshape(total, 2 * states))
     rate_re = spread(flow_re, members)
     rate_im = spread(-flow_im if reverse else flow_im, members)
     marks = [broken[s] for s in range(broken.shape[0])]
@@ -187,18 +202,24 @@
     zero = jnp.zeros((members, states), F32)
     lax.fori_loop(0, steps, step, (zero, zero), unroll=4)
     own = own_place.shape[0]
-    columns = lax.broadcasted_iota(jnp.int32, (own, total), 1).astype(F32)
-    taken = jnp.where(columns == lanes_to(own_place[...], total), 1.0, 0.0).astype(BF16)
-    high = dealt[...].astype(BF16)
-    low = (dealt[...] - high.astype(F32)).astype(BF16)
-    carries[...] = dot(taken, high) + dot(taken, low)
+    step_rows = min(total, 1024)
+    found = jnp.zeros((own, 2 * states), F32)
+    for at in range(0, total, step_rows):
+        columns = lax.broadcasted_iota(jnp.int32, (own, step_rows), 1).astype(F32) + float(at)
+        taken = jnp.where(columns == lanes_to(own_place[...], step_rows), 1.0, 0.0).astype(BF16)
+        entering = dealt[at : at + step_rows, :]
+        high = entering.astype(BF16)
+        low = (entering - high.astype(F32)).astype(BF16)
+        found = found + (dot(taken, high) + dot(taken, low))
+    carries[...] = found
 
 
 def front_kernel(
-    grid, block_rows, counts, tile, tokens, gain_s, shift_s, through_s, bias_s, real_s, rotation_s, step_s, target_s,
+    grid, block_rows, counts, tile, tokens, cotangent, gain_s, shift_s, through_s, bias_s, real_s, rotation_s, step_s, target_s,
     lengths_s, drive_s, readout_s, mixer_s, perm,
-    dealt, driven, keep, carries, drive, drive_raw, readout_w, mixer_w, vectors, rates, place, own_place, broken,
-    rows_in, normed, xhat, table, drive_w, bits, pieces, dealt_ends, send, recv, local, push_send, push_recv,
+    dealt, rows_p, cot_p, driven, keep, carries, drive, drive_raw, readout_w, mixer_w, vectors, rates, place, own_place, broken,
+    rows_in, normed, xhat, table, drive_w, bits, pieces, chosen, dealt_ends, send, recv, local, push_send, push_recv,
+    table_send, table_recv,
 ):
     i = pl.program_id(0)
     tiles = pl.num_programs(0) - 2
@@ -212,14 +233,22 @@
     chains = tile // span
     tile_blocks = tile // block_rows
     axes = tuple(range(len(grid.shape)))
-    wholes = (table, drive_w, readout_w, mixer_w)
-    orders = ((0, 1, 2), (0, 1, 2), (1, 0, 2), (0, 1, 2))
+    half = mixer_w.shape[-1] // 2
+    wholes = (drive_w, readout_w, mixer_w, mixer_w)
+    cuts = (None, None, pl.ds(0, half), pl.ds(half, half))
+    orders = ((0, 1, 2), (1, 0, 2), (1, 0, 2), (0, 1, 2))
     phases = 3
 
     def phase_copies(k, phase):
         order = orders[k]
         base = k * grid.slots + sum(grid.fan(d) for d in order[:phase])
-        return gather_phase(grid, wholes[k], axes, order[phase], order[:phase], send, recv, base)
+        return gather_phase(grid, wholes[k], cuts[k], axes, order[phase], order[:phase], send, recv, base)
+
+    def table_copies():
+        return [
+            remote(table.at[mine], table.at[mine], table_send.at[k], table_recv.at[k], device)
+            for k, device in enumerate(others(grid, True))
+        ]
 
     def advance(ks, phase):
         for k in ks:
@@ -234,7 +263,7 @@
     def _():
         copies = [
             pltpu.make_async_copy(shard, ref.at[tuple(mine)], local.at[k])
-            for k, (shard, ref) in enumerate(zip((drive_s, readout_s, mixer_s), wholes[1:]))
+            for k, (shard, ref) in enumerate(zip((drive_s, readout_s, mixer_s), wholes))
         ]
         for copy in copies:
             copy.start()
@@ -245,7 +274,7 @@
             own[k : k + 1, : ref.shape[0]] = ref[...].astype(F32).reshape(1, ref.shape[0])
         sequences = lengths_s.shape[1]
         own[4:5, LANES // 2 : LANES // 2 + sequences] = lengths_s[...].astype(F32)
-        announce(grid)
+        announce(grid, True)
         chunks = [
             pltpu.make_async_copy(
                 tokens.at[pl.ds(j * tile, tile)], rows_in.at[pl.ds(j * tile, tile)], local.at[len(copies) + j]
@@ -256,25 +285,31 @@
             copy.start()
         for copy in copies:
             copy.wait()
-        meet(grid)
-        advance((0, 1), 0)
+        meet(grid, True)
+        advance((0,), 0)
+        for copy in table_copies():
+            copy.start()
+        advance((1, 2), 0)
 
         def stats(j, _):
             at = pl.ds(pl.multiple_of(j * tile, tile), tile)
-            moved, rstd = norm_stats(rows_in[at, :].astype(F32))
+            turned = permute_tile(perm[...], rows_in[at, :], span)
+            rows_in[at, :] = turned.astype(BF16)
+            moved, rstd = norm_stats(turned)
             xhat[at, :] = moved * rstd
             return 0
 
         for copy in chunks[: tiles // 2]:
             copy.wait()
         lax.fori_loop(0, tiles // 2, stats, 0)
-        advance((0, 1), 1)
-        advance((2, 3), 0)
+        advance((0,), 1)
+        advance((3,), 0)
+        advance((1, 2), 1)
         for copy in chunks[tiles // 2 :]:
             copy.wait()
         lax.fori_loop(tiles // 2, tiles, stats, 0)
-        advance((0,), 2)
-        advance((0,), 3)
+        for copy in table_copies():
+            copy.wait()
         rows = table[...].reshape(-1, LANES)
         vectors[...] = jnp.zeros_like(vectors)
         for k, size in enumerate((width, width, width, 2 * width)):
@@ -323,26 +358,17 @@
 
         def settle(j, _):
             at = pl.ds(pl.multiple_of(j * tile, tile), tile)
-            rounded = (xhat[at, :] * gain + shift_by).astype(BF16)
-            normed[at, :] = permute_tile(perm[...], rounded, span).astype(BF16)
+            normed[at, :] = (xhat[at, :] * gain + shift_by).astype(BF16)
             return 0
 
-        lax.fori_loop(0, tiles // 2, settle, 0)
-        advance((1,), 2)
-        lax.fori_loop(tiles // 2, tiles, settle, 0)
-        advance((1,), 3)
+        advance((0,), 2)
+        lax.fori_loop(0, tiles, settle, 0)
+        advance((0,), 3)
+        advance((3,), 1)
         drive_raw[...] = drive_w[...].reshape(width, both)
         raw = drive_raw[...].astype(F32)
         drive[:, :states] = (scale_re * raw[:, :states] - scale_im * raw[:, states:]).astype(BF16)
         drive[:, states:] = (scale_re * raw[:, states:] + scale_im * raw[:, :states]).astype(BF16)
-
-    @pl.when(i == 1)
-    def _():
-        advance((2, 3), 1)
-
-    @pl.when(i == tiles // 2 + 1)
-    def _():
-        advance((2, 3), 2)
 
     def push_far(at):
         return [
@@ -360,6 +386,8 @@
     def _():
         j = i - 1
         dealt[...] = normed[pl.ds(pl.multiple_of(j * tile, tile), tile), :]
+        rows_p[...] = rows_in[pl.ds(pl.multiple_of(j * tile, tile), tile), :]
+        cot_p[...] = permute_tile(perm[...], cotangent[...], span).astype(BF16)
         driven[...] = dot(dealt[...], drive[...])
         rate_re = spread(rates[0:1, :], SUB)
         rate_im = spread(rates[1:2, :], SUB)
@@ -385,36 +413,74 @@
 
     @pl.when(i == tiles + 1)
     def _():
-        onward = []
-        for k, copy in enumerate(push_far((column,))):
-            copy.wait()
-            there = 2 * lax.rem(mine[1] + grid.shape[1] - 1 - k, grid.shape[1]) + mine[2]
-            onward.append(push_near((there,), far + 1 + k))
-            onward[-1].start()
-        push_near((column,), far).wait()
-        for copy in onward:
-            copy.wait()
+        def arrive():
+            onward = []
+            for k, copy in enumerate(push_far((column,))):
+                copy.wait()
+                there = 2 * lax.rem(mine[1] + grid.shape[1] - 1 - k, grid.shape[1]) + mine[2]
+                onward.append(push_near((there,), far + 1 + k))
+                onward[-1].start()
+            advance((1, 2, 3), 2)
+            push_near((column,), far).wait()
+            for copy in onward:
+                copy.wait()
+
         cross_blocks(
-            members, False, pieces, place, own_place, broken, rates[2:3, :], rates[3:4, :], dealt_ends, carries
+            members, False, arrive, pieces, place, own_place, broken, rates[2:3, :], rates[3:4, :], chosen, dealt_ends,
+            carries,
         )
-        advance((2, 3), phases)
-
-
-def main_kernel(
-    grid, block_rows, cotangent, dealt, driven, carry, keep, rates, readout, vectors, mixer, perm, back, place,
-    own_place, broken,
-    gated_low, mixed_low, joined, joined_grad, weight_grad, bias_grad, through_grad, readout_grad, mixed_sum, coming,
-    pieces, dealt_heads, push_send, push_recv,
+        advance((1, 2, 3), phases)
+
+
+def split(values):
+    high = values.astype(BF16)
+    rest = values - high.astype(F32)
+    middle = rest.astype(BF16)
+    return high, middle, (rest - middle.astype(F32)).astype(BF16)
+
+
+def row_times(row, matrix):
+    wide = [jnp.broadcast_to(piece.astype(F32), (SUB, row.shape[1])).astype(BF16) for piece in split(row)]
+    return sum(contract_cols(piece, matrix) for piece in wide)[0:1]
+
+
+def row_sums(matrix):
+    ones = jnp.ones((SUB, matrix.shape[1]), BF16)
+    return sum(contract_cols(ones, piece) for piece in split(matrix))[0:1]
+
+
+def back_kernel(
+    grid, block_rows, orders, cotangent, dealt, driven, carry, keep, rows_p, rates, readout, vectors, mixer, place,
+    own_place, broken, drive, drive_raw,
+    gated_low, token_part, drive_sum, readout_sum, weight_sum, vector_sum,
+    joined_all, joined_grad_all, mixed_all, coming, weight_grad, bias_grad, through_grad, readout_grad, mixed_sum,
+    drive_grad, decay_cot, driven_sum, pieces, chosen, dealt_heads, push_send, push_recv, *rest,
 ):
     i = pl.program_id(0)
-    tiles = pl.num_programs(0) - 1
-    _, column, _ = grid.here()
+    tiles = (pl.num_programs(0) - 2) // 3
+    row, column, mine = grid.here()
     members = grid.members
+    core = 2
+    phases = 3
     span = SUB * block_rows
     tile, width = cotangent.shape
-    states = rates.shape[1]
+    both = joined_all.shape[1]
+    states = both // 2
     chains = tile // span
     tile_blocks = tile // block_rows
+    rest = list(rest)
+    parts = (readout_grad, weight_grad, drive_grad)
+    outs = (readout_sum, weight_sum, drive_sum)
+    count = len(parts)
+    accs = [rest.pop(0) for _ in range(count)]
+    stages = [[rest.pop(0) for _ in range(phases)] for _ in range(count)]
+    landed = [[rest.pop(0) for _ in range(phases)] for _ in range(count)]
+    vector_stage, across, along, send, recv, vector_send, vector_recv = rest
+    plans = [reduce_plan(grid, order) for order in orders]
+    every = (0, 1, 2)
+    kept = every[:-1]
+    first_a = tiles + 1
+    first_b = 2 * tiles + 1
 
     def push_to(at):
         return [
@@ -425,21 +491,103 @@
             for away in range(1, members)
         ]
 
+    def combos(left):
+        return list(itertools.product(*[range(grid.shape[d]) for d in left]))
+
+    def at_of(dim, index, left, combo, dims):
+        chosen_of = dict(zip(left, combo))
+        chosen_of[dim] = index
+        return tuple(chosen_of[d] if d in chosen_of else mine[d] for d in dims)
+
+    def piece_of(k, dim, index, left, combo):
+        if dim != core:
+            return accs[k][at_of(dim, index, left, combo, kept)]
+        size = outs[k].shape[0]
+        down, half, low = at_of(dim, index, left, combo, every)
+        start = ((down * grid.shape[1] + half) * 2 + low) * size
+        if size % SUB == 0:
+            return parts[k][pl.ds(pl.multiple_of(start, size), size), :]
+        low_row = jnp.minimum(lax.div(start, SUB) * SUB, parts[k].shape[0] - 2 * SUB)
+        window = parts[k][pl.ds(pl.multiple_of(low_row, SUB), 2 * SUB), :]
+        return pltpu.roll(window, lax.rem(2 * SUB - (start - low_row), 2 * SUB), 0)[:size]
+
+    def hops(k, phase):
+        dim = plans[k][phase][0]
+        base = k * grid.slots + sum(grid.fan(d) for d in orders[k][:phase])
+        return [
+            (
+                remote(
+                    stages[k][phase].at[slot], landed[k][phase].at[slot], send.at[base + slot], recv.at[base + slot],
+                    device,
+                ),
+                slot,
+                index,
+            )
+            for slot, device, index in grid.peers(dim)
+        ]
+
+    def begin(k, phase):
+        dim, _, left = plans[k][phase]
+        for copy, slot, index in hops(k, phase):
+            for combo in combos(left):
+                stages[k][phase][(slot,) + combo] = piece_of(k, dim, index, left, combo).astype(BF16)
+            copy.start()
+
+    def finish(k, phase):
+        dim, _, left = plans[k][phase]
+        copies = hops(k, phase)
+        for copy, _, _ in copies:
+            copy.wait()
+        for combo in combos(left):
+            piece = piece_of(k, dim, mine[dim], left, combo)
+            for _, slot, _ in copies:
+                piece = piece + landed[k][phase][(slot,) + combo].astype(F32)
+            accs[k][at_of(dim, mine[dim], left, combo, kept)] = piece
+
+    def advance(ks, phase):
+        for k in ks:
+            if phase:
+                finish(k, phase - 1)
+            if phase < phases:
+                begin(k, phase)
+            else:
+                outs[k][...] = accs[k][mine[:-1]]
+
+    def vector_across():
+        return [
+            remote(
+                vector_stage, across.at[away - 1], vector_send.at[away - 1], vector_recv.at[away - 1],
+                {"fsdp": lax.rem(column + away, members)},
+            )
+            for away in range(1, members)
+        ]
+
+    def vector_along():
+        return [
+            remote(
+                vector_sum, along.at[slot], vector_send.at[members - 1 + slot], vector_recv.at[members - 1 + slot], device
+            )
+            for slot, device, _ in grid.peers(0)
+        ]
+
+    rate_re = spread(rates[0:1, :], SUB)
+    rate_im = spread(rates[1:2, :], SUB)
+
     @pl.when(i == 0)
     def _():
-        weight_grad[...] = jnp.zeros_like(weight_grad)
-        bias_grad[...] = jnp.zeros_like(bias_grad)
-        through_grad[...] = jnp.zeros_like(through_grad)
-        readout_grad[...] = jnp.zeros_like(readout_grad)
-        mixed_sum[...] = jnp.zeros_like(mixed_sum)
+        for total in (
+            weight_grad, bias_grad, through_grad, readout_grad, mixed_sum, drive_grad, decay_cot, driven_sum
+        ):
+            total[...] = jnp.zeros_like(total)
         announce(grid)
 
     @pl.when(i < tiles)
     def _():
         through = vectors[2:3, :width]
         bias = vectors[3:4, : 2 * width]
-        rate_re = spread(rates[0:1, :], SUB)
-        rate_im = spread(rates[1:2, :], SUB)
+        here = pl.ds(pl.multiple_of(i * tile, tile), tile)
+        joined = joined_all.at[here]
+        joined_grad = joined_grad_all.at[here]
         state = [
             (carry[c * SUB : (c + 1) * SUB, :states], carry[c * SUB : (c + 1) * SUB, states:])
             for c in range(chains)
@@ -462,10 +610,10 @@
         dealt_f32 = dealt[...].astype(F32)
         mixed = dot(joined[...], readout[...]) + through * dealt_f32
         activated, slope = gelu_parts(mixed)
-        features = permute_tile(back[...], activated.astype(BF16), span).astype(BF16)
+        features = activated.astype(BF16)
         hidden = dot(features, mixer[...]) + bias
         value = hidden[:, :width]
-        sig = 1.0 / (1.0 + jnp.exp(-hidden[:, width:]))
+        sig = 0.5 + 0.5 * jnp.tanh(0.5 * hidden[:, width:])
         gated_low[...] = (value * sig).astype(BF16)
         cot_sig = cotangent[...].astype(F32) * sig
         hidden_low = jnp.concatenate(
@@ -474,8 +622,8 @@
         weight_grad[...] += contract_rows(features, hidden_low)
         bias_grad[...] += jnp.sum(hidden_low.astype(F32), axis=0, keepdims=True)
         feature_grad = contract_cols(hidden_low, mixer[...]).astype(BF16)
-        mixed_grad = (permute_tile(perm[...], feature_grad, span) * slope).astype(BF16)
-        mixed_low[...] = mixed_grad
+        mixed_grad = (feature_grad.astype(F32) * slope).astype(BF16)
+        mixed_all[here, :] = mixed_grad
         mixed_f32 = mixed_grad.astype(F32)
         through_grad[...] += jnp.sum(mixed_f32 * dealt_f32, axis=0, keepdims=True)
         mixed_sum[...] += jnp.sum(mixed_f32, axis=0, keepdims=True)
@@ -503,169 +651,43 @@
 
     @pl.when(i == tiles)
     def _():
-        for copy in push_to((column,)):
-            copy.wait()
+        def arrive():
+            advance((0, 1), 0)
+            for copy in push_to((column,)):
+                copy.wait()
+
         cross_blocks(
-            members, True, pieces, place, own_place, broken, rates[2:3, :], rates[3:4, :], dealt_heads, coming
+            members, True, arrive, pieces, place, own_place, broken, rates[2:3, :], rates[3:4, :], chosen, dealt_heads,
+            coming,
         )
-
-
-def split(values):
-    high = values.astype(BF16)
-    rest = values - high.astype(F32)
-    middle = rest.astype(BF16)
-    return high, middle, (rest - middle.astype(F32)).astype(BF16)
-
-
-def row_times(row, matrix):
-    wide = [jnp.broadcast_to(piece.astype(F32), (SUB, row.shape[1])).astype(BF16) for piece in split(row)]
-    return sum(contract_cols(piece, matrix) for piece in wide)[0:1]
-
-
-def row_sums(matrix):
-    ones = jnp.ones((SUB, matrix.shape[1]), BF16)
-    return sum(contract_cols(ones, piece) for piece in split(matrix))[0:1]
-
-
-def last_kernel(
-    grid, block_rows, orders, dealt, joined, joined_grad, carry, coming, keep, mixed_low, tokens, rates, vectors, drive,
-    drive_raw, back, readout_grad, weight_grad, bias_grad, through_grad, mixed_sum,
-    token_part, drive_sum, readout_sum, weight_sum, vector_sum,
-    driven_all, drive_grad, drive_parts, decay_cot, driven_sum, *rest,
-):
-    i = pl.program_id(0)
-    tiles = (pl.num_programs(0) - 1) // 2
-    row, column, mine = grid.here()
-    members = grid.members
-    core = 2
-    phases = 3
-    span = SUB * block_rows
-    tile, width = tokens.shape
-    both = joined.shape[1]
-    states = both // 2
-    chains = tile // span
-    rest = list(rest)
-    parts = (readout_grad, weight_grad, drive_parts)
-    outs = (readout_sum, weight_sum, drive_sum)
-    count = len(parts)
-    accs = [rest.pop(0) for _ in range(count)]
-    stages = [[rest.pop(0) for _ in range(phases)] for _ in range(count)]
-    landed = [[rest.pop(0) for _ in range(phases)] for _ in range(count)]
-    vector_stage, across, along, send, recv, vector_send, vector_recv = rest
-    plans = [reduce_plan(grid, order) for order in orders]
-    every = (0, 1, 2)
-    kept = every[:-1]
-
-    def combos(left):
-        return list(itertools.product(*[range(grid.shape[d]) for d in left]))
-
-    def at(dim, index, left, combo, dims):
-        chosen = dict(zip(left, combo))
-        chosen[dim] = index
-        return tuple(chosen[d] if d in chosen else mine[d] for d in dims)
-
-    def hops(k, phase):
-        dim = plans[k][phase][0]
-        base = k * grid.slots + sum(grid.fan(d) for d in orders[k][:phase])
-        return [
-            (
-                remote(
-                    stages[k][phase].at[slot], landed[k][phase].at[slot], send.at[base + slot], recv.at[base + slot],
-                    device,
-                ),
-                slot,
-                index,
-            )
-            for slot, device, index in grid.peers(dim)
-        ]
-
-    def begin(k, phase):
-        dim, _, left = plans[k][phase]
-        for copy, slot, index in hops(k, phase):
-            for combo in combos(left):
-                if dim == core:
-                    piece = parts[k][at(dim, index, left, combo, every)]
-                else:
-                    piece = accs[k][at(dim, index, left, combo, kept)]
-                stages[k][phase][(slot,) + combo] = piece.astype(BF16)
-            copy.start()
-
-    def finish(k, phase):
-        dim, _, left = plans[k][phase]
-        copies = hops(k, phase)
-        for copy, _, _ in copies:
-            copy.wait()
-        for combo in combos(left):
-            if dim == core:
-                piece = parts[k][at(dim, mine[dim], left, combo, every)]
-            else:
-                piece = accs[k][at(dim, mine[dim], left, combo, kept)]
-            for _, slot, _ in copies:
-                piece = piece + landed[k][phase][(slot,) + combo].astype(F32)
-            accs[k][at(dim, mine[dim], left, combo, kept)] = piece
-
-    def advance(ks, phase):
-        for k in ks:
-            if phase:
-                finish(k, phase - 1)
-            if phase < phases:
-                begin(k, phase)
-            else:
-                outs[k][...] = accs[k][mine[:-1]]
-
-    rate_re = spread(rates[0:1, :], SUB)
-    rate_im = spread(rates[1:2, :], SUB)
-
-    def vector_across():
-        return [
-            remote(
-                vector_stage, across.at[away - 1], vector_send.at[away - 1], vector_recv.at[away - 1],
-                {"fsdp": lax.rem(column + away, members)},
-            )
-            for away in range(1, members)
-        ]
-
-    def vector_along():
-        return [
-            remote(
-                vector_sum, along.at[slot], vector_send.at[members - 1 + slot], vector_recv.at[members - 1 + slot], device
-            )
-            for slot, device, _ in grid.peers(0)
-        ]
-
-    @pl.when(i == 0)
-    def _():
-        drive_grad[...] = jnp.zeros_like(drive_grad)
-        decay_cot[...] = jnp.zeros_like(decay_cot)
-        driven_sum[...] = jnp.zeros_like(driven_sum)
-        announce(grid)
-
-    @pl.when(i == 1)
-    def _():
-        meet(grid)
-        advance((0, 1), 0)
-
-    @pl.when(i == 3)
-    def _():
         advance((0, 1), 1)
 
-    @pl.when(i == tiles - 1)
+    @pl.when(i == first_a + tiles // 2)
+    def _():
+        advance((1,), 2)
+
+    @pl.when(i == first_a + tiles - 2)
     def _():
         advance((0,), 2)
 
-    @pl.when(i == tiles + 2)
-    def _():
-        advance((1,), 2)
-
-    @pl.when(i == 2 * tiles - 1)
-    def _():
-        advance((0, 1), 3)
-
-    @pl.when(i < tiles)
-    def _():
-        driven_low = driven_all.at[pl.ds(pl.multiple_of(i * tile, tile), tile)]
+    @pl.when(i == first_b)
+    def _():
+        advance((1,), 3)
+
+    @pl.when(i == first_b + 2)
+    def _():
+        advance((0,), 3)
+
+    @pl.when((i >= first_a) & (i < first_b))
+    def _():
+        j = first_b - 1 - i
+        here = pl.ds(pl.multiple_of(j * tile, tile), tile)
+        joined = joined_all.at[here]
+        driven_low = joined
+        joined_grad = joined_grad_all.at[here]
+        entering = coming[pl.ds(pl.multiple_of(j * tile_blocks, tile_blocks), tile_blocks), :]
         going = [
-            (coming[c * SUB : (c + 1) * SUB, :states], coming[c * SUB : (c + 1) * SUB, states:])
+            (entering[c * SUB : (c + 1) * SUB, :states], entering[c * SUB : (c + 1) * SUB, states:])
             for c in range(chains)
         ]
         total = [(jnp.zeros((SUB, states), F32), jnp.zeros((SUB, states), F32)) for _ in range(chains)]
@@ -707,11 +729,8 @@
             driven_sum[...] += jnp.concatenate(sums[c], axis=1)
         drive_grad[...] += contract_rows(dealt[...], driven_low[...])
 
-    @pl.when(i == tiles)
-    def _():
-        shard = drive_parts.shape[-2]
-        for s, place in enumerate(itertools.product(*[range(size) for size in grid.shape])):
-            drive_parts[place] = drive_grad[s * shard : (s + 1) * shard, :]
+    @pl.when(i == first_b)
+    def _():
         advance((2,), 0)
         cot = jnp.sum(decay_cot[...], axis=0, keepdims=True)
         factor_re, factor_im = rates[0:1, :], rates[1:2, :]
@@ -736,11 +755,11 @@
         for copy in vector_across():
             copy.start()
 
-    @pl.when(i == tiles + 1)
+    @pl.when(i == first_b + 1)
     def _():
         advance((2,), 1)
 
-    @pl.when(i == tiles + 3)
+    @pl.when(i == first_b + 3)
     def _():
         for copy in vector_across():
             copy.wait()
@@ -751,11 +770,11 @@
         for copy in vector_along():
             copy.start()
 
-    @pl.when(i == tiles + 5)
+    @pl.when(i == first_b + tiles - 2)
     def _():
         advance((2,), 2)
 
-    @pl.when(i == 2 * tiles)
+    @pl.when(i == first_b + tiles)
     def _():
         for copy in vector_along():
             copy.wait()
@@ -765,13 +784,14 @@
         vector_sum[...] = total
         advance((2,), 3)
 
-    @pl.when((i >= tiles) & (i < 2 * tiles))
-    def _():
-        j = i - tiles
-        driven_low = driven_all[pl.ds(pl.multiple_of(j * tile, tile), tile), :]
-        normed_grad = vectors[2:3, :width] * mixed_low[...].astype(F32) + contract_cols(driven_low, drive[...])
-        given = permute_tile(back[...], normed_grad.astype(BF16), span)
-        moved, rstd = norm_stats(tokens[...].astype(F32))
+    @pl.when((i >= first_b) & (i < first_b + tiles))
+    def _():
+        j = i - first_b
+        here = pl.ds(pl.multiple_of(j * tile, tile), tile)
+        driven_low = joined_all[here, :]
+        normed_grad = vectors[2:3, :width] * mixed_all[here, :].astype(F32) + contract_cols(driven_low, drive[...])
+        given = normed_grad.astype(BF16).astype(F32)
+        moved, rstd = norm_stats(rows_p[...].astype(F32))
         xhat = moved * rstd
         scaled = given * vectors[0:1, :width]
         inner = jnp.mean(scaled * xhat, axis=-1, keepdims=True)
@@ -781,15 +801,15 @@
 
 
 def tail_kernel(
-    grid, tokens, cotangent, token_part, gated_low, rates, drive_sum, readout_sum, weight_sum, vector_sum,
+    grid, span, tokens, cotangent, token_part, gated_low, back, rates, drive_sum, readout_sum, weight_sum, vector_sum,
     out, token_grad, gain_grad, shift_grad, real_grad, rotation_grad, timestep_grad, drive_grad, readout_grad,
     through_grad, weight_grad, bias_grad,
 ):
     width = tokens.shape[1]
     both = vector_sum.shape[1]
     states = both // 2
-    out[...] = tokens[...].astype(F32) + gated_low[...].astype(F32)
-    token_grad[...] = cotangent[...].astype(F32) + token_part[...].astype(F32)
+    out[...] = tokens[...].astype(F32) + permute_tile(back[...], gated_low[...], span)
+    token_grad[...] = cotangent[...].astype(F32) + permute_tile(back[...], token_part[...], span)
 
     @pl.when(pl.program_id(0) == 0)
     def _():
@@ -860,10 +880,11 @@
     states = both // 2
     block_rows = rows // blocks
     span = SUB * block_rows
-    tile = 2 * span
+    tile = 2 * span if members <= SUB else span
     tiles = rows // tile
     tile_blocks = tile // block_rows
     total = blocks * members
+    chunk = min(total, 2**30 // total**2)
     sequences = sequence_lengths.shape[1]
     shape = jax.ShapeDtypeStruct
     anywhere = pl.BlockSpec(memory_space=pl.ANY)
@@ -874,12 +895,6 @@
     perm = jnp.asarray(source[:, None] == order[None], BF16)
     back = jnp.asarray(order[:, None] == source[None], BF16)
 
-    def early(rows_of, columns):
-        return pl.BlockSpec((rows_of, columns), lambda i: (jnp.minimum(i, tiles - 1), 0))
-
-    def late(rows_of, columns):
-        return pl.BlockSpec((rows_of, columns), lambda i: (jnp.clip(i - tiles, 0, tiles - 1), 0))
-
     def flat(size):
         return pl.BlockSpec((size,), lambda i: (0,))
 
@@ -891,20 +906,22 @@
     def shifted(rows_of, columns):
         return pl.BlockSpec((rows_of, columns), lambda i: (jnp.clip(i - 1, 0, tiles - 1), 0))
 
-    dealt, driven, keep, carry, drive, drive_raw, readout, mixer, vectors, rates, place, own_place, broken = pl.pallas_call(
+    dealt, rows_p, cot_p, driven, keep, carry, drive, drive_raw, readout, mixer, vectors, rates, place, own_place, broken = pl.pallas_call(
         functools.partial(front_kernel, grid, block_rows, counts, tile),
         grid=(tiles + 2,),
-        in_specs=[anywhere]
+        in_specs=[anywhere, shifted(tile, width)]
         + [flat(size) for size in counts]
         + [whole((1, sequences)), anywhere, anywhere, anywhere, whole((span, span))],
         out_specs=[
-            shifted(tile, width), shifted(tile, both), shifted(tile, LANES), total_of((blocks, both)),
+            shifted(tile, width), shifted(tile, width), shifted(tile, width), shifted(tile, both), shifted(tile, LANES),
+            total_of((blocks, both)),
             total_of((width, both)),
             total_of((width, both)), anywhere, anywhere, total_of((SUB, 2 * width)), total_of((SUB, states)),
             total_of((1, total)), total_of((blocks, LANES)), total_of((sequences, members, LANES)),
         ],
         out_shape=[
-            shape((rows, width), BF16), shape((rows, both), F32), shape((rows, LANES), F32), shape((blocks, both), F32),
+            shape((rows, width), BF16), shape((rows, width), BF16), shape((rows, width), BF16),
+            shape((rows, both), F32), shape((rows, LANES), F32), shape((blocks, both), F32),
             shape((width, both), BF16), shape((width, both), BF16),
             shape(grid.shape + readout_matrix.shape, BF16), shape(grid.shape + mixer_weight.shape, BF16),
             shape((SUB, 2 * width), F32), shape((SUB, states), F32), shape((1, total), F32),
@@ -918,42 +935,28 @@
             pltpu.VMEM(grid.shape + drive_matrix.shape, BF16),
             pltpu.VMEM((blocks, LANES), jnp.int32),
             pltpu.VMEM((members, blocks, both), BF16),
+            pltpu.VMEM((chunk, total), BF16),
             pltpu.VMEM((total, both), F32),
             regular((4 * slots,)), regular((4 * slots,)), regular((len(shards) + tiles,)), regular((members,)),
-            regular((members,)),
+            regular((members,)), regular((grid.dp * members - 1,)), regular((grid.dp * members - 1,)),
         ],
         compiler_params=params(0),
         name="front",
-    )(tokens, *small, sequence_lengths, *shards, perm)
+    )(tokens, cotangent, *small, sequence_lengths, *shards, perm)
     readout = readout.reshape(both, width)
     mixer = mixer.reshape(width, 2 * width)
 
-    gated_low, mixed_low, joined, joined_grad, weight_grad, bias_grad, through_grad, readout_grad, mixed_sum, coming = pl.pallas_call(
-        functools.partial(main_kernel, grid, block_rows),
-        grid=(tiles + 1,),
-        in_specs=[
-            early(tile, width), early(tile, width), early(tile, both), early(tile_blocks, both),
-            early(tile, LANES), whole((SUB, states)), whole((both, width)), whole((SUB, 2 * width)),
-            whole((width, 2 * width)), whole((span, span)), whole((span, span)), whole((1, total)),
-            whole((blocks, LANES)), whole((sequences, members, LANES)),
-        ],
-        out_specs=[
-            early(tile, width), early(tile, width), early(tile, both), early(tile, both),
-            total_of((width, 2 * width)), total_of((1, 2 * width)), total_of((1, width)), total_of((both, width)),
-            total_of((1, width)), total_of((blocks, both)),
-        ],
-        out_shape=[
-            shape((rows, width), BF16), shape((rows, width), BF16), shape((rows, both), BF16),
-            shape((rows, both), F32), shape((width, 2 * width), F32), shape((1, 2 * width), F32),
-            shape((1, width), F32), shape((both, width), F32), shape((1, width), F32), shape((blocks, both), F32),
-        ],
-        scratch_shapes=[
-            pltpu.VMEM((members, blocks, both), BF16), pltpu.VMEM((total, both), F32), regular((members - 1,)),
-            regular((members - 1,)),
-        ],
-        compiler_params=params(1),
-        name="main",
-    )(cotangent, dealt, driven, carry, keep, rates, readout, vectors, mixer, perm, back, place, own_place, broken)
+    def first(rows_of, columns):
+        return pl.BlockSpec((rows_of, columns), lambda i: (jnp.minimum(i, tiles - 1), 0))
+
+    def twice(rows_of, columns):
+        def index(i):
+            return (jnp.where(i <= tiles, jnp.minimum(i, tiles - 1), jnp.maximum(2 * tiles - i, 0)), 0)
+
+        return pl.BlockSpec((rows_of, columns), index)
+
+    def final(rows_of, columns):
+        return pl.BlockSpec((rows_of, columns), lambda i: (jnp.clip(i - 2 * tiles - 1, 0, tiles - 1), 0))
 
     orders = ((2, 0, 1), (2, 1, 0), (2, 1, 0))
     weights = (readout_matrix, mixer_weight, drive_matrix)
@@ -961,27 +964,30 @@
     for turn, weight in zip(orders, weights):
         for dim, _, left in reduce_plan(grid, turn):
             buffers.append(pltpu.VMEM((grid.fan(dim),) + tuple(grid.shape[d] for d in left) + weight.shape, BF16))
-    token_part, drive_sum, readout_sum, weight_sum, vector_sum = pl.pallas_call(
-        functools.partial(last_kernel, grid, block_rows, orders),
-        grid=(2 * tiles + 1,),
+    gated_low, token_part, drive_sum, readout_sum, weight_sum, vector_sum = pl.pallas_call(
+        functools.partial(back_kernel, grid, block_rows, orders),
+        grid=(3 * tiles + 2,),
         in_specs=[
-            early(tile, width), early(tile, both), early(tile, both), early(tile_blocks, both), early(tile_blocks, both),
-            early(tile, LANES), late(tile, width), late(tile, width), whole((SUB, states)), whole((SUB, 2 * width)),
-            whole((width, both)), whole((width, both)), whole((span, span)), whole(grid.shape + readout_matrix.shape),
-            whole(grid.shape + mixer_weight.shape), whole((1, 2 * width)), whole((1, width)), whole((1, width)),
+            first(tile, width), twice(tile, width), first(tile, both), twice(tile_blocks, both), twice(tile, LANES),
+            final(tile, width), whole((SUB, states)), whole((both, width)), whole((SUB, 2 * width)),
+            whole((width, 2 * width)), whole((1, total)), whole((blocks, LANES)), whole((sequences, members, LANES)),
+            whole((width, both)), whole((width, both)),
         ],
         out_specs=[
-            late(tile, width), total_of(drive_matrix.shape), total_of(readout_matrix.shape),
+            first(tile, width), final(tile, width), total_of(drive_matrix.shape), total_of(readout_matrix.shape),
             total_of(mixer_weight.shape), total_of((SUB, both)),
         ],
         out_shape=[
-            shape((rows, width), BF16), shape(drive_matrix.shape, F32), shape(readout_matrix.shape, F32),
-            shape(mixer_weight.shape, F32), shape((SUB, both), F32),
+            shape((rows, width), BF16), shape((rows, width), BF16), shape(drive_matrix.shape, F32),
+            shape(readout_matrix.shape, F32), shape(mixer_weight.shape, F32), shape((SUB, both), F32),
         ],
         scratch_shapes=[
-            pltpu.VMEM((rows, both), BF16), pltpu.VMEM((width, both), F32),
-            pltpu.VMEM(grid.shape + drive_matrix.shape, F32), pltpu.VMEM((SUB, both), F32),
-            pltpu.VMEM((SUB, both), F32),
+            pltpu.VMEM((rows, both), BF16), pltpu.VMEM((rows, both), F32), pltpu.VMEM((rows, width), BF16),
+            pltpu.VMEM((blocks, both), F32), pltpu.VMEM((width, 2 * width), F32), pltpu.VMEM((1, 2 * width), F32),
+            pltpu.VMEM((1, width), F32), pltpu.VMEM((both, width), F32), pltpu.VMEM((1, width), F32),
+            pltpu.VMEM((width, both), F32), pltpu.VMEM((SUB, both), F32), pltpu.VMEM((SUB, both), F32),
+            pltpu.VMEM((members, blocks, both), BF16), pltpu.VMEM((chunk, total), BF16), pltpu.VMEM((total, both), F32),
+            regular((members - 1,)), regular((members - 1,)),
         ]
         + [pltpu.VMEM(grid.shape[:-1] + weight.shape, F32) for weight in weights]
         + buffers
@@ -991,22 +997,21 @@
             pltpu.VMEM((grid.dp - 1, SUB, both), F32), regular((3 * slots,)), regular((3 * slots,)),
             regular((members + grid.dp - 2,)), regular((members + grid.dp - 2,)),
         ],
-        compiler_params=params(2),
-        name="last",
+        compiler_params=params(1),
+        name="back",
     )(
-        dealt, joined, joined_grad, carry, coming, keep, mixed_low, tokens, rates, vectors, drive, drive_raw, back,
-        readout_grad.reshape(grid.shape + readout_matrix.shape), weight_grad.reshape(grid.shape + mixer_weight.shape),
-        bias_grad, through_grad, mixed_sum,
+        cot_p, dealt, driven, carry, keep, rows_p, rates, readout, vectors, mixer, place, own_place, broken, drive,
+        drive_raw,
     )
 
     vector_sizes = [v.shape[0] for v in (norm_gain, norm_shift, decay_real, decay_rotation, log_timestep)]
     slab = 2 * tile
     outs = pl.pallas_call(
-        functools.partial(tail_kernel, grid),
+        functools.partial(tail_kernel, grid, span),
         grid=(rows // slab,),
         in_specs=[tiled(slab, width)] * 4
         + [
-            whole((SUB, states)), whole(drive_matrix.shape), whole(readout_matrix.shape),
+            whole((span, span)), whole((SUB, states)), whole(drive_matrix.shape), whole(readout_matrix.shape),
             whole(mixer_weight.shape), whole((SUB, both)),
         ],
         out_specs=[tiled(slab, width)] * 2
@@ -1023,7 +1028,7 @@
         ],
         compiler_params=params(),
         name="tail",
-    )(tokens, cotangent, token_part, gated_low, rates, drive_sum, readout_sum, weight_sum, vector_sum)
+    )(tokens, cotangent, token_part, gated_low, back, rates, drive_sum, readout_sum, weight_sum, vector_sum)
     return tuple(outs)
 
 

time: 148 us -> 138 us (0.932)
  Pallas kernels: 147 us -> 137 us
    pallas_call x3 -> x2, Pallas kernels: 102 us -> 92.4 us  [the longest x1 79.7 us: body(): pl.pallas_call(functools.partial(back_kernel, grid, block_rows, orders),...]
where the time goes in v3:
time: 138 us
  Pallas kernels  137 us (99%)
    pallas_call x1, Pallas kernels, body(): pl.pallas_call(functools.partial(back_kernel, grid, block_rows, orders),...  79.7 us
    pallas_call x1, Pallas kernels, body(): pl.pallas_call(functools.partial(front_kernel, grid, block_rows, counts,...  44.8 us
    pallas_call x1, Pallas kernels, body(): pl.pallas_call(functools.partial(tail_kernel, grid, span), grid=(rows //...  12.6 us

profile of v3, /device:TPU:0, one launch (start us, length us, event | category | flops | bytes accessed | tf_op | source)
XLA Modules:
  0.0 137.9 jit_solution(15403373182559350467)
XLA Ops:
  0.6 44.8 %front.1 = (bf16[4096,512]{1,0:T(8,128)(2,1)}, bf16[4096,512]{1,0:T(8,128)(2,1)}, bf16[4096,512]{1,0:T(8,128)(2,1)}, f32[4096,768]{1,0:T(8,128)}, f32[4096,128]{...) custom-call(bf16[4096,512]{1,0:T(8,128)(2,1)} %tokens.3, ...), custom_call_target="tpu_custom_call" | custom-call | tf_op jit(solution)/shard_map/front/pallas_call | solution.py:909
  45.4 79.7 %back.2 = (bf16[4096,512]{1,0:T(8,128)(2,1)}, bf16[4096,512]{1,0:T(8,128)(2,1)}, f32[16,768]{1,0:T(8,128)}, f32[24,512]{1,0:T(8,128)}, f32[16,1024]{1,0:T(8,128)}, /*index=5*/f32[8,768]{1,0:T(8,128)}) custom-call(bf16[4096,512]{1,0:T(8,128)(2,1)} %get-tuple-element.33.cotangent, bf16[4096,512]{1,0:T(8,128)(2,1)} %get-tuple-element.34.dealt, ...), custom_call_target="tpu_custom_call" | custom-call | tf_op jit(solution)/shard_map/back/pallas_call | solution.py:967
  125.2 12.6 %tail.1 = (f32[4096,512]{1,0:T(8,128)}, f32[4096,512]{1,0:T(8,128)}, f32[16]{0:T(128)}, f32[16]{0:T(128)}, f32[12]{0:T(128)}, /*index=5*/f32[12]{0:T(128)}, f32[...) custom-call(bf16[4096,512]{1,0:T(8,128)(2,1)} %tokens.3, ...), custom_call_target="tpu_custom_call" | custom-call | tf_op jit(solution)/shard_map/tail/pallas_call | solution.py:1009

commit v4 on v3

--- a/solution.py
+++ b/solution.py
@@ -15,7 +15,7 @@
 BF16 = jnp.bfloat16
 LANES = 128
 SUB = 8
-VMEM_LIMIT = 63 * 1024 * 1024
+VMEM_LIMIT = 65400 * 1024
 
 
 def dot(left, right):
@@ -164,10 +164,19 @@
     return timestep, factor_re, factor_im, modulus, scale_re, scale_im
 
 
-def cross_blocks(members, reverse, arrive, pieces, place, own_place, broken, flow_re, flow_im, chosen, dealt, carries):
+def encode(values, inverse):
+    scaled = values * inverse
+    most = jnp.maximum(jnp.max(jnp.abs(scaled), axis=1, keepdims=True), 1e-30)
+    power = jnp.broadcast_to(jnp.ceil(jnp.log2(most)), (values.shape[0], LANES))
+    steps = jnp.round(scaled * lanes_to(32000.0 * jnp.exp2(-power), values.shape[1]))
+    return jnp.concatenate([steps, power], axis=1).astype(jnp.int32).astype(jnp.int16)
+
+
+def cross_blocks(members, reverse, arrive, pieces, norm, place, own_place, broken, flow_re, flow_im, chosen, dealt, carries):
     states = flow_re.shape[1]
     total = place.shape[1]
     steps = total // members
+    blocks = steps
     chunk = chosen.shape[0]
 
     def choose(at):
@@ -179,7 +188,17 @@
     for at in range(0, total, chunk):
         if at:
             chosen[...] = choose(at)
-        dealt[at : at + chunk, :] = dot(chosen[...], pieces[...].reshape(total, 2 * states))
+        moved, power = 0.0, 0.0
+        for first in range(0, members, 4):
+            held = pieces[first : first + 4].reshape(4 * blocks, -1).astype(jnp.int32)
+            picked = chosen[:, first * blocks : (first + 4) * blocks]
+            ints = held[:, : 2 * states]
+            high = (ints & -256).astype(F32).astype(BF16)
+            low = (ints & 255).astype(F32).astype(BF16)
+            moved = moved + (dot(picked, high) + dot(picked, low))
+            power = power + dot(picked, held[:, 2 * states :].astype(F32).astype(BF16))
+        moved = moved * (lanes_to(jnp.exp2(power) * (1.0 / 32000.0), 2 * states) * norm)
+        dealt[at : at + chunk, :] = moved.astype(dealt.dtype)
     rate_re = spread(flow_re, members)
     rate_im = spread(-flow_im if reverse else flow_im, members)
     marks = [broken[s] for s in range(broken.shape[0])]
@@ -188,12 +207,12 @@
         re, im = state
         p = steps - 1 - i if reverse else i
         at = pl.multiple_of(p * members, members)
-        here = dealt[pl.ds(at, members), :]
+        here = dealt[pl.ds(at, members), :].astype(F32)
         met = marks[0] == p
         for mark in marks[1:]:
             met = met | (mark == p)
         mask = lanes_to(jnp.where(met, 0.0, 1.0), states)
-        dealt[pl.ds(at, members), :] = jnp.concatenate([re, im], axis=1)
+        dealt[pl.ds(at, members), :] = jnp.concatenate([re, im], axis=1).astype(dealt.dtype)
         return (
             mask * (rate_re * re - rate_im * im) + here[:, :states],
             mask * (rate_re * im + rate_im * re) + here[:, states:],
@@ -207,42 +226,62 @@
     for at in range(0, total, step_rows):
         columns = lax.broadcasted_iota(jnp.int32, (own, step_rows), 1).astype(F32) + float(at)
         taken = jnp.where(columns == lanes_to(own_place[...], step_rows), 1.0, 0.0).astype(BF16)
-        entering = dealt[at : at + step_rows, :]
+        entering = dealt[at : at + step_rows, :].astype(F32)
         high = entering.astype(BF16)
         low = (entering - high.astype(F32)).astype(BF16)
         found = found + (dot(taken, high) + dot(taken, low))
     carries[...] = found
 
 
-def front_kernel(
-    grid, block_rows, counts, tile, tokens, cotangent, gain_s, shift_s, through_s, bias_s, real_s, rotation_s, step_s, target_s,
-    lengths_s, drive_s, readout_s, mixer_s, perm,
-    dealt, rows_p, cot_p, driven, keep, carries, drive, drive_raw, readout_w, mixer_w, vectors, rates, place, own_place, broken,
-    rows_in, normed, xhat, table, drive_w, bits, pieces, chosen, dealt_ends, send, recv, local, push_send, push_recv,
-    table_send, table_recv,
+def split(values):
+    high = values.astype(BF16)
+    rest = values - high.astype(F32)
+    middle = rest.astype(BF16)
+    return high, middle, (rest - middle.astype(F32)).astype(BF16)
+
+
+def row_times(row, matrix):
+    wide = [jnp.broadcast_to(piece.astype(F32), (SUB, row.shape[1])).astype(BF16) for piece in split(row)]
+    return sum(contract_cols(piece, matrix) for piece in wide)[0:1]
+
+
+def row_sums(matrix):
+    ones = jnp.ones((SUB, matrix.shape[1]), BF16)
+    return sum(contract_cols(ones, piece) for piece in split(matrix))[0:1]
+
+
+def layer_kernel(
+    grid, block_rows, counts, tile, orders, tokens, cotangent, gain_s, shift_s, through_s, bias_s, real_s, rotation_s,
+    step_s, target_s, lengths_s, drive_s, readout_s, mixer_s, perm,
+    gated_low, token_part, drive_sum, readout_sum, weight_sum, vector_sum, rates,
+    rows_in, normed, mixed_all, big, joined_all, table, drive_w, readout_w, mixer_w, drive, readout, mixer,
+    vectors, place, own_place, broken, bits, carry, coming, pieces_ends, pieces, chosen, dealt_x, weight_grad,
+    bias_grad, through_grad, readout_grad, mixed_sum, drive_grad, decay_cot, driven_sum, send_w, recv_w, local,
+    ends_send, ends_recv, table_send, table_recv, push_send, push_recv, *rest,
 ):
     i = pl.program_id(0)
-    tiles = pl.num_programs(0) - 2
+    tiles = (pl.num_programs(0) - 2) // 3
     row, column, mine = grid.here()
     members = grid.members
+    core = 2
+    phases = 3
+    span = SUB * block_rows
+    width = rows_in.shape[1]
+    both = joined_all.shape[1]
+    states = both // 2
     blocks = target_s.shape[0]
-    width = tokens.shape[1]
-    both = drive.shape[1]
-    states = both // 2
-    span = SUB * block_rows
     chains = tile // span
     tile_blocks = tile // block_rows
-    axes = tuple(range(len(grid.shape)))
+    axes = (0, 1, 2)
     half = mixer_w.shape[-1] // 2
     wholes = (drive_w, readout_w, mixer_w, mixer_w)
     cuts = (None, None, pl.ds(0, half), pl.ds(half, half))
-    orders = ((0, 1, 2), (1, 0, 2), (1, 0, 2), (0, 1, 2))
-    phases = 3
+    ways = ((0, 1, 2), (1, 0, 2), (1, 0, 2), (0, 1, 2))
 
     def phase_copies(k, phase):
-        order = orders[k]
+        order = ways[k]
         base = k * grid.slots + sum(grid.fan(d) for d in order[:phase])
-        return gather_phase(grid, wholes[k], cuts[k], axes, order[phase], order[:phase], send, recv, base)
+        return gather_phase(grid, wholes[k], cuts[k], axes, order[phase], order[:phase], send_w, recv_w, base)
 
     def table_copies():
         return [
@@ -250,7 +289,7 @@
             for k, device in enumerate(others(grid, True))
         ]
 
-    def advance(ks, phase):
+    def gather_on(ks, phase):
         for k in ks:
             if phase:
                 for copy in phase_copies(k, phase - 1):
@@ -258,6 +297,156 @@
             if phase < phases:
                 for copy in phase_copies(k, phase):
                     copy.start()
+
+    def push_far(at):
+        return [
+            remote(pieces_ends.at[at], pieces_ends.at[at], ends_send.at[slot], ends_recv.at[slot], device)
+            for slot, device, _ in grid.peers(1)
+        ]
+
+    def push_near(at, slot):
+        device = grid.peers(2)[0][1]
+        return remote(pieces_ends.at[at], pieces_ends.at[at], ends_send.at[slot], ends_recv.at[slot], device)
+
+    far = grid.fan(1)
+
+    def tile_at(j):
+        return pl.ds(pl.multiple_of(j * tile, tile), tile)
+
+    def mask_of(marks, c, t):
+        single = 1 << t if t < 31 else -(1 << 31)
+        return lanes_to(jnp.where((marks[c * SUB : (c + 1) * SUB] & single) == 0, 1.0, 0.0), states)
+
+    def marks_of(j):
+        return bits[pl.ds(pl.multiple_of(j * tile_blocks, tile_blocks), tile_blocks), :]
+
+    def of_blocks(ref, j):
+        return ref[pl.ds(pl.multiple_of(j * tile_blocks, tile_blocks), tile_blocks), :]
+
+    def note_norm(k, squares):
+        norm = jnp.sqrt(squares[:, :states] + squares[:, states:])
+        norm = jnp.maximum(jnp.concatenate([norm, norm], axis=1), 1e-20)
+        vectors[k : k + 1, :both] = norm
+        vectors[k + 1 : k + 2, :both] = 1.0 / norm
+
+    def flatten(source, target):
+        size = source.shape[-2]
+        for k, where in enumerate(itertools.product(*[range(n) for n in grid.shape])):
+            target[k * size : (k + 1) * size, :] = source[where]
+
+    rest = list(rest)
+    parts = (readout_grad, weight_grad, drive_grad)
+    outs = (readout_sum, weight_sum, drive_sum)
+    count = len(parts)
+    aligned = [out.shape[0] % SUB == 0 for out in outs]
+    accs = [None if whole_rows else rest.pop(0) for whole_rows in aligned]
+    stages = [[rest.pop(0) for _ in range(phases)] for _ in range(count)]
+    landed = [[rest.pop(0) for _ in range(phases)] for _ in range(count)]
+    vector_stage, across, along, send, recv, vector_send, vector_recv = rest
+    plans = [reduce_plan(grid, order) for order in orders]
+    every = (0, 1, 2)
+    kept = every[:-1]
+    first_a = tiles + 1
+    first_b = 2 * tiles + 1
+
+    def push_to(at):
+        return [
+            remote(
+                pieces.at[at], pieces.at[at], push_send.at[away - 1], push_recv.at[away - 1],
+                {"fsdp": lax.rem(column + away, members)},
+            )
+            for away in range(1, members)
+        ]
+
+    def combos(left):
+        return list(itertools.product(*[range(grid.shape[d]) for d in left]))
+
+    def at_of(dim, index, left, combo, dims):
+        chosen_of = dict(zip(left, combo))
+        chosen_of[dim] = index
+        return tuple(chosen_of[d] if d in chosen_of else mine[d] for d in dims)
+
+    def rows_of(k, where):
+        size = outs[k].shape[0]
+        down, half_of, low = where
+        return pl.ds(pl.multiple_of(((down * grid.shape[1] + half_of) * 2 + low) * size, size), size)
+
+    def keep_piece(k, dim, left, combo, piece):
+        if aligned[k]:
+            parts[k][rows_of(k, at_of(dim, mine[dim], left, combo, every)), :] = piece
+        else:
+            accs[k][at_of(dim, mine[dim], left, combo, kept)] = piece
+
+    def piece_of(k, dim, index, left, combo):
+        if aligned[k]:
+            return parts[k][rows_of(k, at_of(dim, index, left, combo, every)), :]
+        if dim != core:
+            return accs[k][at_of(dim, index, left, combo, kept)]
+        size = outs[k].shape[0]
+        down, half, low = at_of(dim, index, left, combo, every)
+        start = ((down * grid.shape[1] + half) * 2 + low) * size
+        low_row = jnp.minimum(lax.div(start, SUB) * SUB, parts[k].shape[0] - 2 * SUB)
+        window = parts[k][pl.ds(pl.multiple_of(low_row, SUB), 2 * SUB), :]
+        return pltpu.roll(window, lax.rem(2 * SUB - (start - low_row), 2 * SUB), 0)[:size]
+
+    def hops(k, phase):
+        dim = plans[k][phase][0]
+        base = k * grid.slots + sum(grid.fan(d) for d in orders[k][:phase])
+        return [
+            (
+                remote(
+                    stages[k][phase].at[slot], landed[k][phase].at[slot], send.at[base + slot], recv.at[base + slot],
+                    device,
+                ),
+                slot,
+                index,
+            )
+            for slot, device, index in grid.peers(dim)
+        ]
+
+    def begin(k, phase):
+        dim, _, left = plans[k][phase]
+        for copy, slot, index in hops(k, phase):
+            for combo in combos(left):
+                stages[k][phase][(slot,) + combo] = piece_of(k, dim, index, left, combo).astype(BF16)
+            copy.start()
+
+    def finish(k, phase):
+        dim, _, left = plans[k][phase]
+        copies = hops(k, phase)
+        for copy, _, _ in copies:
+            copy.wait()
+        for combo in combos(left):
+            piece = piece_of(k, dim, mine[dim], left, combo)
+            for _, slot, _ in copies:
+                piece = piece + landed[k][phase][(slot,) + combo].astype(F32)
+            keep_piece(k, dim, left, combo, piece)
+
+    def advance(ks, phase):
+        for k in ks:
+            if phase:
+                finish(k, phase - 1)
+            if phase < phases:
+                begin(k, phase)
+            else:
+                outs[k][...] = parts[k][rows_of(k, mine), :] if aligned[k] else accs[k][mine[:-1]]
+
+    def vector_across():
+        return [
+            remote(
+                vector_stage, across.at[away - 1], vector_send.at[away - 1], vector_recv.at[away - 1],
+                {"fsdp": lax.rem(column + away, members)},
+            )
+            for away in range(1, members)
+        ]
+
+    def vector_along():
+        return [
+            remote(
+                vector_sum, along.at[slot], vector_send.at[members - 1 + slot], vector_recv.at[members - 1 + slot], device
+            )
+            for slot, device, _ in grid.peers(0)
+        ]
 
     @pl.when(i == 0)
     def _():
@@ -275,39 +464,45 @@
         sequences = lengths_s.shape[1]
         own[4:5, LANES // 2 : LANES // 2 + sequences] = lengths_s[...].astype(F32)
         announce(grid, True)
+        taps = [
+            pltpu.make_async_copy(
+                cotangent.at[pl.ds(j * tile, tile)], mixed_all.at[pl.ds(j * tile, tile)],
+                local.at[len(copies) + tiles + j],
+            )
+            for j in range(tiles)
+        ]
         chunks = [
             pltpu.make_async_copy(
                 tokens.at[pl.ds(j * tile, tile)], rows_in.at[pl.ds(j * tile, tile)], local.at[len(copies) + j]
             )
             for j in range(tiles)
         ]
-        for copy in chunks:
+        for copy in chunks + taps:
             copy.start()
         for copy in copies:
             copy.wait()
         meet(grid, True)
-        advance((0,), 0)
+        gather_on((0,), 0)
         for copy in table_copies():
             copy.start()
-        advance((1, 2), 0)
-
-        def stats(j, _):
-            at = pl.ds(pl.multiple_of(j * tile, tile), tile)
-            turned = permute_tile(perm[...], rows_in[at, :], span)
-            rows_in[at, :] = turned.astype(BF16)
-            moved, rstd = norm_stats(turned)
-            xhat[at, :] = moved * rstd
-            return 0
+        gather_on((1, 2), 0)
+
+        def turn(ref):
+            def one(j, _):
+                ref[tile_at(j), :] = permute_tile(perm[...], ref[tile_at(j), :], span).astype(BF16)
+                return 0
+
+            return one
 
         for copy in chunks[: tiles // 2]:
             copy.wait()
-        lax.fori_loop(0, tiles // 2, stats, 0)
-        advance((0,), 1)
-        advance((3,), 0)
-        advance((1, 2), 1)
+        lax.fori_loop(0, tiles // 2, turn(rows_in), 0)
+        gather_on((0,), 1)
+        gather_on((3,), 0)
+        gather_on((1, 2), 1)
         for copy in chunks[tiles // 2 :]:
             copy.wait()
-        lax.fori_loop(tiles // 2, tiles, stats, 0)
+        lax.fori_loop(tiles // 2, tiles, turn(rows_in), 0)
         for copy in table_copies():
             copy.wait()
         rows = table[...].reshape(-1, LANES)
@@ -357,62 +552,47 @@
         shift_by = vectors[1:2, :width]
 
         def settle(j, _):
-            at = pl.ds(pl.multiple_of(j * tile, tile), tile)
-            normed[at, :] = (xhat[at, :] * gain + shift_by).astype(BF16)
+            moved, rstd = norm_stats(rows_in[tile_at(j), :].astype(F32))
+            normed[tile_at(j), :] = (moved * rstd * gain + shift_by).astype(BF16)
             return 0
 
-        advance((0,), 2)
-        lax.fori_loop(0, tiles, settle, 0)
-        advance((0,), 3)
-        advance((3,), 1)
-        drive_raw[...] = drive_w[...].reshape(width, both)
-        raw = drive_raw[...].astype(F32)
+        lax.fori_loop(0, tiles // 2, settle, 0)
+        gather_on((0,), 2)
+        lax.fori_loop(tiles // 2, tiles, settle, 0)
+        gather_on((0,), 3)
+        gather_on((3,), 1)
+        raw = drive_w[...].reshape(width, both).astype(F32)
         drive[:, :states] = (scale_re * raw[:, :states] - scale_im * raw[:, states:]).astype(BF16)
         drive[:, states:] = (scale_re * raw[:, states:] + scale_im * raw[:, :states]).astype(BF16)
-
-    def push_far(at):
-        return [
-            remote(pieces.at[at], pieces.at[at], push_send.at[slot], push_recv.at[slot], device)
-            for slot, device, _ in grid.peers(1)
-        ]
-
-    def push_near(at, slot):
-        device = grid.peers(2)[0][1]
-        return remote(pieces.at[at], pieces.at[at], push_send.at[slot], push_recv.at[slot], device)
-
-    far = grid.fan(1)
-
-    @pl.when((i >= 1) & (i <= tiles))
-    def _():
-        j = i - 1
-        dealt[...] = normed[pl.ds(pl.multiple_of(j * tile, tile), tile), :]
-        rows_p[...] = rows_in[pl.ds(pl.multiple_of(j * tile, tile), tile), :]
-        cot_p[...] = permute_tile(perm[...], cotangent[...], span).astype(BF16)
-        driven[...] = dot(dealt[...], drive[...])
+        note_norm(4, jnp.sum(jnp.square(drive[...].astype(F32)), axis=0, keepdims=True))
         rate_re = spread(rates[0:1, :], SUB)
         rate_im = spread(rates[1:2, :], SUB)
-        first = pl.multiple_of(j * tile_blocks, tile_blocks)
-        mark = bits[pl.ds(first, tile_blocks), :]
-        state = [(jnp.zeros((SUB, states), F32), jnp.zeros((SUB, states), F32)) for _ in range(chains)]
-        for t in range(block_rows):
-            single = 1 << t if t < 31 else -(1 << 31)
-            for c in range(chains):
-                at = c * span + t * SUB
-                narrow = jnp.where((mark[c * SUB : (c + 1) * SUB] & single) == 0, 1.0, 0.0)
-                keep[at : at + SUB, :] = narrow
-                mask = lanes_to(narrow, states)
-                re, im = state[c]
-                now_re = mask * (rate_re * re - rate_im * im) + driven[at : at + SUB, :states]
-                now_im = mask * (rate_re * im + rate_im * re) + driven[at : at + SUB, states:]
-                state[c] = (now_re, now_im)
-        ends = jnp.concatenate([jnp.concatenate(state[c], axis=1) for c in range(chains)], axis=0)
-        pieces[column, pl.ds(first, tile_blocks), :] = ends.astype(BF16)
-        at = (column, pl.ds(first, tile_blocks))
-        for copy in push_far(at) + [push_near(at, far)]:
-            copy.start()
-
-    @pl.when(i == tiles + 1)
-    def _():
+
+        def begin_tile(j, _):
+            driven = big.at[tile_at(j)]
+            driven[...] = dot(normed[tile_at(j), :], drive[...]).astype(big.dtype)
+            marks = marks_of(j)
+            state = [(jnp.zeros((SUB, states), F32), jnp.zeros((SUB, states), F32)) for _ in range(chains)]
+            for t in range(block_rows):
+                for c in range(chains):
+                    at = c * span + t * SUB
+                    mask = mask_of(marks, c, t)
+                    re, im = state[c]
+                    now_re = mask * (rate_re * re - rate_im * im) + driven[at : at + SUB, :states].astype(F32)
+                    now_im = mask * (rate_re * im + rate_im * re) + driven[at : at + SUB, states:].astype(F32)
+                    state[c] = (now_re, now_im)
+            ends = jnp.concatenate([jnp.concatenate(state[c], axis=1) for c in range(chains)], axis=0)
+            at = (column, pl.ds(pl.multiple_of(j * tile_blocks, tile_blocks), tile_blocks))
+            pieces_ends[at + (slice(None),)] = encode(ends, vectors[5:6, :both])
+            for copy in push_far(at) + [push_near(at, far)]:
+                copy.start()
+            return 0
+
+        lax.fori_loop(0, tiles, begin_tile, 0)
+        for copy in taps:
+            copy.wait()
+        lax.fori_loop(0, tiles, turn(mixed_all), 0)
+
         def arrive():
             onward = []
             for k, copy in enumerate(push_far((column,))):
@@ -420,176 +600,39 @@
                 there = 2 * lax.rem(mine[1] + grid.shape[1] - 1 - k, grid.shape[1]) + mine[2]
                 onward.append(push_near((there,), far + 1 + k))
                 onward[-1].start()
-            advance((1, 2, 3), 2)
+            gather_on((1, 2, 3), 2)
             push_near((column,), far).wait()
             for copy in onward:
                 copy.wait()
 
         cross_blocks(
-            members, False, arrive, pieces, place, own_place, broken, rates[2:3, :], rates[3:4, :], chosen, dealt_ends,
-            carries,
+            members, False, arrive, pieces_ends, vectors[4:5, :both], place, own_place, broken, rates[2:3, :], rates[3:4, :], chosen, dealt_x,
+            carry,
         )
-        advance((1, 2, 3), phases)
-
-
-def split(values):
-    high = values.astype(BF16)
-    rest = values - high.astype(F32)
-    middle = rest.astype(BF16)
-    return high, middle, (rest - middle.astype(F32)).astype(BF16)
-
-
-def row_times(row, matrix):
-    wide = [jnp.broadcast_to(piece.astype(F32), (SUB, row.shape[1])).astype(BF16) for piece in split(row)]
-    return sum(contract_cols(piece, matrix) for piece in wide)[0:1]
-
-
-def row_sums(matrix):
-    ones = jnp.ones((SUB, matrix.shape[1]), BF16)
-    return sum(contract_cols(ones, piece) for piece in split(matrix))[0:1]
-
-
-def back_kernel(
-    grid, block_rows, orders, cotangent, dealt, driven, carry, keep, rows_p, rates, readout, vectors, mixer, place,
-    own_place, broken, drive, drive_raw,
-    gated_low, token_part, drive_sum, readout_sum, weight_sum, vector_sum,
-    joined_all, joined_grad_all, mixed_all, coming, weight_grad, bias_grad, through_grad, readout_grad, mixed_sum,
-    drive_grad, decay_cot, driven_sum, pieces, chosen, dealt_heads, push_send, push_recv, *rest,
-):
-    i = pl.program_id(0)
-    tiles = (pl.num_programs(0) - 2) // 3
-    row, column, mine = grid.here()
-    members = grid.members
-    core = 2
-    phases = 3
-    span = SUB * block_rows
-    tile, width = cotangent.shape
-    both = joined_all.shape[1]
-    states = both // 2
-    chains = tile // span
-    tile_blocks = tile // block_rows
-    rest = list(rest)
-    parts = (readout_grad, weight_grad, drive_grad)
-    outs = (readout_sum, weight_sum, drive_sum)
-    count = len(parts)
-    accs = [rest.pop(0) for _ in range(count)]
-    stages = [[rest.pop(0) for _ in range(phases)] for _ in range(count)]
-    landed = [[rest.pop(0) for _ in range(phases)] for _ in range(count)]
-    vector_stage, across, along, send, recv, vector_send, vector_recv = rest
-    plans = [reduce_plan(grid, order) for order in orders]
-    every = (0, 1, 2)
-    kept = every[:-1]
-    first_a = tiles + 1
-    first_b = 2 * tiles + 1
-
-    def push_to(at):
-        return [
-            remote(
-                pieces.at[at], pieces.at[at], push_send.at[away - 1], push_recv.at[away - 1],
-                {"fsdp": lax.rem(column + away, members)},
-            )
-            for away in range(1, members)
-        ]
-
-    def combos(left):
-        return list(itertools.product(*[range(grid.shape[d]) for d in left]))
-
-    def at_of(dim, index, left, combo, dims):
-        chosen_of = dict(zip(left, combo))
-        chosen_of[dim] = index
-        return tuple(chosen_of[d] if d in chosen_of else mine[d] for d in dims)
-
-    def piece_of(k, dim, index, left, combo):
-        if dim != core:
-            return accs[k][at_of(dim, index, left, combo, kept)]
-        size = outs[k].shape[0]
-        down, half, low = at_of(dim, index, left, combo, every)
-        start = ((down * grid.shape[1] + half) * 2 + low) * size
-        if size % SUB == 0:
-            return parts[k][pl.ds(pl.multiple_of(start, size), size), :]
-        low_row = jnp.minimum(lax.div(start, SUB) * SUB, parts[k].shape[0] - 2 * SUB)
-        window = parts[k][pl.ds(pl.multiple_of(low_row, SUB), 2 * SUB), :]
-        return pltpu.roll(window, lax.rem(2 * SUB - (start - low_row), 2 * SUB), 0)[:size]
-
-    def hops(k, phase):
-        dim = plans[k][phase][0]
-        base = k * grid.slots + sum(grid.fan(d) for d in orders[k][:phase])
-        return [
-            (
-                remote(
-                    stages[k][phase].at[slot], landed[k][phase].at[slot], send.at[base + slot], recv.at[base + slot],
-                    device,
-                ),
-                slot,
-                index,
-            )
-            for slot, device, index in grid.peers(dim)
-        ]
-
-    def begin(k, phase):
-        dim, _, left = plans[k][phase]
-        for copy, slot, index in hops(k, phase):
-            for combo in combos(left):
-                stages[k][phase][(slot,) + combo] = piece_of(k, dim, index, left, combo).astype(BF16)
-            copy.start()
-
-    def finish(k, phase):
-        dim, _, left = plans[k][phase]
-        copies = hops(k, phase)
-        for copy, _, _ in copies:
-            copy.wait()
-        for combo in combos(left):
-            piece = piece_of(k, dim, mine[dim], left, combo)
-            for _, slot, _ in copies:
-                piece = piece + landed[k][phase][(slot,) + combo].astype(F32)
-            accs[k][at_of(dim, mine[dim], left, combo, kept)] = piece
-
-    def advance(ks, phase):
-        for k in ks:
-            if phase:
-                finish(k, phase - 1)
-            if phase < phases:
-                begin(k, phase)
-            else:
-                outs[k][...] = accs[k][mine[:-1]]
-
-    def vector_across():
-        return [
-            remote(
-                vector_stage, across.at[away - 1], vector_send.at[away - 1], vector_recv.at[away - 1],
-                {"fsdp": lax.rem(column + away, members)},
-            )
-            for away in range(1, members)
-        ]
-
-    def vector_along():
-        return [
-            remote(
-                vector_sum, along.at[slot], vector_send.at[members - 1 + slot], vector_recv.at[members - 1 + slot], device
-            )
-            for slot, device, _ in grid.peers(0)
-        ]
-
-    rate_re = spread(rates[0:1, :], SUB)
-    rate_im = spread(rates[1:2, :], SUB)
-
-    @pl.when(i == 0)
-    def _():
+        gather_on((1, 2, 3), 3)
+        flatten(readout_w, readout)
+        flatten(mixer_w, mixer)
+        note_norm(6, row_sums(jnp.square(readout[...].astype(F32))))
         for total in (
             weight_grad, bias_grad, through_grad, readout_grad, mixed_sum, drive_grad, decay_cot, driven_sum
         ):
             total[...] = jnp.zeros_like(total)
-        announce(grid)
+
+    rate_re = spread(rates[0:1, :], SUB)
+    rate_im = spread(rates[1:2, :], SUB)
 
     @pl.when(i < tiles)
     def _():
         through = vectors[2:3, :width]
         bias = vectors[3:4, : 2 * width]
-        here = pl.ds(pl.multiple_of(i * tile, tile), tile)
+        here = tile_at(i)
         joined = joined_all.at[here]
-        joined_grad = joined_grad_all.at[here]
+        driven = big.at[here]
+        joined_grad = big.at[here]
+        marks = marks_of(i)
+        entering = of_blocks(carry, i)
         state = [
-            (carry[c * SUB : (c + 1) * SUB, :states], carry[c * SUB : (c + 1) * SUB, states:])
+            (entering[c * SUB : (c + 1) * SUB, :states], entering[c * SUB : (c + 1) * SUB, states:])
             for c in range(chains)
         ]
         for t in range(0, block_rows, 2):
@@ -597,17 +640,17 @@
                 held = []
                 for step in (t, t + 1):
                     at = c * span + step * SUB
-                    mask = lanes_to(keep[at : at + SUB, :], states)
+                    mask = mask_of(marks, c, step)
                     re, im = state[c]
-                    now_re = mask * (rate_re * re - rate_im * im) + driven[at : at + SUB, :states]
-                    now_im = mask * (rate_re * im + rate_im * re) + driven[at : at + SUB, states:]
+                    now_re = mask * (rate_re * re - rate_im * im) + driven[at : at + SUB, :states].astype(F32)
+                    now_im = mask * (rate_re * im + rate_im * re) + driven[at : at + SUB, states:].astype(F32)
                     state[c] = (now_re, now_im)
                     held.append(state[c])
                 at = c * span + t * SUB
                 joined[at : at + 2 * SUB, :states] = jnp.concatenate([held[0][0], held[1][0]], axis=0).astype(BF16)
                 joined[at : at + 2 * SUB, states:] = (-jnp.concatenate([held[0][1], held[1][1]], axis=0)).astype(BF16)
 
-        dealt_f32 = dealt[...].astype(F32)
+        dealt_f32 = normed[here, :].astype(F32)
         mixed = dot(joined[...], readout[...]) + through * dealt_f32
         activated, slope = gelu_parts(mixed)
         features = activated.astype(BF16)
@@ -615,7 +658,7 @@
         value = hidden[:, :width]
         sig = 0.5 + 0.5 * jnp.tanh(0.5 * hidden[:, width:])
         gated_low[...] = (value * sig).astype(BF16)
-        cot_sig = cotangent[...].astype(F32) * sig
+        cot_sig = mixed_all[here, :].astype(F32) * sig
         hidden_low = jnp.concatenate(
             [cot_sig.astype(BF16), (cot_sig * value * (1.0 - sig)).astype(BF16)], axis=1
         )
@@ -628,23 +671,19 @@
         through_grad[...] += jnp.sum(mixed_f32 * dealt_f32, axis=0, keepdims=True)
         mixed_sum[...] += jnp.sum(mixed_f32, axis=0, keepdims=True)
         readout_grad[...] += contract_rows(joined[...], mixed_grad)
-        joined_grad[...] = contract_cols(mixed_grad, readout[...])
+        joined_grad[...] = contract_cols(mixed_grad, readout[...]).astype(big.dtype)
 
         going = [(jnp.zeros((SUB, states), F32), jnp.zeros((SUB, states), F32)) for _ in range(chains)]
         for t in reversed(range(block_rows)):
             for c in range(chains):
                 at = c * span + t * SUB
-                mask = lanes_to(keep[at : at + SUB, :], states)
-                re = joined_grad[at : at + SUB, :states] + going[c][0]
-                im = going[c][1] - joined_grad[at : at + SUB, states:]
+                mask = mask_of(marks, c, t)
+                re = joined_grad[at : at + SUB, :states].astype(F32) + going[c][0]
+                im = going[c][1] - joined_grad[at : at + SUB, states:].astype(F32)
                 going[c] = (mask * (rate_re * re + rate_im * im), mask * (rate_re * im - rate_im * re))
         heads = jnp.concatenate([jnp.concatenate(going[c], axis=1) for c in range(chains)], axis=0)
         at = (column, pl.ds(pl.multiple_of(i * tile_blocks, tile_blocks), tile_blocks))
-        pieces[at + (slice(None),)] = heads.astype(BF16)
-
-        @pl.when(i == 0)
-        def _():
-            meet(grid)
+        pieces[at + (slice(None),)] = encode(heads, vectors[7:8, :both])
 
         for copy in push_to(at):
             copy.start()
@@ -657,7 +696,7 @@
                 copy.wait()
 
         cross_blocks(
-            members, True, arrive, pieces, place, own_place, broken, rates[2:3, :], rates[3:4, :], chosen, dealt_heads,
+            members, True, arrive, pieces, vectors[6:7, :both], place, own_place, broken, rates[2:3, :], rates[3:4, :], chosen, dealt_x,
             coming,
         )
         advance((0, 1), 1)
@@ -681,11 +720,13 @@
     @pl.when((i >= first_a) & (i < first_b))
     def _():
         j = first_b - 1 - i
-        here = pl.ds(pl.multiple_of(j * tile, tile), tile)
+        here = tile_at(j)
         joined = joined_all.at[here]
         driven_low = joined
-        joined_grad = joined_grad_all.at[here]
-        entering = coming[pl.ds(pl.multiple_of(j * tile_blocks, tile_blocks), tile_blocks), :]
+        joined_grad = big.at[here]
+        marks = marks_of(j)
+        entering = of_blocks(coming, j)
+        before = of_blocks(carry, j)
         going = [
             (entering[c * SUB : (c + 1) * SUB, :states], entering[c * SUB : (c + 1) * SUB, states:])
             for c in range(chains)
@@ -698,17 +739,17 @@
                 here_re = joined[pair : pair + SUB, :states].astype(F32)
                 here_im = -joined[pair : pair + SUB, states:].astype(F32)
                 if t == 0:
-                    past_re = carry[c * SUB : (c + 1) * SUB, :states]
-                    past_im = carry[c * SUB : (c + 1) * SUB, states:]
+                    past_re = before[c * SUB : (c + 1) * SUB, :states]
+                    past_im = before[c * SUB : (c + 1) * SUB, states:]
                 else:
                     past_re = joined[pair - SUB : pair, :states].astype(F32)
                     past_im = -joined[pair - SUB : pair, states:].astype(F32)
                 held = {}
                 for step, (prev_re, prev_im) in ((t + 1, (here_re, here_im)), (t, (past_re, past_im))):
                     where = c * span + step * SUB
-                    mask = lanes_to(keep[where : where + SUB, :], states)
-                    re = joined_grad[where : where + SUB, :states] + going[c][0]
-                    im = going[c][1] - joined_grad[where : where + SUB, states:]
+                    mask = mask_of(marks, c, step)
+                    re = joined_grad[where : where + SUB, :states].astype(F32) + going[c][0]
+                    im = going[c][1] - joined_grad[where : where + SUB, states:].astype(F32)
                     held[step] = (re, im)
                     sums[c] = (sums[c][0] + re, sums[c][1] + im)
                     on_re = mask * (rate_re * re + rate_im * im)
@@ -727,7 +768,7 @@
         for c in range(chains):
             decay_cot[...] += jnp.concatenate(total[c], axis=1)
             driven_sum[...] += jnp.concatenate(sums[c], axis=1)
-        drive_grad[...] += contract_rows(dealt[...], driven_low[...])
+        drive_grad[...] += contract_rows(normed[here, :], driven_low[...])
 
     @pl.when(i == first_b)
     def _():
@@ -748,7 +789,8 @@
         vector_stage[5:6, :states] = (cot[:, :states] * factor_re - cot[:, states:] * factor_im) / size
         vector_stage[5:6, states:] = (cot[:, :states] * factor_im + cot[:, states:] * factor_re) / size
         d_re, d_im = drive_grad[:, :states], drive_grad[:, states:]
-        b_re, b_im = drive_raw[:, :states].astype(F32), drive_raw[:, states:].astype(F32)
+        raw = drive_w[...].reshape(width, both).astype(F32)
+        b_re, b_im = raw[:, :states], raw[:, states:]
         vector_stage[6:7, :states] = jnp.sum(d_re * b_re + d_im * b_im, axis=0, keepdims=True)
         vector_stage[6:7, states:] = jnp.sum(d_im * b_re - d_re * b_im, axis=0, keepdims=True)
 
@@ -787,11 +829,11 @@
     @pl.when((i >= first_b) & (i < first_b + tiles))
     def _():
         j = i - first_b
-        here = pl.ds(pl.multiple_of(j * tile, tile), tile)
+        here = tile_at(j)
         driven_low = joined_all[here, :]
         normed_grad = vectors[2:3, :width] * mixed_all[here, :].astype(F32) + contract_cols(driven_low, drive[...])
         given = normed_grad.astype(BF16).astype(F32)
-        moved, rstd = norm_stats(rows_p[...].astype(F32))
+        moved, rstd = norm_stats(rows_in[here, :].astype(F32))
         xhat = moved * rstd
         scaled = given * vectors[0:1, :width]
         inner = jnp.mean(scaled * xhat, axis=-1, keepdims=True)
@@ -884,7 +926,7 @@
     tiles = rows // tile
     tile_blocks = tile // block_rows
     total = blocks * members
-    chunk = min(total, 2**30 // total**2)
+    chunk = min(total, 2**29 // total**2)
     sequences = sequence_lengths.shape[1]
     shape = jax.ShapeDtypeStruct
     anywhere = pl.BlockSpec(memory_space=pl.ANY)
@@ -902,58 +944,10 @@
     counts = tuple(v.shape[0] for v in small)
     shards = (drive_matrix, readout_matrix, mixer_weight)
     slots = grid.slots
-
-    def shifted(rows_of, columns):
-        return pl.BlockSpec((rows_of, columns), lambda i: (jnp.clip(i - 1, 0, tiles - 1), 0))
-
-    dealt, rows_p, cot_p, driven, keep, carry, drive, drive_raw, readout, mixer, vectors, rates, place, own_place, broken = pl.pallas_call(
-        functools.partial(front_kernel, grid, block_rows, counts, tile),
-        grid=(tiles + 2,),
-        in_specs=[anywhere, shifted(tile, width)]
-        + [flat(size) for size in counts]
-        + [whole((1, sequences)), anywhere, anywhere, anywhere, whole((span, span))],
-        out_specs=[
-            shifted(tile, width), shifted(tile, width), shifted(tile, width), shifted(tile, both), shifted(tile, LANES),
-            total_of((blocks, both)),
-            total_of((width, both)),
-            total_of((width, both)), anywhere, anywhere, total_of((SUB, 2 * width)), total_of((SUB, states)),
-            total_of((1, total)), total_of((blocks, LANES)), total_of((sequences, members, LANES)),
-        ],
-        out_shape=[
-            shape((rows, width), BF16), shape((rows, width), BF16), shape((rows, width), BF16),
-            shape((rows, both), F32), shape((rows, LANES), F32), shape((blocks, both), F32),
-            shape((width, both), BF16), shape((width, both), BF16),
-            shape(grid.shape + readout_matrix.shape, BF16), shape(grid.shape + mixer_weight.shape, BF16),
-            shape((SUB, 2 * width), F32), shape((SUB, states), F32), shape((1, total), F32),
-            shape((blocks, LANES), F32), shape((sequences, members, LANES), jnp.int32),
-        ],
-        scratch_shapes=[
-            pltpu.VMEM((rows, width), BF16),
-            pltpu.VMEM((rows, width), BF16),
-            pltpu.VMEM((rows, width), F32),
-            pltpu.VMEM(grid.shape + (SUB, LANES), F32),
-            pltpu.VMEM(grid.shape + drive_matrix.shape, BF16),
-            pltpu.VMEM((blocks, LANES), jnp.int32),
-            pltpu.VMEM((members, blocks, both), BF16),
-            pltpu.VMEM((chunk, total), BF16),
-            pltpu.VMEM((total, both), F32),
-            regular((4 * slots,)), regular((4 * slots,)), regular((len(shards) + tiles,)), regular((members,)),
-            regular((members,)), regular((grid.dp * members - 1,)), regular((grid.dp * members - 1,)),
-        ],
-        compiler_params=params(0),
-        name="front",
-    )(tokens, cotangent, *small, sequence_lengths, *shards, perm)
-    readout = readout.reshape(both, width)
-    mixer = mixer.reshape(width, 2 * width)
+    kept_type = F32 if members <= SUB else BF16
 
     def first(rows_of, columns):
         return pl.BlockSpec((rows_of, columns), lambda i: (jnp.minimum(i, tiles - 1), 0))
-
-    def twice(rows_of, columns):
-        def index(i):
-            return (jnp.where(i <= tiles, jnp.minimum(i, tiles - 1), jnp.maximum(2 * tiles - i, 0)), 0)
-
-        return pl.BlockSpec((rows_of, columns), index)
 
     def final(rows_of, columns):
         return pl.BlockSpec((rows_of, columns), lambda i: (jnp.clip(i - 2 * tiles - 1, 0, tiles - 1), 0))
@@ -964,32 +958,43 @@
     for turn, weight in zip(orders, weights):
         for dim, _, left in reduce_plan(grid, turn):
             buffers.append(pltpu.VMEM((grid.fan(dim),) + tuple(grid.shape[d] for d in left) + weight.shape, BF16))
-    gated_low, token_part, drive_sum, readout_sum, weight_sum, vector_sum = pl.pallas_call(
-        functools.partial(back_kernel, grid, block_rows, orders),
+    gated_low, token_part, drive_sum, readout_sum, weight_sum, vector_sum, rates = pl.pallas_call(
+        functools.partial(layer_kernel, grid, block_rows, counts, tile, orders),
         grid=(3 * tiles + 2,),
-        in_specs=[
-            first(tile, width), twice(tile, width), first(tile, both), twice(tile_blocks, both), twice(tile, LANES),
-            final(tile, width), whole((SUB, states)), whole((both, width)), whole((SUB, 2 * width)),
-            whole((width, 2 * width)), whole((1, total)), whole((blocks, LANES)), whole((sequences, members, LANES)),
-            whole((width, both)), whole((width, both)),
-        ],
+        in_specs=[anywhere, anywhere]
+        + [flat(size) for size in counts]
+        + [whole((1, sequences)), anywhere, anywhere, anywhere, whole((span, span))],
         out_specs=[
             first(tile, width), final(tile, width), total_of(drive_matrix.shape), total_of(readout_matrix.shape),
-            total_of(mixer_weight.shape), total_of((SUB, both)),
+            total_of(mixer_weight.shape), total_of((SUB, both)), total_of((SUB, states)),
         ],
         out_shape=[
             shape((rows, width), BF16), shape((rows, width), BF16), shape(drive_matrix.shape, F32),
             shape(readout_matrix.shape, F32), shape(mixer_weight.shape, F32), shape((SUB, both), F32),
+            shape((SUB, states), F32),
         ],
         scratch_shapes=[
-            pltpu.VMEM((rows, both), BF16), pltpu.VMEM((rows, both), F32), pltpu.VMEM((rows, width), BF16),
-            pltpu.VMEM((blocks, both), F32), pltpu.VMEM((width, 2 * width), F32), pltpu.VMEM((1, 2 * width), F32),
-            pltpu.VMEM((1, width), F32), pltpu.VMEM((both, width), F32), pltpu.VMEM((1, width), F32),
-            pltpu.VMEM((width, both), F32), pltpu.VMEM((SUB, both), F32), pltpu.VMEM((SUB, both), F32),
-            pltpu.VMEM((members, blocks, both), BF16), pltpu.VMEM((chunk, total), BF16), pltpu.VMEM((total, both), F32),
+            pltpu.VMEM((rows, width), BF16), pltpu.VMEM((rows, width), BF16), pltpu.VMEM((rows, width), BF16),
+            pltpu.VMEM((rows, both), kept_type), pltpu.VMEM((rows, both), BF16),
+            pltpu.VMEM(grid.shape + (SUB, LANES), F32),
+        ]
+        + [pltpu.VMEM(grid.shape + shard.shape, BF16) for shard in shards]
+        + [
+            pltpu.VMEM((width, both), BF16), pltpu.VMEM((both, width), BF16),
+            pltpu.VMEM((width, 2 * width), BF16), pltpu.VMEM((SUB, 2 * width), F32), pltpu.VMEM((1, total), F32),
+            pltpu.VMEM((blocks, LANES), F32), pltpu.VMEM((sequences, members, LANES), jnp.int32),
+            pltpu.VMEM((blocks, LANES), jnp.int32), pltpu.VMEM((blocks, both), F32), pltpu.VMEM((blocks, both), F32),
+            pltpu.VMEM((members, blocks, both + LANES), jnp.int16),
+            pltpu.VMEM((members, blocks, both + LANES), jnp.int16),
+            pltpu.VMEM((chunk, total), BF16), pltpu.VMEM((total, both), kept_type),
+            pltpu.VMEM((width, 2 * width), F32), pltpu.VMEM((1, 2 * width), F32), pltpu.VMEM((1, width), F32),
+            pltpu.VMEM((both, width), F32), pltpu.VMEM((1, width), F32), pltpu.VMEM((width, both), F32),
+            pltpu.VMEM((SUB, both), F32), pltpu.VMEM((SUB, both), F32),
+            regular((4 * slots,)), regular((4 * slots,)), regular((len(shards) + 2 * tiles,)), regular((members,)),
+            regular((members,)), regular((grid.dp * members - 1,)), regular((grid.dp * members - 1,)),
             regular((members - 1,)), regular((members - 1,)),
         ]
-        + [pltpu.VMEM(grid.shape[:-1] + weight.shape, F32) for weight in weights]
+        + [pltpu.VMEM(grid.shape[:-1] + weight.shape, F32) for weight in weights if weight.shape[0] % SUB]
         + buffers
         + buffers
         + [
@@ -997,12 +1002,9 @@
             pltpu.VMEM((grid.dp - 1, SUB, both), F32), regular((3 * slots,)), regular((3 * slots,)),
             regular((members + grid.dp - 2,)), regular((members + grid.dp - 2,)),
         ],
-        compiler_params=params(1),
-        name="back",
-    )(
-        cot_p, dealt, driven, carry, keep, rows_p, rates, readout, vectors, mixer, place, own_place, broken, drive,
-        drive_raw,
-    )
+        compiler_params=params(0),
+        name="layer",
+    )(tokens, cotangent, *small, sequence_lengths, *shards, perm)
 
     vector_sizes = [v.shape[0] for v in (norm_gain, norm_shift, decay_real, decay_rotation, log_timestep)]
     slab = 2 * tile

time: 138 us -> 135 us (0.978)
  Pallas kernels: 137 us -> 134 us
    pallas_call x2 -> x1, Pallas kernels: 125 us -> 122 us  [body(): pl.pallas_call(functools.partial(layer_kernel, grid, block_rows, counts,...]
where the time goes in v4:
time: 135 us
  Pallas kernels  134 us (99%)
    pallas_call x1, Pallas kernels, body(): pl.pallas_call(functools.partial(layer_kernel, grid, block_rows, counts,...  122 us
    pallas_call x1, Pallas kernels, body(): pl.pallas_call(functools.partial(tail_kernel, grid, span), grid=(rows //...  12.6 us

profile of v4, /device:TPU:0, one launch (start us, length us, event | category | flops | bytes accessed | tf_op | source)
XLA Modules:
  0.0 134.9 jit_solution(10975509009049622899)
XLA Ops:
  0.6 121.7 %layer.1 = (bf16[4096,512]{1,0:T(8,128)(2,1)}, bf16[4096,512]{1,0:T(8,128)(2,1)}, f32[16,768]{1,0:T(8,128)}, f32[24,512]{1,0:T(8,128)}, f32[16,1024]{1,0:T(8,128)}, /*index=5*/f32[8,768]{1,0:T(8,128)}, f32[8,384]{1,0:T(8,128)}) custom-call(bf16[4096,512]{1,0:T(8,128)(2,1)} %tokens.3, bf16[4096,512]{1,0:T(8,128)(2,1)} %cotangent.3, bf16[16]{0:T(256)(128)(2,1)} %gain_s.1, ...), custom_call_target="tpu_custom_call" | custom-call | tf_op jit(solution)/shard_map/layer/pallas_call | solution.py:961
  122.3 12.6 %tail.1 = (f32[4096,512]{1,0:T(8,128)}, f32[4096,512]{1,0:T(8,128)}, f32[16]{0:T(128)}, f32[16]{0:T(128)}, f32[12]{0:T(128)}, /*index=5*/f32[12]{0:T(128)}, f32[...) custom-call(bf16[4096,512]{1,0:T(8,128)(2,1)} %tokens.3, ...), custom_call_target="tpu_custom_call" | custom-call | tf_op jit(solution)/shard_map/tail/pallas_call | solution.py:1011

commit v5 on v4

--- a/solution.py
+++ b/solution.py
@@ -178,27 +178,33 @@
     steps = total // members
     blocks = steps
     chunk = chosen.shape[0]
-
-    def choose(at):
-        rows = lax.broadcasted_iota(jnp.int32, (chunk, total), 0).astype(F32) + float(at)
-        return jnp.where(rows == place[...], 1.0, 0.0).astype(BF16)
-
-    chosen[...] = choose(0)
-    arrive()
-    for at in range(0, total, chunk):
-        if at:
-            chosen[...] = choose(at)
-        moved, power = 0.0, 0.0
-        for first in range(0, members, 4):
-            held = pieces[first : first + 4].reshape(4 * blocks, -1).astype(jnp.int32)
-            picked = chosen[:, first * blocks : (first + 4) * blocks]
-            ints = held[:, : 2 * states]
-            high = (ints & -256).astype(F32).astype(BF16)
-            low = (ints & 255).astype(F32).astype(BF16)
-            moved = moved + (dot(picked, high) + dot(picked, low))
-            power = power + dot(picked, held[:, 2 * states :].astype(F32).astype(BF16))
-        moved = moved * (lanes_to(jnp.exp2(power) * (1.0 / 32000.0), 2 * states) * norm)
-        dealt[at : at + chunk, :] = moved.astype(dealt.dtype)
+    part = blocks // 2
+
+    def choose(group, at):
+        rows = lax.broadcasted_iota(jnp.int32, (chunk, total // 2), 0).astype(F32) + float(at)
+        wanted = place[:, group * (total // 2) : (group + 1) * (total // 2)]
+        chosen[...] = jnp.where(rows == wanted, 1.0, 0.0).astype(BF16)
+
+    for group in range(2):
+        choose(group, 0)
+        arrive(group)
+        for at in range(0, total, chunk):
+            if at:
+                choose(group, at)
+            moved, power = 0.0, 0.0
+            for first in range(0, members, 8):
+                held = pieces[first : first + 8, group * part : (group + 1) * part].reshape(8 * part, -1)
+                held = held.astype(jnp.int32)
+                picked = chosen[:, first * part : (first + 8) * part]
+                ints = held[:, : 2 * states]
+                high = (ints & -256).astype(F32).astype(BF16)
+                low = (ints & 255).astype(F32).astype(BF16)
+                moved = moved + (dot(picked, high) + dot(picked, low))
+                power = power + dot(picked, held[:, 2 * states :].astype(F32).astype(BF16))
+            moved = moved * (lanes_to(jnp.exp2(power) * (1.0 / 32000.0), 2 * states) * norm)
+            if group:
+                moved = moved + dealt[at : at + chunk, :].astype(F32)
+            dealt[at : at + chunk, :] = moved.astype(dealt.dtype)
     rate_re = spread(flow_re, members)
     rate_im = spread(-flow_im if reverse else flow_im, members)
     marks = [broken[s] for s in range(broken.shape[0])]
@@ -298,15 +304,20 @@
                 for copy in phase_copies(k, phase):
                     copy.start()
 
-    def push_far(at):
+    def push_far(at, group):
         return [
-            remote(pieces_ends.at[at], pieces_ends.at[at], ends_send.at[slot], ends_recv.at[slot], device)
+            remote(pieces_ends.at[at], pieces_ends.at[at], ends_send.at[group, slot], ends_recv.at[group, slot], device)
             for slot, device, _ in grid.peers(1)
         ]
 
-    def push_near(at, slot):
+    def push_near(at, group, slot):
         device = grid.peers(2)[0][1]
-        return remote(pieces_ends.at[at], pieces_ends.at[at], ends_send.at[slot], ends_recv.at[slot], device)
+        return remote(
+            pieces_ends.at[at], pieces_ends.at[at], ends_send.at[group, slot], ends_recv.at[group, slot], device
+        )
+
+    def group_rows(group):
+        return pl.ds(group * (blocks // 2), blocks // 2)
 
     far = grid.fan(1)
 
@@ -349,10 +360,10 @@
     first_a = tiles + 1
     first_b = 2 * tiles + 1
 
-    def push_to(at):
+    def push_to(at, group):
         return [
             remote(
-                pieces.at[at], pieces.at[at], push_send.at[away - 1], push_recv.at[away - 1],
+                pieces.at[at], pieces.at[at], push_send.at[group, away - 1], push_recv.at[group, away - 1],
                 {"fsdp": lax.rem(column + away, members)},
             )
             for away in range(1, members)
@@ -503,6 +514,10 @@
         for copy in chunks[tiles // 2 :]:
             copy.wait()
         lax.fori_loop(tiles // 2, tiles, turn(rows_in), 0)
+        for total in (
+            weight_grad, bias_grad, through_grad, readout_grad, mixed_sum, drive_grad, decay_cot, driven_sum
+        ):
+            total[...] = jnp.zeros_like(total)
         for copy in table_copies():
             copy.wait()
         rows = table[...].reshape(-1, LANES)
@@ -522,7 +537,10 @@
         for m in range(members):
             q = group[m * SUB + 7 : m * SUB + 8, :blocks]
             d = jnp.floor(q * (1.0 / blocks))
-            place[:, m * blocks : (m + 1) * blocks] = (q - d * blocks) * members + d
+            q = (q - d * blocks) * members + d
+            for side in range(2):
+                start = (side * members + m) * (blocks // 2)
+                place[:, start : start + blocks // 2] = q[:, side * (blocks // 2) : (side + 1) * (blocks // 2)]
         lengths = jnp.concatenate([group[m * SUB + 4 : m * SUB + 5, :] for m in range(members)], axis=0)
         sequences = lengths_s.shape[1]
         q = table[tuple(mine) + (slice(7, 8), slice(None))]
@@ -584,7 +602,8 @@
             ends = jnp.concatenate([jnp.concatenate(state[c], axis=1) for c in range(chains)], axis=0)
             at = (column, pl.ds(pl.multiple_of(j * tile_blocks, tile_blocks), tile_blocks))
             pieces_ends[at + (slice(None),)] = encode(ends, vectors[5:6, :both])
-            for copy in push_far(at) + [push_near(at, far)]:
+            group = lax.div(j, tiles // 2)
+            for copy in push_far(at, group) + [push_near(at, group, far)]:
                 copy.start()
             return 0
 
@@ -592,16 +611,20 @@
         for copy in taps:
             copy.wait()
         lax.fori_loop(0, tiles, turn(mixed_all), 0)
-
-        def arrive():
+        gather_on((1, 2, 3), 2)
+        gather_on((1, 2, 3), 3)
+        flatten(readout_w, readout)
+        flatten(mixer_w, mixer)
+        note_norm(6, row_sums(jnp.square(readout[...].astype(F32))))
+
+        def arrive(group):
             onward = []
-            for k, copy in enumerate(push_far((column,))):
+            for k, copy in enumerate(push_far((column, group_rows(group)), group)):
                 copy.wait()
                 there = 2 * lax.rem(mine[1] + grid.shape[1] - 1 - k, grid.shape[1]) + mine[2]
-                onward.append(push_near((there,), far + 1 + k))
+                onward.append(push_near((there, group_rows(group)), group, far + 1 + k))
                 onward[-1].start()
-            gather_on((1, 2, 3), 2)
-            push_near((column,), far).wait()
+            push_near((column, group_rows(group)), group, far).wait()
             for copy in onward:
                 copy.wait()
 
@@ -609,14 +632,6 @@
             members, False, arrive, pieces_ends, vectors[4:5, :both], place, own_place, broken, rates[2:3, :], rates[3:4, :], chosen, dealt_x,
             carry,
         )
-        gather_on((1, 2, 3), 3)
-        flatten(readout_w, readout)
-        flatten(mixer_w, mixer)
-        note_norm(6, row_sums(jnp.square(readout[...].astype(F32))))
-        for total in (
-            weight_grad, bias_grad, through_grad, readout_grad, mixed_sum, drive_grad, decay_cot, driven_sum
-        ):
-            total[...] = jnp.zeros_like(total)
 
     rate_re = spread(rates[0:1, :], SUB)
     rate_im = spread(rates[1:2, :], SUB)
@@ -685,37 +700,24 @@
         at = (column, pl.ds(pl.multiple_of(i * tile_blocks, tile_blocks), tile_blocks))
         pieces[at + (slice(None),)] = encode(heads, vectors[7:8, :both])
 
-        for copy in push_to(at):
+        for copy in push_to(at, lax.div(i, tiles // 2)):
             copy.start()
 
     @pl.when(i == tiles)
     def _():
-        def arrive():
-            advance((0, 1), 0)
-            for copy in push_to((column,)):
+        def arrive(group):
+            advance((0, 1), group)
+            for copy in push_to((column, group_rows(group)), group):
                 copy.wait()
 
         cross_blocks(
             members, True, arrive, pieces, vectors[6:7, :both], place, own_place, broken, rates[2:3, :], rates[3:4, :], chosen, dealt_x,
             coming,
         )
-        advance((0, 1), 1)
-
-    @pl.when(i == first_a + tiles // 2)
+
+    @pl.when(i == first_b - 1)
     def _():
         advance((1,), 2)
-
-    @pl.when(i == first_a + tiles - 2)
-    def _():
-        advance((0,), 2)
-
-    @pl.when(i == first_b)
-    def _():
-        advance((1,), 3)
-
-    @pl.when(i == first_b + 2)
-    def _():
-        advance((0,), 3)
 
     @pl.when((i >= first_a) & (i < first_b))
     def _():
@@ -801,6 +803,10 @@
     def _():
         advance((2,), 1)
 
+    @pl.when(i == first_b + 2)
+    def _():
+        advance((0,), 2)
+
     @pl.when(i == first_b + 3)
     def _():
         for copy in vector_across():
@@ -824,7 +830,7 @@
         for k in range(grid.dp - 1):
             total = total + along[k]
         vector_sum[...] = total
-        advance((2,), 3)
+        advance((0, 1, 2), 3)
 
     @pl.when((i >= first_b) & (i < first_b + tiles))
     def _():
@@ -926,7 +932,7 @@
     tiles = rows // tile
     tile_blocks = tile // block_rows
     total = blocks * members
-    chunk = min(total, 2**29 // total**2)
+    chunk = min(total, 2**40 // total**3)
     sequences = sequence_lengths.shape[1]
     shape = jax.ShapeDtypeStruct
     anywhere = pl.BlockSpec(memory_space=pl.ANY)
@@ -986,13 +992,13 @@
             pltpu.VMEM((blocks, LANES), jnp.int32), pltpu.VMEM((blocks, both), F32), pltpu.VMEM((blocks, both), F32),
             pltpu.VMEM((members, blocks, both + LANES), jnp.int16),
             pltpu.VMEM((members, blocks, both + LANES), jnp.int16),
-            pltpu.VMEM((chunk, total), BF16), pltpu.VMEM((total, both), kept_type),
+            pltpu.VMEM((chunk, total // 2), BF16), pltpu.VMEM((total, both), kept_type),
             pltpu.VMEM((width, 2 * width), F32), pltpu.VMEM((1, 2 * width), F32), pltpu.VMEM((1, width), F32),
             pltpu.VMEM((both, width), F32), pltpu.VMEM((1, width), F32), pltpu.VMEM((width, both), F32),
             pltpu.VMEM((SUB, both), F32), pltpu.VMEM((SUB, both), F32),
-            regular((4 * slots,)), regular((4 * slots,)), regular((len(shards) + 2 * tiles,)), regular((members,)),
-            regular((members,)), regular((grid.dp * members - 1,)), regular((grid.dp * members - 1,)),
-            regular((members - 1,)), regular((members - 1,)),
+            regular((4 * slots,)), regular((4 * slots,)), regular((len(shards) + 2 * tiles,)), regular((2, members)),
+            regular((2, members)), regular((grid.dp * members - 1,)), regular((grid.dp * members - 1,)),
+            regular((2, members - 1)), regular((2, members - 1)),
         ]
         + [pltpu.VMEM(grid.shape[:-1] + weight.shape, F32) for weight in weights if weight.shape[0] % SUB]
         + buffers
@@ -1007,7 +1013,7 @@
     )(tokens, cotangent, *small, sequence_lengths, *shards, perm)
 
     vector_sizes = [v.shape[0] for v in (norm_gain, norm_shift, decay_real, decay_rotation, log_timestep)]
-    slab = 2 * tile
+    slab = 4 * tile
     outs = pl.pallas_call(
         functools.partial(tail_kernel, grid, span),
         grid=(rows // slab,),

time: 135 us -> 127 us (0.941)
  Pallas kernels: 134 us -> 126 us
    pallas_call x1, Pallas kernels: 122 us -> 115 us  [body(): pl.pallas_call(functools.partial(layer_kernel, grid, block_rows, counts,...]
where the time goes in v5:
time: 127 us
  Pallas kernels  126 us (99%)
    pallas_call x1, Pallas kernels, body(): pl.pallas_call(functools.partial(layer_kernel, grid, block_rows, counts,...  115 us
    pallas_call x1, Pallas kernels, body(): pl.pallas_call(functools.partial(tail_kernel, grid, span), grid=(rows //...  11.4 us

profile of v5, /device:TPU:0, one launch (start us, length us, event | category | flops | bytes accessed | tf_op | source)
XLA Modules:
  0.0 127.1 jit_solution(14772100955853303291)
XLA Ops:
  0.6 115.0 %layer.1 = (bf16[4096,512]{1,0:T(8,128)(2,1)}, bf16[4096,512]{1,0:T(8,128)(2,1)}, f32[16,768]{1,0:T(8,128)}, f32[24,512]{1,0:T(8,128)}, f32[16,1024]{1,0:T(8,128)}, /*index=5*/f32[8,768]{1,0:T(8,128)}, f32[8,384]{1,0:T(8,128)}) custom-call(bf16[4096,512]{1,0:T(8,128)(2,1)} %tokens.3, bf16[4096,512]{1,0:T(8,128)(2,1)} %cotangent.3, bf16[16]{0:T(256)(128)(2,1)} %gain_s.1, ...), custom_call_target="tpu_custom_call" | custom-call | tf_op jit(solution)/shard_map/layer/pallas_call | solution.py:967
  115.7 11.4 %tail.1 = (f32[4096,512]{1,0:T(8,128)}, f32[4096,512]{1,0:T(8,128)}, f32[16]{0:T(128)}, f32[16]{0:T(128)}, f32[12]{0:T(128)}, /*index=5*/f32[12]{0:T(128)}, f32[...) custom-call(bf16[4096,512]{1,0:T(8,128)(2,1)} %tokens.3, ...), custom_call_target="tpu_custom_call" | custom-call | tf_op jit(solution)/shard_map/tail/pallas_call | solution.py:1017
